TPU v7x, 32 devices: a whole 2x2x4 slice. The times are simulated.
32 devices in a mesh: shard: 8 (over z, y), tp: 4 (over x, core).
Axes of the slice: x: 2, y: 2, z: 4, core: 2. Of those that a mesh axis runs over, the one named last changes fastest.
Arguments:
- tokens: bfloat16 [2048, 8, 1536], P('tp', 'shard'), may hold values from -6 to 6
- w_query: float32 [1536, 1536], P('shard', 'tp'), may hold values from -0.15625 to 0.15625
- w_keyval: float32 [1536, 256], P('shard'), may hold values from -0.15625 to 0.15625
- w_out: float32 [1536, 1536], P('tp', 'shard'), may hold values from -0.875 to 0.875
- w_gate: float32 [1536, 4608], P('shard', 'tp'), may hold values from -0.15625 to 0.15625
- w_up: float32 [1536, 4608], P('shard', 'tp'), may hold values from -0.15625 to 0.15625
- w_down: float32 [4608, 1536], P('tp', 'shard'), may hold values from -0.09375 to 0.09375
- gain_attn: float32 [1536], P('shard'), may hold values from 0.5 to 1.5
- gain_mlp: float32 [1536], P('shard'), may hold values from 0.5 to 1.5
- cotangent: bfloat16 [2048, 8, 1536], P(None, 'shard'), may hold values from -6 to 6
Outputs:
- output: bfloat16 [2048, 8, 1536], P('tp', 'shard')
- grad_tokens: float32 [2048, 8, 1536], P('tp', 'shard')
- grad_query: float32 [1536, 1536], P('shard', 'tp')
- grad_keyval: float32 [1536, 256], P('shard')
- grad_out: float32 [1536, 1536], P('tp', 'shard')
- grad_gate: float32 [1536, 4608], P('shard', 'tp')
- up_weight_gradient: float32 [1536, 4608], P('shard', 'tp')
- down_weight_gradient: float32 [4608, 1536], P('tp', 'shard')
- grad_gain_attn: float32 [1536], P('shard')
- grad_gain_mlp: float32 [1536], P('shard')
All inputs are finite; a program needn't handle non-finite values.
Results may differ from a plain program's by a relative error of at most 0.02.
Values may be sent and summed in bfloat16 or wider, within the bound.
No kernel may reach another device: no remote copies, remote signals or barrier semaphores. Data moves between devices by JAX's collectives and lax.ppermute only.
A program may use at most 192 MiB of HBM per device.

v0:
```python
import jax
import jax.numpy as jnp
from jax import lax
from jax.sharding import PartitionSpec as P

HD = 128
WINDOW = 1024
BLOCK = 512


EPS = 1e-06


def rms_scale(hidden, weight_gain):
    return hidden * lax.rsqrt(jnp.mean(hidden * hidden, axis=-1, keepdims=True) + EPS) * weight_gain


def block_mask(start):
    row_index = jnp.arange(BLOCK, dtype=jnp.int32)[:, None]
    col_index = jnp.arange(WINDOW + BLOCK, dtype=jnp.int32)[None, :]
    offset = row_index + WINDOW - col_index
    return (offset >= 0) & (offset < WINDOW) & (col_index >= WINDOW - start)


def block_scores(query_block, key_block, start):
    scores = HD ** (-0.5) * jnp.einsum(
        "asnd,csd->snac", query_block, key_block, preferred_element_type=jnp.float32
    )
    return jnp.where(block_mask(start)[None, None], scores, -1e30)


def padded_pairs(keyval):
    padding = jnp.zeros((WINDOW,) + keyval.shape[1:], keyval.dtype)
    return jnp.concatenate([padding, keyval], 0)


def attend_forward(query, keyval):
    length = query.shape[0]
    key_pad = padded_pairs(keyval)
    starts = jnp.arange(length // BLOCK, dtype=jnp.int32) * BLOCK

    def one_block(start):
        query_block = lax.dynamic_slice_in_dim(query, start, BLOCK, 0)
        pairs = lax.dynamic_slice_in_dim(key_pad, start, WINDOW + BLOCK, 0)
        scores = block_scores(query_block, pairs[..., :HD], start)
        maximum = jnp.max(scores, axis=-1, keepdims=True)
        logsum = maximum + jnp.log(jnp.sum(jnp.exp(scores - maximum), axis=-1, keepdims=True))
        probs = jnp.exp(scores - logsum).astype(jnp.bfloat16)
        mixed = jnp.einsum(
            "snac,csd->asnd", probs, pairs[..., HD:], preferred_element_type=jnp.float32
        )
        return (mixed.astype(jnp.bfloat16), logsum[..., 0])

    mixed, logsum = lax.map(one_block, starts)
    return (mixed.reshape(query.shape), logsum)


def attend_backward(query, keyval, logsum, grad_mixed):
    length = query.shape[0]
    key_pad = padded_pairs(keyval)
    starts = jnp.arange(length // BLOCK, dtype=jnp.int32) * BLOCK
    scale = HD ** (-0.5)

    def one_block(carry, element):
        start, block_logsum = element
        query_block = lax.dynamic_slice_in_dim(query, start, BLOCK, 0)
        grad_block = lax.dynamic_slice_in_dim(grad_mixed, start, BLOCK, 0)
        pairs = lax.dynamic_slice_in_dim(key_pad, start, WINDOW + BLOCK, 0)
        keys = pairs[..., :HD]
        values = pairs[..., HD:]
        probs = jnp.exp(block_scores(query_block, keys, start) - block_logsum[..., None])
        grad_probs = jnp.einsum(
            "asnd,csd->snac", grad_block, values, preferred_element_type=jnp.float32
        )
        inner = jnp.sum(probs * grad_probs, axis=-1, keepdims=True)
        grad_scores = (probs * (grad_probs - inner)).astype(jnp.bfloat16)
        grad_query = scale * jnp.einsum(
            "snac,csd->asnd", grad_scores, keys, preferred_element_type=jnp.float32
        )
        grad_keys = scale * jnp.einsum(
            "snac,asnd->csd", grad_scores, query_block, preferred_element_type=jnp.float32
        )
        grad_values = jnp.einsum(
            "snac,asnd->csd",
            probs.astype(jnp.bfloat16),
            grad_block,
            preferred_element_type=jnp.float32,
        )
        current = lax.dynamic_slice_in_dim(carry, start, WINDOW + BLOCK, 0)
        update = jnp.concatenate([grad_keys, grad_values], -1)
        carry = lax.dynamic_update_slice_in_dim(carry, current + update, start, 0)
        return (carry, grad_query.astype(jnp.bfloat16))

    initial = jnp.zeros((WINDOW + length,) + keyval.shape[1:], jnp.float32)
    carry, grad_query = lax.scan(one_block, initial, (starts, logsum))
    return (grad_query.reshape(query.shape), carry[WINDOW:])


def geglu(gate_in, up_in):
    return jax.nn.gelu(gate_in) * up_in


def local(tokens, w_query, w_keyval, w_out, w_gate, w_up, w_down, gain_attn, gain_mlp, cotangent):
    query_full, keyval_full, out_full, gain_one = (
        lax.all_gather(w_query.astype(jnp.bfloat16), "shard", axis=0, tiled=True),
        lax.all_gather(w_keyval.astype(jnp.bfloat16), "shard", axis=0, tiled=True),
        lax.all_gather(w_out.astype(jnp.bfloat16), "shard", axis=1, tiled=True),
        lax.all_gather(gain_attn.astype(jnp.bfloat16), "shard", axis=0, tiled=True),
    )
    row_count = tokens.shape[0]
    seq_count = tokens.shape[1]
    tp_start = lax.axis_index("tp") * row_count
    gain_first = gain_one.astype(jnp.float32)
    inputs = tokens.astype(jnp.float32)
    normed = lax.all_gather(
        rms_scale(inputs, gain_first).astype(jnp.bfloat16), "tp", axis=0, tiled=True
    )
    length = normed.shape[0]
    query = jnp.dot(normed, query_full, preferred_element_type=jnp.float32).astype(jnp.bfloat16)
    keyval = jnp.dot(normed, keyval_full, preferred_element_type=jnp.float32).astype(jnp.bfloat16)
    head_count = query.shape[-1] // HD
    query_heads = query.reshape(length, seq_count, head_count, HD)
    mixed_heads, logsum = attend_forward(query_heads, keyval)
    mixed = mixed_heads.reshape(length, seq_count, head_count * HD)
    gate_full, up_full, down_full, gain_two = (
        lax.all_gather(w_gate.astype(jnp.bfloat16), "shard", axis=0, tiled=True),
        lax.all_gather(w_up.astype(jnp.bfloat16), "shard", axis=0, tiled=True),
        lax.all_gather(w_down.astype(jnp.bfloat16), "shard", axis=1, tiled=True),
        lax.all_gather(gain_mlp.astype(jnp.bfloat16), "shard", axis=0, tiled=True),
    )
    gain_second = gain_two.astype(jnp.float32)
    hidden_rows = inputs + lax.psum_scatter(
        jnp.dot(mixed, out_full, preferred_element_type=jnp.float32),
        "tp",
        scatter_dimension=0,
        tiled=True,
    )
    feedforward_normed_input = lax.all_gather(
        rms_scale(hidden_rows, gain_second).astype(jnp.bfloat16), "tp", axis=0, tiled=True
    )
    gate = jnp.dot(feedforward_normed_input, gate_full, preferred_element_type=jnp.float32)
    upward = jnp.dot(feedforward_normed_input, up_full, preferred_element_type=jnp.float32)
    gated_product = geglu(gate, upward).astype(jnp.bfloat16)
    output = (
        hidden_rows
        + lax.psum_scatter(
            jnp.dot(gated_product, down_full, preferred_element_type=jnp.float32).astype(
                jnp.bfloat16
            ),
            "tp",
            scatter_dimension=0,
            tiled=True,
        ).astype(jnp.float32)
    ).astype(jnp.bfloat16)
    query_back, keyval_back, out_back, gate_back, up_back, down_projection_backward = (
        lax.all_gather(w_query.astype(jnp.bfloat16), "shard", axis=0, tiled=True),
        lax.all_gather(w_keyval.astype(jnp.bfloat16), "shard", axis=0, tiled=True),
        lax.all_gather(w_out.astype(jnp.bfloat16), "shard", axis=1, tiled=True),
        lax.all_gather(w_gate.astype(jnp.bfloat16), "shard", axis=0, tiled=True),
        lax.all_gather(w_up.astype(jnp.bfloat16), "shard", axis=0, tiled=True),
        lax.all_gather(w_down.astype(jnp.bfloat16), "shard", axis=1, tiled=True),
    )
    grad_product = jnp.einsum(
        "eut,kt->euk", cotangent, down_projection_backward, preferred_element_type=jnp.float32
    )
    down_weight_gradient = jnp.einsum(
        "tij,tiy->jy", gated_product, cotangent, preferred_element_type=jnp.float32
    )
    unused_value, geglu_pull = jax.vjp(geglu, gate, upward)
    gate_activation_gradient, up_activation_gradient = geglu_pull(grad_product)
    gate_activation_gradient = gate_activation_gradient.astype(jnp.bfloat16)
    up_activation_gradient = up_activation_gradient.astype(jnp.bfloat16)
    first = jnp.einsum(
        "rsf,df->rsd", gate_activation_gradient, gate_back, preferred_element_type=jnp.float32
    )
    grad_normed_mlp = lax.psum_scatter(
        (
            first
            + jnp.einsum(
                "rsf,df->rsd", up_activation_gradient, up_back, preferred_element_type=jnp.float32
            )
        ).astype(jnp.bfloat16),
        "tp",
        scatter_dimension=0,
        tiled=True,
    ).astype(jnp.float32)
    grad_gate = jnp.einsum(
        "xhk,xhz->kz",
        feedforward_normed_input,
        gate_activation_gradient,
        preferred_element_type=jnp.float32,
    )
    up_weight_gradient = jnp.einsum(
        "xhk,xhz->kz",
        feedforward_normed_input,
        up_activation_gradient,
        preferred_element_type=jnp.float32,
    )
    mlp_grads = (
        lax.psum_scatter(
            grad_gate.astype(jnp.bfloat16), "shard", scatter_dimension=0, tiled=True
        ).astype(jnp.float32),
        lax.psum_scatter(
            up_weight_gradient.astype(jnp.bfloat16), "shard", scatter_dimension=0, tiled=True
        ).astype(jnp.float32),
        lax.psum_scatter(
            down_weight_gradient.astype(jnp.bfloat16), "shard", scatter_dimension=1, tiled=True
        ).astype(jnp.float32),
    )
    unused_norm, second_pull = jax.vjp(rms_scale, hidden_rows, gain_second)
    grad_hidden_norm, gain_second_part = second_pull(grad_normed_mlp)
    grad_out_rows = lax.dynamic_slice_in_dim(cotangent, tp_start, row_count, 0).astype(jnp.float32)
    grad_hidden = grad_out_rows + grad_hidden_norm
    grad_branch = lax.all_gather(grad_hidden.astype(jnp.bfloat16), "tp", axis=0, tiled=True)
    grad_mixed = jnp.einsum(
        "lsd,kd->lsk", grad_branch, out_back, preferred_element_type=jnp.float32
    ).astype(jnp.bfloat16)
    grad_out = jnp.einsum("lsk,lsd->kd", mixed, grad_branch, preferred_element_type=jnp.float32)
    grad_query_heads, grad_keyval_part = attend_backward(
        query_heads, keyval, logsum, grad_mixed.reshape(length, seq_count, head_count, HD)
    )
    grad_keyval_act = lax.psum(grad_keyval_part.astype(jnp.bfloat16), "tp")
    grad_query_act = grad_query_heads.reshape(length, seq_count, head_count * HD)
    grad_query = jnp.einsum(
        "lsd,lsk->dk", normed, grad_query_act, preferred_element_type=jnp.float32
    )
    grad_keyval = jnp.einsum(
        "lsd,lsk->dk", normed, grad_keyval_act, preferred_element_type=jnp.float32
    )
    own_keyval = lax.dynamic_slice_in_dim(grad_keyval_act, tp_start, row_count, 0)
    grad_normed = lax.psum_scatter(
        jnp.einsum(
            "rsk,dk->rsd", grad_query_act, query_back, preferred_element_type=jnp.float32
        ).astype(jnp.bfloat16),
        "tp",
        scatter_dimension=0,
        tiled=True,
    ).astype(jnp.float32)
    grad_normed = grad_normed + jnp.einsum(
        "rsk,dk->rsd", own_keyval, keyval_back, preferred_element_type=jnp.float32
    )
    unused_first, first_pull = jax.vjp(rms_scale, inputs, gain_first)
    grad_inputs, gain_first_part = first_pull(grad_normed)
    grad_tokens = grad_hidden + grad_inputs
    gain_first_sum, gain_second_sum = lax.psum((gain_first_part, gain_second_part), "tp")
    attn_grads = (
        lax.psum_scatter(
            grad_query.astype(jnp.bfloat16), "shard", scatter_dimension=0, tiled=True
        ).astype(jnp.float32),
        lax.psum_scatter(
            grad_keyval.astype(jnp.bfloat16), "shard", scatter_dimension=0, tiled=True
        ).astype(jnp.float32),
        lax.psum_scatter(
            grad_out.astype(jnp.bfloat16), "shard", scatter_dimension=1, tiled=True
        ).astype(jnp.float32),
        lax.psum_scatter(
            gain_first_sum.astype(jnp.bfloat16), "shard", scatter_dimension=0, tiled=True
        ).astype(jnp.float32),
        lax.psum_scatter(
            gain_second_sum.astype(jnp.bfloat16), "shard", scatter_dimension=0, tiled=True
        ).astype(jnp.float32),
    )
    return (
        output,
        grad_tokens,
        attn_grads[0],
        attn_grads[1],
        attn_grads[2],
        mlp_grads[0],
        mlp_grads[1],
        mlp_grads[2],
        attn_grads[3],
        attn_grads[4],
    )


def solution(mesh):
    in_specs = (
        P("tp", "shard", None),
        P("shard", "tp"),
        P("shard", None),
        P("tp", "shard"),
        P("shard", "tp"),
        P("shard", "tp"),
        P("tp", "shard"),
        P("shard"),
        P("shard"),
        P(None, "shard", None),
    )
    out_specs = (
        P("tp", "shard", None),
        P("tp", "shard", None),
        P("shard", "tp"),
        P("shard", None),
        P("tp", "shard"),
        P("shard", "tp"),
        P("shard", "tp"),
        P("tp", "shard"),
        P("shard"),
        P("shard"),
    )
    return jax.shard_map(local, mesh=mesh, in_specs=in_specs, out_specs=out_specs, check_vma=False)
```

profile of v0, /device:TPU:0, one launch (start us, length us, event | category | flops | bytes accessed | tf_op | source)
XLA Modules:
  0.0 1546.1 jit_solution(9011149128958545960)
XLA Ops:
  12.9 23.3 %all-reduce.7 = (bf16[1536]{0:T(1024)(128)(2,1)S(1)}, bf16[1536]{0:T(1024)(128)(2,1)S(1)}) all-reduce(bf16[1536]{0:T(1024)(128)(2,1)S(1)} %dynamic-update-slice, bf16[1536]{0:T(1024)(128)(2,1)S(1)} %dynamic-update-slice.1), channel_id=1, replica_groups=mesh['shard'=8,'tp'=4] {'shard'}, use_global_device_ids=true, to_apply=%add.1 | all-reduce | flops 3072 | bytes 12288
  41.8 32.9 %all_gather.41 = bf16[1536,256]{1,0:T(8,128)(2,1)S(1)} all-gather(bf16[192,256]{1,0:T(8,128)(2,1)S(1)} %convert_element_type.187), channel_id=1, replica_groups=mesh['shard'=8,'tp'=4] {'shard'}, dimensions={0}, use_global_device_ids=true | all-gather | bytes 884736 | tf_op jit(solution)/shard_map/all_gather | solution.py:106
  74.7 33.0 %all-gather.9.cloned.1.call-done = bf16[2048,1,1536]{2,0,1:T(8,128)(2,1)} async-done(((bf16[512,1,1536]{2,0,1:T(8,128)(2,1)}), bf16[2048,1,1536]{2,0,1:T(8,128)(2,1)}) %all-gather.9.cloned.1.call-update) | async-done | bytes 6291472 | tf_op jit(solution)/shard_map/all_gather | solution.py:115
  120.4 57.1 %while.24 = (s32[]{:T(128)}, bf16[4,512,1,3,128]{1,4,3,2,0:T(8,128)(2,1)S(1)}, f32[4,1,3,512]{3,2,1,0:T(4,128)S(1)}, s32[4]{0:T(128)S(1)}, bf16[3072,1,256]{2,0,...) while((s32[]{:T(128)}, ...), condition=%wide.region_4.5_spmd, body=%wide.region_1.4_spmd.sunk | while | flops 1238041088 | bytes 33096952 | solution.py:54
  189.5 97.2 %reduce-scatter.11.cloned.1.call-done = f32[512,1,1536]{2,0,1:T(8,128)} async-done(((f32[2048,1,1536]{2,0,1:T(8,128)}), f32[512,1,1536]{2,0,1:T(8,128)}) %reduce-scatter.11.cloned.1.call-update) | async-done | bytes 3145744 | tf_op jit(solution)/shard_map/reduce_scatter | solution.py:132
  295.4 59.1 %all-gather.19.cloned.1.call-done = bf16[1536,1152]{1,0:T(8,128)(2,1)} async-done(((bf16[192,1152]{1,0:T(8,128)(2,1)}), bf16[1536,1152]{1,0:T(8,128)(2,1)}) %all-gather.19.cloned.1.call-update) | async-done | bytes 3538960 | tf_op jit(solution)/shard_map/all_gather | solution.py:127
  354.5 46.9 %all-gather.15.cloned.1.call-done = bf16[2048,1,1536]{2,0,1:T(8,128)(2,1)} async-done(((bf16[512,1,1536]{2,0,1:T(8,128)(2,1)}), bf16[2048,1,1536]{2,0,1:T(8,128)(2,1)}) %all-gather.15.cloned.1.call-update) | async-done | bytes 6291472 | tf_op jit(solution)/shard_map/all_gather | solution.py:138
  414.9 54.4 %all-gather.17.cloned.1.call-done = bf16[1536,1152]{1,0:T(8,128)(2,1)} async-done(((bf16[192,1152]{1,0:T(8,128)(2,1)}), bf16[1536,1152]{1,0:T(8,128)(2,1)}) %all-gather.17.cloned.1.call-update) | async-done | bytes 3538960 | tf_op jit(solution)/shard_map/all_gather | solution.py:126
  469.3 13.6 fusion.81
  483.0 52.9 %all-gather.21.cloned.1.call-done = bf16[1152,1536]{0,1:T(8,128)(2,1)} async-done(((bf16[1152,192]{0,1:T(8,128)(2,1)}), bf16[1152,1536]{0,1:T(8,128)(2,1)}) %all-gather.21.cloned.1.call-update) | async-done | bytes 3538960 | tf_op jit(solution)/shard_map/all_gather | solution.py:128
  535.8 23.9 %multiply_convert_fusion = (bf16[2048,1152]{1,0:T(8,128)(2,1)}, bf16[2048,1152]{1,0:T(8,128)(2,1)}, bf16[2048,1152]{1,0:T(8,128)(2,1)}) fusion(f32[2048,1152]{1,0:T(8,128)} %fusion.81, f32[2048,1152]{1,0:T(8,128)} %fusion.79, bf16[1152,1536]{0,1:T(8,128)(2,1)} %all-gather.21.cloned.1.call-done, bf16[2048,1,1536]{2,0,1:T(8,128)(2,1)} %param.23), kind=kOutput, calls=%fused_computation.83 | convolution fusion | flops 7309099008 | bytes 42860544 | tf_op jit(solution)/shard_map/eut,kt->euk/dot_general | solution.py:163
  559.7 14.6 fusion.133
  587.0 56.9 %reduce-scatter.15.cloned.1.call-done = bf16[512,1,1536]{2,0,1:T(8,128)(2,1)} async-done(((bf16[2048,1,1536]{2,0,1:T(8,128)(2,1)}), bf16[512,1,1536]{2,0,1:T(8,128)(2,1)}) %reduce-scatter.15.cloned.1.call-update) | async-done | bytes 1572880 | tf_op jit(solution)/shard_map/reduce_scatter | solution.py:176
  651.2 46.5 %all-gather.23.cloned.1.call-done = bf16[2048,1,1536]{2,0,1:T(8,128)(2,1)} async-done(((bf16[512,1,1536]{2,0,1:T(8,128)(2,1)}), bf16[2048,1,1536]{2,0,1:T(8,128)(2,1)}) %all-gather.23.cloned.1.call-update) | async-done | bytes 6291472 | tf_op jit(solution)/shard_map/all_gather | solution.py:214
  707.9 181.3 %while.25 = (s32[]{:T(128)}, f32[3072,1,256]{0,2,1:T(8,128)}, bf16[4,512,1,3,128]{1,4,3,2,0:T(8,128)(2,1)}, s32[4]{0:T(128)S(1)}, bf16[2048,1,3,128]{3,0,2,1:T(8...) while((s32[]{:T(128)}, f32[3072,1,256]{0,2,1:T(8,128)}, ...), condition=%wide.region_12.13_spmd, body=%wide.region_10.12_spmd.sunk | while | flops 3046441472 | bytes 154180960 | solution.py:95
  977.4 33.8 %reduce-scatter.29.cloned.1.call-done = bf16[1152,192]{0,1:T(8,128)(2,1)} async-done(((bf16[1152,1536]{0,1:T(8,128)(2,1)}), bf16[1152,192]{0,1:T(8,128)(2,1)}) %reduce-scatter.29.cloned.1.call-update) | async-done | bytes 442384 | tf_op jit(solution)/shard_map/reduce_scatter | solution.py:206
  1013.2 80.2 %reduce-scatter.27.cloned.1.call-done = bf16[192,1152]{1,0:T(8,128)(2,1)} async-done(((bf16[1536,1152]{1,0:T(8,128)(2,1)}), bf16[192,1152]{1,0:T(8,128)(2,1)}) %reduce-scatter.27.cloned.1.call-update) | async-done | bytes 442384 | tf_op jit(solution)/shard_map/reduce_scatter | solution.py:203
  1095.4 80.2 %reduce-scatter.25.cloned.1.call-done = bf16[192,1152]{1,0:T(8,128)(2,1)} async-done(((bf16[1536,1152]{1,0:T(8,128)(2,1)}), bf16[192,1152]{1,0:T(8,128)(2,1)}) %reduce-scatter.25.cloned.1.call-update) | async-done | bytes 442384 | tf_op jit(solution)/shard_map/reduce_scatter | solution.py:200
  1177.6 63.2 %reduce-scatter.21.cloned.1.call-done = bf16[192,256]{1,0:T(8,128)(2,1)} async-done(((bf16[1536,256]{1,0:T(8,128)(2,1)}), bf16[192,256]{1,0:T(8,128)(2,1)}) %reduce-scatter.21.cloned.1.call-update) | async-done | bytes 98320 | tf_op jit(solution)/shard_map/reduce_scatter | solution.py:250
  1242.4 65.6 %reduce-scatter.23.cloned.1.call-done = bf16[384,192]{0,1:T(8,128)(2,1)} async-done(((bf16[384,1536]{0,1:T(8,128)(2,1)}), bf16[384,192]{0,1:T(8,128)(2,1)}) %reduce-scatter.23.cloned.1.call-update) | async-done | bytes 147472 | tf_op jit(solution)/shard_map/reduce_scatter | solution.py:253
  1309.6 65.6 %reduce-scatter.19.cloned.1.call-done = bf16[192,384]{1,0:T(8,128)(2,1)} async-done(((bf16[1536,384]{1,0:T(8,128)(2,1)}), bf16[192,384]{1,0:T(8,128)(2,1)}) %reduce-scatter.19.cloned.1.call-update) | async-done | bytes 147472 | tf_op jit(solution)/shard_map/reduce_scatter | solution.py:247
  1376.9 58.2 %reduce-scatter.17.cloned.1.call-done = bf16[512,1,1536]{2,0,1:T(8,128)(2,1)} async-done(((bf16[2048,1,1536]{2,0,1:T(8,128)(2,1)}), bf16[512,1,1536]{2,0,1:T(8,128)(2,1)}) %reduce-scatter.17.cloned.1.call-update) | async-done | bytes 1572880 | tf_op jit(solution)/shard_map/reduce_scatter | solution.py:231
  1440.3 55.8 %reduce-scatter.13.cloned.1.call-done = bf16[512,1,1536]{2,0,1:T(8,128)(2,1)} async-done(((bf16[2048,1,1536]{2,0,1:T(8,128)(2,1)}), bf16[512,1,1536]{2,0,1:T(8,128)(2,1)}) %reduce-scatter.13.cloned.1.call-update) | async-done | bytes 1572880 | tf_op jit(solution)/shard_map/reduce_scatter | solution.py:146
  1516.7 21.7 %all-reduce.6 = (bf16[1536]{0:T(1024)(128)(2,1)S(1)}, bf16[1536]{0:T(1024)(128)(2,1)S(1)}) all-reduce(bf16[1536]{0:T(1024)(128)(2,1)S(1)} %get-tuple-element.194, bf16[1536]{0:T(1024)(128)(2,1)S(1)} %get-tuple-element.195), channel_id=12, replica_groups=mesh['shard'=8,'tp'=4] {'shard'}, use_global_device_ids=true, to_apply=%region_24.25.clone | all-reduce | flops 3072 | bytes 12288
  (269 shorter events, 418.2 us)
Async XLA Ops:
  7.2 67.5 %all-gather.11.cloned.1.call-start = ((), (), s32[]{:S(2)}) async-start(), calls=%async_computation.11 | async-start | bytes 1327104 | tf_op jit(solution)/shard_map/all_gather | solution.py:105
  9.0 98.7 %all-gather.9.cloned.1.call-start = ((), (), s32[]{:S(2)}) async-start(), calls=%async_computation.10 | async-start | bytes 7864320 | tf_op jit(solution)/shard_map/all_gather | solution.py:115
  40.9 138.3 %all-gather.13.cloned.1.call-start = ((), (), s32[]{:S(2)}) async-start(), calls=%async_computation.12 | async-start | bytes 1327104 | tf_op jit(solution)/shard_map/all_gather | solution.py:107
  41.7 244.9 %reduce-scatter.11.cloned.1.call-start = ((), (), s32[]{:S(2)}) async-start(), calls=%async_computation.13 | async-start | bytes 15728640 | tf_op jit(solution)/shard_map/reduce_scatter | solution.py:132
  187.4 167.0 %all-gather.19.cloned.1.call-start = ((), (), s32[]{:S(2)}) async-start(), calls=%async_computation.16 | async-start | bytes 3981312 | tf_op jit(solution)/shard_map/all_gather | solution.py:127
  189.4 211.9 %all-gather.15.cloned.1.call-start = ((), (), s32[]{:S(2)}) async-start(), calls=%async_computation.14 | async-start | bytes 7864320 | tf_op jit(solution)/shard_map/all_gather | solution.py:138
  189.5 457.6 %copy-start.14 = (f32[1536]{0:T(1024)}, f32[1536]{0:T(1024)S(1)}, u32[]{:S(2)}) copy-start(f32[1536]{0:T(1024)S(1)} %convert_element_type.194) | copy-start | bytes 18436
  289.5 357.6 %copy-start.2 = (f32[512,1,1536]{2,0,1:T(8,128)}, f32[512,1,1536]{2,0,1:T(8,128)S(1)}, u32[]{:S(2)}) copy-start(f32[512,1,1536]{2,0,1:T(8,128)S(1)} %get-tuple-element.203) | copy-start | bytes 9437188
  289.5 357.6 %copy-start.19 = (f32[512]{0:T(512)}, f32[512]{0:T(512)S(1)}, u32[]{:S(2)}) copy-start(f32[512]{0:T(512)S(1)} %fusion.129) | copy-start | bytes 6148
  291.2 178.1 %all-gather.17.cloned.1.call-start = ((), (), s32[]{:S(2)}) async-start(), calls=%async_computation.15 | async-start | bytes 3981312 | tf_op jit(solution)/shard_map/all_gather | solution.py:126
  293.3 242.5 %all-gather.21.cloned.1.call-start = ((), (), s32[]{:S(2)}) async-start(), calls=%async_computation.17 | async-start | bytes 3981312 | tf_op jit(solution)/shard_map/all_gather | solution.py:128
  295.3 348.7 %reduce-scatter.15.cloned.1.call-start = ((), (), s32[]{:S(2)}) async-start(), calls=%async_computation.19 | async-start | bytes 7864320 | tf_op jit(solution)/shard_map/reduce_scatter | solution.py:176
  587.0 110.8 %all-gather.23.cloned.1.call-start = ((), (), s32[]{:S(2)}) async-start(), calls=%async_computation.20 | async-start | bytes 7864320 | tf_op jit(solution)/shard_map/all_gather | solution.py:214
  651.2 281.0 %all-reduce.10.cloned.1.call-start = ((), (), s32[]{:S(2)}) async-start(), calls=%async_computation.22 | async-start | bytes 2097152 | tf_op jit(solution)/shard_map/psum | solution.py:222
  892.0 119.2 %reduce-scatter.29.cloned.1.call-start = ((), (), s32[]{:S(2)}) async-start(), calls=%async_computation.28 | async-start | bytes 3981312 | tf_op jit(solution)/shard_map/reduce_scatter | solution.py:206
  905.4 188.0 %reduce-scatter.27.cloned.1.call-start = ((), (), s32[]{:S(2)}) async-start(), calls=%async_computation.27 | async-start | bytes 3981312 | tf_op jit(solution)/shard_map/reduce_scatter | solution.py:203
  918.6 257.0 %reduce-scatter.25.cloned.1.call-start = ((), (), s32[]{:S(2)}) async-start(), calls=%async_computation.26 | async-start | bytes 3981312 | tf_op jit(solution)/shard_map/reduce_scatter | solution.py:200
  932.1 308.7 %reduce-scatter.21.cloned.1.call-start = ((), (), s32[]{:S(2)}) async-start(), calls=%async_computation.24 | async-start | bytes 884736 | tf_op jit(solution)/shard_map/reduce_scatter | solution.py:250
  938.1 369.9 %reduce-scatter.23.cloned.1.call-start = ((), (), s32[]{:S(2)}) async-start(), calls=%async_computation.25 | async-start | bytes 1327104 | tf_op jit(solution)/shard_map/reduce_scatter | solution.py:253
  945.8 429.5 %reduce-scatter.19.cloned.1.call-start = ((), (), s32[]{:S(2)}) async-start(), calls=%async_computation.23 | async-start | bytes 1327104 | tf_op jit(solution)/shard_map/reduce_scatter | solution.py:247
  956.6 478.5 %reduce-scatter.17.cloned.1.call-start = ((), (), s32[]{:S(2)}) async-start(), calls=%async_computation.21 | async-start | bytes 7864320 | tf_op jit(solution)/shard_map/reduce_scatter | solution.py:231
  962.1 534.0 %reduce-scatter.13.cloned.1.call-start = ((), (), s32[]{:S(2)}) async-start(), calls=%async_computation.18 | async-start | bytes 7864320 | tf_op jit(solution)/shard_map/reduce_scatter | solution.py:146
  976.7 458.4 %copy-start.18 = (f32[1536]{0:T(1024)S(1)}, f32[1536]{0:T(1024)}, u32[]{:S(2)}) copy-start(f32[1536]{0:T(1024)} %copy-done.17) | copy-start | bytes 18436
  976.7 458.4 %copy-start.27 = (f32[512]{0:T(512)S(1)}, f32[512]{0:T(512)}, u32[]{:S(2)}) copy-start(f32[512]{0:T(512)} %copy-done.26) | copy-start | bytes 6148
  (36 other events, 755.1 us)
Sparse Core Ops, SparseCore 0:
  10.8 49.2 all-gather.10
  62.2 45.4 all-gather.8
  110.5 41.0 all-gather.12
  187.6 99.0 reduce-scatter.10
  289.2 65.1 all-gather.18
  356.5 44.8 all-gather.14
  404.1 65.1 all-gather.16
  472.1 63.6 all-gather.20
  587.1 56.8 reduce-scatter.14
  651.3 46.3 all-gather.22
  892.1 36.0 all-reduce.9
  931.7 79.4 reduce-scatter.28
  1014.9 78.4 reduce-scatter.26
  1096.9 78.7 reduce-scatter.24
  1178.8 62.0 reduce-scatter.20
  1245.0 62.9 reduce-scatter.22
  1312.2 63.0 reduce-scatter.18
  1377.8 57.2 reduce-scatter.16
  1437.7 58.3 reduce-scatter.12
where the time goes:
time: 1550 us
  waiting for transfers between devices  950 us (61%)
  matrix products  292 us (19%)
  other arithmetic  105 us (7%)
  blocking collectives  88.1 us (6%)
  local copies, waits for them, and re-layouts  61.7 us (4%)
  loops' own time  32 us (2%)
  between operations  16.2 us (1%)
    reduce_scatter x1, waiting for transfers between devices, local(): lax.psum_scatter(jnp.dot(mixed, out_full, preferred_element_type=jnp.floa...  97.2 us
    reduce_scatter x1, waiting for transfers between devices, local(): lax.psum_scatter(grad_gate.astype(jnp.bfloat16), 'shard', scatter_dimensi...  80.2 us
    reduce_scatter x1, waiting for transfers between devices, local(): lax.psum_scatter(up_weight_gradient.astype(jnp.bfloat16), 'shard', scatte...  80.2 us
    reduce_scatter x1, waiting for transfers between devices, local(): lax.psum_scatter(grad_query.astype(jnp.bfloat16), 'shard', scatter_dimens...  65.6 us
    reduce_scatter x1, waiting for transfers between devices, local(): lax.psum_scatter(grad_out.astype(jnp.bfloat16), 'shard', scatter_dimensio...  65.6 us
    reduce_scatter x1, waiting for transfers between devices, local(): lax.psum_scatter(grad_keyval.astype(jnp.bfloat16), 'shard', scatter_dimen...  63.2 us
    all_gather x1, waiting for transfers between devices, local(): lax.all_gather(w_up.astype(jnp.bfloat16), 'shard', axis=0, tiled=True)  59.1 us
    reduce_scatter x1, waiting for transfers between devices, local(): lax.psum_scatter(jnp.einsum('rsk,dk->rsd', grad_query_act, query_back, pr...  58.2 us
  transfers between devices with their start and end apart: 19, of which 16 were waited for; matrix products, arithmetic and copies ran while one was open for 13% of the time, Pallas kernels for 0%

commit v1 on v0

v1 whole, which is shorter than its diff:
```python
import functools

import jax
import jax.numpy as jnp
from jax import lax
from jax.experimental import pallas as pl
from jax.experimental.pallas import tpu as pltpu
from jax.sharding import PartitionSpec as P

HD = 128
WINDOW = 1024
QB = 256
GROUP = 3
EPS = 1e-06
LOG2E = 1.4426950408889634
LN2 = 0.6931471805599453
NEG = -1e30
BF = jnp.bfloat16
F32 = jnp.float32
NT = (((1,), (1,)), ((), ()))
TN = (((0,), (0,)), ((), ()))
NN = (((1,), (0,)), ((), ()))


def dot(a, b, dims=NN):
    return lax.dot_general(a, b, dims, preferred_element_type=F32)


def after(value, *others):
    return lax.optimization_barrier((value, *others))[0]


def forward_attention_kernel(chip_ref, q_ref, k_ref, vt_ref, o_ref, lse_ref):
    block = pl.program_id(0)
    chunks = WINDOW // QB
    key_row = lax.broadcasted_iota(jnp.int32, (QB, QB), 0)
    query_col = lax.broadcasted_iota(jnp.int32, (QB, QB), 1)

    def rows_of(chunk):
        return pl.ds(pl.multiple_of((block + chunk) * QB, QB), QB)

    def finish(head, top, total, mixed):
        cols = slice(head * HD, (head + 1) * HD)
        o_ref[:, cols] = jnp.transpose(mixed / total).astype(BF)
        lse_ref[head : head + 1, :] = top + jnp.log(total) * LOG2E

    @pl.when(chip_ref[0] != 0)
    def _():
        for head in range(GROUP):
            query = q_ref[:, head * HD : (head + 1) * HD]
            scores = []
            for chunk in range(chunks + 1):
                part = dot(k_ref[rows_of(chunk), :], query, NT)
                if chunk == 0:
                    part = jnp.where(key_row > query_col, part, NEG)
                if chunk == chunks:
                    part = jnp.where(key_row <= query_col, part, NEG)
                scores.append(part)
            top = jnp.max(functools.reduce(jnp.maximum, scores), axis=0, keepdims=True)
            total = jnp.zeros((1, QB), F32)
            mixed = jnp.zeros((HD, QB), F32)
            for chunk in range(chunks + 1):
                probs = jnp.exp2(scores[chunk] - top)
                total = total + jnp.sum(probs, axis=0, keepdims=True)
                mixed = mixed + dot(vt_ref[:, rows_of(chunk)], probs.astype(BF))
            finish(head, top, total, mixed)

    @pl.when(chip_ref[0] == 0)
    def _():
        for head in range(GROUP):
            query = q_ref[:, head * HD : (head + 1) * HD]

            def step(chunk, carry):
                top, total, mixed = carry
                part = dot(k_ref[rows_of(chunk), :], query, NT)
                part = jnp.where((key_row <= query_col) | (chunk < chunks), part, NEG)
                new_top = jnp.maximum(top, jnp.max(part, axis=0, keepdims=True))
                shrink = jnp.exp2(top - new_top)
                probs = jnp.exp2(part - new_top)
                total = total * shrink + jnp.sum(probs, axis=0, keepdims=True)
                mixed = mixed * shrink + dot(vt_ref[:, rows_of(chunk)], probs.astype(BF))
                return (new_top, total, mixed)

            first = (jnp.full((1, QB), NEG, F32), jnp.zeros((1, QB), F32), jnp.zeros((HD, QB), F32))
            top, total, mixed = lax.fori_loop(chunks - block, chunks + 1, step, first)
            finish(head, top, total, mixed)


def forward_attention(chip, query, keys, values_t):
    rows = query.shape[0]
    width = GROUP * HD
    return pl.pallas_call(
        forward_attention_kernel,
        grid_spec=pltpu.PrefetchScalarGridSpec(
            num_scalar_prefetch=1,
            grid=(rows // QB,),
            in_specs=[
                pl.BlockSpec((QB, width), lambda b, s: (b, 0)),
                pl.BlockSpec((2 * rows, HD), lambda b, s: (0, 0)),
                pl.BlockSpec((HD, 2 * rows), lambda b, s: (0, 0)),
            ],
            out_specs=[
                pl.BlockSpec((QB, width), lambda b, s: (b, 0)),
                pl.BlockSpec((8, QB), lambda b, s: (0, b)),
            ],
        ),
        out_shape=(
            jax.ShapeDtypeStruct((rows, width), BF),
            jax.ShapeDtypeStruct((8, rows), F32),
        ),
        compiler_params=pltpu.CompilerParams(vmem_limit_bytes=40 << 20),
        cost_estimate=pl.CostEstimate(
            flops=9_000_000_000, transcendentals=4_000_000, bytes_accessed=4_000_000
        ),
        name="attention_forward",
    )(chip, query, keys, values_t)


def backward_attention_kernel(
    chip_ref, q_ref, g_ref, o_ref, lse_ref, k_ref, kt_ref, v_ref, dq_ref, dk_ref, dv_ref
):
    block = pl.program_id(0)
    chunks = WINDOW // QB
    key_row = lax.broadcasted_iota(jnp.int32, (QB, QB), 0)
    query_col = lax.broadcasted_iota(jnp.int32, (QB, QB), 1)

    @pl.when(block == 0)
    def _():
        dk_ref[...] = jnp.zeros_like(dk_ref)
        dv_ref[...] = jnp.zeros_like(dv_ref)

    def rows_of(chunk):
        return pl.ds(pl.multiple_of((block + chunk) * QB, QB), QB)

    deltas = []
    for head in range(GROUP):
        cols = slice(head * HD, (head + 1) * HD)
        both = g_ref[:, cols].astype(F32) * o_ref[:, cols].astype(F32)
        deltas.append(jnp.sum(jnp.transpose(both), axis=0, keepdims=True))

    def one_chunk(chunk, keep, totals):
        rows = rows_of(chunk)
        keys = k_ref[rows, :]
        values = v_ref[rows, :]
        keys_t = kt_ref[:, rows]
        grad_keys = jnp.zeros((QB, HD), F32)
        grad_values = jnp.zeros((QB, HD), F32)
        new = []
        for head in range(GROUP):
            cols = slice(head * HD, (head + 1) * HD)
            query = q_ref[:, cols]
            grad = g_ref[:, cols]
            probs = jnp.exp2(dot(keys, query, NT) - lse_ref[head : head + 1, :])
            if keep is not None:
                probs = jnp.where(keep, probs, 0.0)
            grad_scores = (probs * (dot(values, grad, NT) - deltas[head])).astype(BF)
            grad_values = grad_values + dot(probs.astype(BF), grad)
            grad_keys = grad_keys + dot(grad_scores, query)
            new.append(totals[head] + dot(keys_t, grad_scores))
        dk_ref[rows, :] += grad_keys
        dv_ref[rows, :] += grad_values
        return tuple(new)

    def finish(totals):
        for head in range(GROUP):
            cols = slice(head * HD, (head + 1) * HD)
            dq_ref[:, cols] = (jnp.transpose(totals[head]) * HD ** (-0.5)).astype(BF)

    zeros = tuple(jnp.zeros((HD, QB), F32) for _ in range(GROUP))

    @pl.when(chip_ref[0] != 0)
    def _():
        totals = zeros
        for chunk in range(chunks + 1):
            keep = None
            if chunk == 0:
                keep = key_row > query_col
            if chunk == chunks:
                keep = key_row <= query_col
            totals = one_chunk(chunk, keep, totals)
        finish(totals)

    @pl.when(chip_ref[0] == 0)
    def _():
        def step(chunk, totals):
            return one_chunk(chunk, (key_row <= query_col) | (chunk < chunks), totals)

        finish(lax.fori_loop(chunks - block, chunks + 1, step, zeros))


def backward_attention(chip, query, grad, mixed, lse, keys, keys_t, values):
    rows = query.shape[0]
    width = GROUP * HD
    wide = pl.BlockSpec((QB, width), lambda b, s: (b, 0))
    whole = pl.BlockSpec((2 * rows, HD), lambda b, s: (0, 0))
    return pl.pallas_call(
        backward_attention_kernel,
        grid_spec=pltpu.PrefetchScalarGridSpec(
            num_scalar_prefetch=1,
            grid=(rows // QB,),
            in_specs=[
                wide,
                wide,
                wide,
                pl.BlockSpec((8, QB), lambda b, s: (0, b)),
                whole,
                pl.BlockSpec((HD, 2 * rows), lambda b, s: (0, 0)),
                whole,
            ],
            out_specs=[wide, whole, whole],
        ),
        out_shape=(
            jax.ShapeDtypeStruct((rows, width), BF),
            jax.ShapeDtypeStruct((2 * rows, HD), F32),
            jax.ShapeDtypeStruct((2 * rows, HD), F32),
        ),
        compiler_params=pltpu.CompilerParams(vmem_limit_bytes=40 << 20),
        cost_estimate=pl.CostEstimate(
            flops=18_000_000_000, transcendentals=4_000_000, bytes_accessed=8_000_000
        ),
        name="attention_backward",
    )(chip, query, grad, mixed, lse, keys, keys_t, values)


def assemble_kernel(count, place_ref, *refs):
    pieces, whole = refs[:count], refs[count]
    depth = pieces[0].shape[0]
    for i in range(count):
        whole[pl.ds(pl.multiple_of(place_ref[i] * depth, depth), depth), :] = pieces[i][...]


def assemble(places, pieces):
    count = len(pieces)
    depth, width = pieces[0].shape
    piece = pl.BlockSpec((depth, width), lambda i, s: (0, 0), pipeline_mode=pl.Buffered(1))
    return pl.pallas_call(
        functools.partial(assemble_kernel, count),
        grid_spec=pltpu.PrefetchScalarGridSpec(
            num_scalar_prefetch=1,
            grid=(1,),
            in_specs=[piece] * count,
            out_specs=pl.BlockSpec((count * depth, width), lambda i, s: (0, 0)),
        ),
        out_shape=jax.ShapeDtypeStruct((count * depth, width), pieces[0].dtype),
        compiler_params=pltpu.CompilerParams(vmem_limit_bytes=24 << 20),
        cost_estimate=pl.CostEstimate(
            flops=0, transcendentals=0, bytes_accessed=4 * count * depth * width
        ),
        name="assemble_pieces",
    )(places, *pieces)


def split_kernel(count, place_ref, whole, *pieces):
    depth = pieces[0].shape[0]
    for i in range(count):
        pieces[i][...] = whole[pl.ds(pl.multiple_of(place_ref[i] * depth, depth), depth), :]


def split(places, whole, count):
    depth, width = whole.shape[0] // count, whole.shape[1]
    piece = pl.BlockSpec((depth, width), lambda i, s: (0, 0), pipeline_mode=pl.Buffered(1))
    return pl.pallas_call(
        functools.partial(split_kernel, count),
        grid_spec=pltpu.PrefetchScalarGridSpec(
            num_scalar_prefetch=1,
            grid=(1,),
            in_specs=[pl.BlockSpec(whole.shape, lambda i, s: (0, 0))],
            out_specs=[piece] * count,
        ),
        out_shape=(jax.ShapeDtypeStruct((depth, width), whole.dtype),) * count,
        compiler_params=pltpu.CompilerParams(vmem_limit_bytes=24 << 20),
        cost_estimate=pl.CostEstimate(
            flops=0, transcendentals=0, bytes_accessed=4 * count * depth * width
        ),
        name="split_pieces",
    )(places, whole)


class Shards:
    def __init__(self, count):
        self.count = count
        self.half = count // 2
        index = lax.axis_index("shard").astype(jnp.int32)
        hi, lo = index // 2, index % 2
        mine = [(hi ^ k) * 2 + lo for k in range(self.half)]
        partner = [(hi ^ k) * 2 + (1 - lo) for k in range(self.half)]
        self.places = jnp.stack(mine + partner)

    def far(self, value, k):
        return lax.ppermute(
            value, "shard", [(i, ((i // 2) ^ k) * 2 + i % 2) for i in range(self.count)]
        )

    def near(self, value):
        return lax.ppermute(value, "shard", [(i, i ^ 1) for i in range(self.count)])

    def gather_far(self, piece):
        return [piece] + [self.far(piece, k) for k in range(1, self.half)]

    def gather_near(self, pieces):
        return pieces + [self.near(piece) for piece in pieces]

    def whole(self, pieces):
        return assemble(self.places, pieces)

    def scatter(self, value):
        pieces = split(self.places, value, self.count)
        kept, sent = pieces[: self.half], pieces[self.half :]
        sums = [
            (a.astype(F32) + self.near(b).astype(F32)).astype(BF) for a, b in zip(kept, sent)
        ]
        total = sums[0].astype(F32)
        for k in range(1, self.half):
            total = total + self.far(sums[k], k).astype(F32)
        return total


def tp_swap(value, mask):
    return lax.ppermute(value, "tp", [(i, i ^ mask) for i in range(4)])


def gelu_parts(gate):
    inner = 0.7978845608028654 * (gate + 0.044715 * gate * gate * gate)
    t = jnp.tanh(inner)
    value = 0.5 * gate * (1.0 + t)
    slope = 0.5 * (1.0 + t) + 0.5 * gate * (1.0 - t * t) * 0.7978845608028654 * (
        1.0 + 3.0 * 0.044715 * gate * gate
    )
    return value, slope


def local(count, tokens, w_query, w_keyval, w_out, w_gate, w_up, w_down, gain_attn, gain_mlp, cotangent):
    rows, width = tokens.shape[0], tokens.shape[2]
    tp = lax.axis_index("tp").astype(jnp.int32)
    core, chip = tp % 2, tp // 2
    first_core = core == 0
    chip_table = jnp.reshape(chip, (1,))
    shards = Shards(count)

    def in_order(own, other):
        return jnp.where(
            first_core, jnp.concatenate([own, other], 0), jnp.concatenate([other, own], 0)
        )

    gain_one = gain_attn.astype(BF).astype(F32)[:, None]
    gain_two = gain_mlp.astype(BF).astype(F32)[:, None]
    own_query = w_query.astype(BF).astype(F32)
    own_keyval = w_keyval.astype(BF).astype(F32)
    own_gate = w_gate.astype(BF).astype(F32)
    own_up = w_up.astype(BF).astype(F32)
    keyval_half = jnp.where(first_core, own_keyval[:, :HD], own_keyval[:, HD:])
    send_in = (jnp.concatenate([own_query, keyval_half], 1) * gain_one).astype(BF)
    send_out = jnp.transpose(w_out).astype(BF)
    send_gate = (own_gate * gain_two).astype(BF)
    send_up = (own_up * gain_two).astype(BF)
    send_down = jnp.transpose(w_down).astype(BF)

    far_in = shards.gather_far(send_in)
    far_out = shards.gather_far(after(send_out, *far_in[1:]))
    far_gate = shards.gather_far(after(send_gate, *far_out[1:]))
    far_up = shards.gather_far(after(send_up, *far_gate[1:]))
    far_down = shards.gather_far(after(send_down, *far_up[1:]))

    inputs = tokens.reshape(rows, width).astype(F32)
    scale_one = lax.rsqrt(jnp.mean(inputs * inputs, axis=-1, keepdims=True) + EPS)
    unit_own = (inputs * scale_one).astype(BF)
    unit = in_order(unit_own, tp_swap(unit_own, 1))
    cot = cotangent.reshape(4, rows, width)
    cots = [lax.dynamic_index_in_dim(cot, tp ^ k, 0, keepdims=False) for k in range(4)]
    cot_near = jnp.concatenate(cots[:2], 0)
    cot_far = jnp.concatenate(cots[2:], 0)

    in_full = shards.whole(shards.gather_near(far_in))
    in_query = in_full[:, : GROUP * HD]
    in_key = in_full[:, GROUP * HD :]
    in_query_b = tp_swap(in_query, 2)
    out_full = shards.whole(shards.gather_near(far_out))
    out_full_b = tp_swap(after(out_full, in_query_b), 2)

    half = dot(unit, in_key).astype(BF)
    half_other = tp_swap(half, 1)
    before = lax.ppermute(half, "tp", [(0, 2), (1, 3)])
    before_other = tp_swap(before, 1)
    own_pair = jnp.concatenate([before, half], 0)
    other_pair = jnp.concatenate([before_other, half_other], 0)
    keys = jnp.where(first_core, own_pair, other_pair)
    values = jnp.where(first_core, other_pair, own_pair)
    keys_t = jnp.transpose(keys)
    values_t = jnp.transpose(values)

    scale = HD ** (-0.5)
    query_a = (dot(unit, in_query) * (scale * LOG2E)).astype(BF)
    mixed_a, lse_a = forward_attention(chip_table, query_a, keys, values_t)
    query_b = (dot(unit, in_query_b) * (scale * LOG2E)).astype(BF)
    mixed_b, lse_b = forward_attention(chip_table, query_b, keys, values_t)

    branch = dot(mixed_a, out_full, NT) + dot(mixed_b, out_full_b, NT)
    branch_own = lax.dynamic_slice_in_dim(branch, core * rows, rows, 0)
    branch_other = lax.dynamic_slice_in_dim(branch, (1 - core) * rows, rows, 0).astype(BF)
    hidden = inputs + (branch_own + tp_swap(branch_other, 1).astype(F32))
    scale_two = lax.rsqrt(jnp.mean(hidden * hidden, axis=-1, keepdims=True) + EPS)
    norm_own = (hidden * scale_two).astype(BF)
    norm_x = tp_swap(norm_own, 2)
    norm_near = jnp.concatenate([norm_own, tp_swap(norm_own, 1)], 0)
    norm_far = jnp.concatenate([norm_x, tp_swap(norm_x, 1)], 0)

    gate_full = shards.whole(shards.gather_near(far_gate))
    up_full = shards.whole(shards.gather_near(far_up))
    down_full = shards.whole(shards.gather_near(far_down))

    def feed_forward(norm, cot_part):
        gate = dot(norm, gate_full)
        up = dot(norm, up_full)
        value, slope = gelu_parts(gate)
        product = (value * up).astype(BF)
        grad_product = dot(cot_part, down_full)
        grad_gate = (grad_product * up * slope).astype(BF)
        grad_up = (grad_product * value).astype(BF)
        return product, grad_gate, grad_up

    product_near, dgate_near, dup_near = feed_forward(norm_near, cot_near)
    product_far, dgate_far, dup_far = feed_forward(norm_far, cot_far)

    def reduce_rows(near, far):
        out_far = far[:rows] + tp_swap(far[rows:].astype(BF), 1).astype(F32)
        mine = near[:rows] + tp_swap(near[rows:].astype(BF), 1).astype(F32)
        return mine + tp_swap(out_far.astype(BF), 2).astype(F32)

    back_far = dot(dgate_far, gate_full, NT) + dot(dup_far, up_full, NT)
    back_near = dot(dgate_near, gate_full, NT) + dot(dup_near, up_full, NT)
    grad_norm = reduce_rows(back_near, back_far)

    down_far = dot(product_far, down_full, NT)
    down_near = dot(product_near, down_full, NT)
    output = (hidden + reduce_rows(down_near, down_far)).astype(BF)

    norm_all = jnp.concatenate([norm_near, norm_far], 0)
    g_down = dot(
        jnp.concatenate([cot_near, cot_far], 0), jnp.concatenate([product_near, product_far], 0), TN
    ).astype(BF)
    g_gate = dot(norm_all, jnp.concatenate([dgate_near, dgate_far], 0), TN).astype(BF)
    g_up = dot(norm_all, jnp.concatenate([dup_near, dup_far], 0), TN).astype(BF)
    grad_w_down = jnp.transpose(shards.scatter(g_down))
    sum_gate = shards.scatter(g_gate)
    sum_up = shards.scatter(g_up)
    grad_w_gate = sum_gate * gain_two
    grad_w_up = sum_up * gain_two
    gain_two_part = jnp.sum(own_gate * sum_gate + own_up * sum_up, axis=1)

    unit_two = hidden * scale_two
    grad_hidden = cots[0].astype(F32) + scale_two * (
        grad_norm - unit_two * jnp.mean(grad_norm * unit_two, axis=-1, keepdims=True)
    )
    grad_branch_own = grad_hidden.astype(BF)
    grad_branch = in_order(grad_branch_own, tp_swap(grad_branch_own, 1))

    grad_mixed_b = dot(grad_branch, out_full_b).astype(BF)
    dq_b, dk_b, dv_b = backward_attention(
        chip_table, query_b, grad_mixed_b, mixed_b, lse_b, keys, keys_t, values
    )
    g_query_b = dot(unit, dq_b, TN).astype(BF)
    g_out_b = dot(grad_branch, mixed_b, TN).astype(BF)
    grad_mixed_a = dot(grad_branch, out_full).astype(BF)
    dq_a, dk_a, dv_a = backward_attention(
        chip_table, query_a, grad_mixed_a, mixed_a, lse_a, keys, keys_t, values
    )
    g_out = dot(grad_branch, mixed_a, TN) + tp_swap(g_out_b, 2).astype(F32)
    grad_w_out = jnp.transpose(shards.scatter(g_out.astype(BF)))

    grad_keys = (dk_a + dk_b) * LN2
    grad_values = dv_a + dv_b
    mine = jnp.where(first_core, grad_keys, grad_values)
    theirs = jnp.where(first_core, grad_values, grad_keys).astype(BF)
    mine = mine + tp_swap(theirs, 1).astype(F32)
    chip_rows = mine.shape[0] // 2
    earlier = lax.ppermute(mine[:chip_rows].astype(BF), "tp", [(2, 0), (3, 1)])
    grad_half = (mine[chip_rows:] + earlier.astype(F32)).astype(BF)

    g_query = dot(unit, dq_a, TN) + tp_swap(g_query_b, 2).astype(F32)
    g_half = dot(unit, grad_half, TN)
    g_in = jnp.concatenate([g_query, g_half], 1).astype(BF)
    sum_in = shards.scatter(g_in)

    back = dot(dq_a, in_query, NT) + dot(dq_b, in_query_b, NT) + dot(grad_half, in_key, NT)
    back_own = lax.dynamic_slice_in_dim(back, core * rows, rows, 0)
    back_other = lax.dynamic_slice_in_dim(back, (1 - core) * rows, rows, 0).astype(BF)
    grad_unit = back_own + tp_swap(back_other, 1).astype(F32)
    unit_one = inputs * scale_one
    grad_tokens = grad_hidden + scale_one * (
        grad_unit - unit_one * jnp.mean(grad_unit * unit_one, axis=-1, keepdims=True)
    )

    sum_query = sum_in[:, : GROUP * HD]
    sum_half = sum_in[:, GROUP * HD :]
    gain_query_part = jnp.sum(own_query * sum_query, axis=1)
    gain_half_part = jnp.sum(keyval_half * sum_half, axis=1)
    gains = jnp.stack([gain_query_part + gain_half_part, gain_two_part], 0)
    gains = gains + tp_swap(gains, 1)
    gains = gains + tp_swap(gains, 2)
    sum_half = sum_half + tp_swap(sum_half, 2)
    half_swapped = tp_swap(sum_half, 1)
    grad_w_keyval = (
        jnp.where(
            first_core,
            jnp.concatenate([sum_half, half_swapped], 1),
            jnp.concatenate([half_swapped, sum_half], 1),
        )
        * gain_one
    )
    return (
        output.reshape(rows, 1, width),
        grad_tokens.reshape(rows, 1, width),
        sum_query * gain_one,
        grad_w_keyval,
        grad_w_out,
        grad_w_gate,
        grad_w_up,
        grad_w_down,
        gains[0],
        gains[1],
    )


def solution(mesh):
    in_specs = (
        P("tp", "shard", None),
        P("shard", "tp"),
        P("shard", None),
        P("tp", "shard"),
        P("shard", "tp"),
        P("shard", "tp"),
        P("tp", "shard"),
        P("shard"),
        P("shard"),
        P(None, "shard", None),
    )
    out_specs = (
        P("tp", "shard", None),
        P("tp", "shard", None),
        P("shard", "tp"),
        P("shard", None),
        P("tp", "shard"),
        P("shard", "tp"),
        P("shard", "tp"),
        P("tp", "shard"),
        P("shard"),
        P("shard"),
    )
    return jax.shard_map(
        functools.partial(local, mesh.shape["shard"]),
        mesh=mesh,
        in_specs=in_specs,
        out_specs=out_specs,
        check_vma=False,
    )
```

time: 1550 us -> 857 us (0.55)
  waiting for transfers between devices: 950 us -> 369 us
  starting transfers between devices: 1.51 us -> 152 us
  matrix products: 292 us -> 183 us
  blocking collectives: 88.1 us -> 0 us
  other arithmetic: 105 us -> 42.6 us
  Pallas kernels: 0 us -> 60.8 us
  loops' own time: 32 us -> 0 us
  local copies, waits for them, and re-layouts: 61.7 us -> 42.1 us
    reduce_scatter x10 -> x0, waiting for transfers between devices: 657 us -> none  [the longest x1 97.2 us: local(): lax.psum_scatter(jnp.dot(mixed, out_full, preferred_element_type=jnp.floa...]
    ppermute x0 -> x96, waiting for transfers between devices: none -> 369 us  [the longest x30 158 us: far(): lax.ppermute(value, 'shard', [(i, (i // 2 ^ k) * 2 + i % 2) for i in rang...]
    all_gather x8 -> x0, waiting for transfers between devices: 293 us -> none  [the longest x1 59.1 us: local(): lax.all_gather(w_up.astype(jnp.bfloat16), 'shard', axis=0, tiled=True)]
    ppermute x0 -> x96, starting transfers between devices: none -> 152 us  [the longest x30 91.8 us: far(): lax.ppermute(value, 'shard', [(i, (i // 2 ^ k) * 2 + i % 2) for i in rang...]
    dot_general x46 -> x30, matrix products: 292 us -> 183 us  [dot(): return lax.dot_general(a, b, dims, preferred_element_type=F32)]
    pallas_call x0 -> x14, Pallas kernels: none -> 60.8 us  [the longest x2 29.3 us: forward_attention(): pl.pallas_call(forward_attention_kernel, grid_spec=pltpu.PrefetchScalarGr...]
    unnamed x2 -> x0, blocking collectives: 45.1 us -> none
    another operation x4 -> x1, other arithmetic: 44.1 us -> 0.01 us  [local(): gains = jnp.stack([gain_query_part + gain_half_part, gain_two_part], 0)]
  transfers between devices with their start and end apart: 19 -> 96, of which waited for: 16 -> 42; matrix products, arithmetic and copies ran while one was open for 13% -> 25% of each run, Pallas kernels for 0% -> 5%
where the time goes in v1:
time: 857 us; the launch traced here: 853 us
  waiting for transfers between devices  369 us (43%)
  matrix products  183 us (21%)
  starting transfers between devices  152 us (18%)
  Pallas kernels  60.8 us (7%)
  other arithmetic  42.6 us (5%)
  local copies, waits for them, and re-layouts  42.1 us (5%)
    dot_general x30, matrix products, dot(): return lax.dot_general(a, b, dims, preferred_element_type=F32)  183 us
    ppermute x30, waiting for transfers between devices, far(): lax.ppermute(value, 'shard', [(i, (i // 2 ^ k) * 2 + i % 2) for i in rang...  158 us
    ppermute x40, waiting for transfers between devices, near(): return lax.ppermute(value, 'shard', [(i, i ^ 1) for i in range(self.count)])  110 us
    ppermute x30, starting transfers between devices, far(): lax.ppermute(value, 'shard', [(i, (i // 2 ^ k) * 2 + i % 2) for i in rang...  91.8 us
    ppermute x24, waiting for transfers between devices, tp_swap(): return lax.ppermute(value, 'tp', [(i, i ^ mask) for i in range(4)])  54.8 us
    ppermute x1, waiting for transfers between devices, local(): earlier = lax.ppermute(mine[:chip_rows].astype(BF), 'tp', [(2, 0), (3, 1)])  45.9 us
    ppermute x40, starting transfers between devices, near(): return lax.ppermute(value, 'shard', [(i, i ^ 1) for i in range(self.count)])  39 us
    unnamed x223, local copies, waits for them, and re-layouts  29.5 us
  transfers between devices with their start and end apart: 96, of which 42 were waited for; matrix products, arithmetic and copies ran while one was open for 25% of the time, Pallas kernels for 5%

profile of v1, /device:TPU:0, one launch (start us, length us, event | category | flops | bytes accessed | tf_op | source)
XLA Modules:
  0.0 852.7 jit_solution(7821369960756516048)
XLA Ops:
  19.5 9.8 %collective-permute-done.2.refs_2_ = bf16[192,512]{1,0:T(8,128)(2,1)S(1)} collective-permute-done((bf16[192,512]{1,0:T(8,128)(2,1)S(1)}, bf16[192,512]{1,0:T(8,128)(2,1)S(1)}, u32[]{:S(2)}, u32[]{:S(2)}) %collective-permute-start.2) | collective-permute-done | bytes 196640 | tf_op jit(solution)/shard_map/ppermute | solution.py:290
  91.7 14.5 %attention_forward.2 = (bf16[1024,384]{1,0:T(8,128)(2,1)S(1)}, f32[8,1024]{1,0:T(8,128)S(1)}) custom-call(s32[1]{0:T(128)} %bitcast.1.chip_ref, bf16[1024,384]{1,0:T(8,128)(2,1)S(1)} %copy-done.54, bf16[2048,128]{1,0:T(8,128)(2,1)S(1)} %get-tuple-element.149.k_ref, bf16[128,2048]{1,0:T(8,128)(2,1)S(1)} %copy.20.vt_ref), custom_call_target="tpu_custom_call" | custom-call | flops 8999999488 | bytes 4000000 | tf_op jit(solution)/shard_map/attention_forward/pallas_call | solution.py:92
  106.2 14.8 %attention_forward.3 = (bf16[1024,384]{1,0:T(8,128)(2,1)S(1)}, f32[8,1024]{1,0:T(8,128)S(1)}) custom-call(s32[1]{0:T(128)} %bitcast.1.chip_ref, bf16[1024,384]{1,0:T(8,128)(2,1)S(1)} %copy-done.52, bf16[2048,128]{1,0:T(8,128)(2,1)S(1)} %get-tuple-element.149.k_ref, bf16[128,2048]{1,0:T(8,128)(2,1)S(1)} %copy.20.vt_ref), custom_call_target="tpu_custom_call" | custom-call | flops 8999999488 | bytes 4000000 | tf_op jit(solution)/shard_map/attention_forward/pallas_call | solution.py:92
  138.0 10.1 %collective-permute-done.24.refs_3_ = bf16[192,1152]{1,0:T(8,128)(2,1)S(1)} collective-permute-done((bf16[192,1152]{1,0:T(8,128)(2,1)S(1)}, bf16[192,1152]{1,0:T(8,128)(2,1)S(1)}, u32[]{:S(2)}, u32[]{:S(2)}) %collective-permute-start.24) | collective-permute-done | bytes 442400 | tf_op jit(solution)/shard_map/ppermute | solution.py:290
  148.1 25.9 %collective-permute-done.23.refs_2_ = bf16[192,1152]{1,0:T(8,128)(2,1)S(1)} collective-permute-done((bf16[192,1152]{1,0:T(8,128)(2,1)S(1)}, bf16[192,1152]{1,0:T(8,128)(2,1)S(1)}, u32[]{:S(2)}, u32[]{:S(2)}) %collective-permute-start.23) | collective-permute-done | bytes 442400 | tf_op jit(solution)/shard_map/ppermute | solution.py:290
  189.5 22.5 %collective-permute-done.30.refs_2_ = bf16[192,1152]{1,0:T(8,128)(2,1)S(1)} collective-permute-done((bf16[192,1152]{1,0:T(8,128)(2,1)S(1)}, bf16[192,1152]{1,0:T(8,128)(2,1)S(1)}, u32[]{:S(2)}, u32[]{:S(2)}) %collective-permute-start.30) | collective-permute-done | bytes 442400 | tf_op jit(solution)/shard_map/ppermute | solution.py:290
  282.1 9.4 %collective-permute-done.42.refs_7_ = bf16[192,1152]{1,0:T(8,128)(2,1)} collective-permute-done((bf16[192,1152]{1,0:T(8,128)(2,1)}, bf16[192,1152]{1,0:T(8,128)(2,1)}, u32[]{:S(2)}, u32[]{:S(2)}) %collective-permute-start.42) | collective-permute-done | bytes 442400 | tf_op jit(solution)/shard_map/ppermute | solution.py:295
  291.5 9.5 %collective-permute-done.41.refs_6_ = bf16[192,1152]{1,0:T(8,128)(2,1)} collective-permute-done((bf16[192,1152]{1,0:T(8,128)(2,1)}, bf16[192,1152]{1,0:T(8,128)(2,1)}, u32[]{:S(2)}, u32[]{:S(2)}) %collective-permute-start.41) | collective-permute-done | bytes 442400 | tf_op jit(solution)/shard_map/ppermute | solution.py:295
  332.0 10.7 %fusion.15 = (bf16[1024,1152]{1,0:T(8,128)(2,1)}, bf16[1024,1152]{1,0:T(8,128)(2,1)}, bf16[1024,1152]{1,0:T(8,128)(2,1)S(1)}) fusion(f32[1024,1152]{1,0:T(8,128)} %fusion.56, f32[1024,1152]{1,0:T(8,128)S(1)} %fusion.55, bf16[1536,1152]{1,0:T(8,128)(2,1)S(1)} %assemble_pieces.9, bf16[512,1536]{1,0:T(8,128)(2,1)S(1)} %get-tuple-element.143, ...), kind=kOutput, calls=%fused_computation.27 | convolution fusion | flops 3659661312 | bytes 23199744 | tf_op jit(solution)/shard_map/dot_general | solution.py:26
  372.5 11.7 %fusion.20 = (bf16[1024,1152]{1,0:T(8,128)(2,1)}, bf16[1024,1152]{1,0:T(8,128)(2,1)}, bf16[1024,1152]{1,0:T(8,128)(2,1)}) fusion(f32[1024,1152]{1,0:T(8,128)} %fusion.49, f32[1024,1152]{1,0:T(8,128)} %fusion.87, bf16[1024,1536]{1,0:T(8,128)(2,1)S(1)} %constant_dynamic-update-slice_fusion.2, bf16[1536,1152]{1,0:T(8,128)(2,1)S(1)} %assemble_pieces.7), kind=kOutput, calls=%fused_computation.32 | convolution fusion | flops 3653369856 | bytes 23199744 | tf_op jit(solution)/shard_map/dot_general | solution.py:26
  384.2 11.8 %convolution_convert_fusion.whole = bf16[1536,1152]{1,0:T(8,128)(2,1)S(1)} fusion(bf16[512,1536]{1,0:T(8,128)(2,1)S(1)} %copy-done.75, bf16[512,1536]{1,0:T(8,128)(2,1)} %copy-done.76, bf16[512,1536]{1,0:T(8,128)(2,1)} %copy-done.77, bf16[512,1536]{1,0:T(8,128)(2,1)S(1)} %get-tuple-element.140, bf16[1024,1152]{1,0:T(8,128)(2,1)} %get-tuple-element.139, ...), kind=kOutput, calls=%fused_computation | convolution fusion | flops 7284129792 | bytes 14548992 | tf_op jit(solution)/shard_map/dot_general | solution.py:26
  406.9 11.7 %convolution_convert_fusion.1.whole = bf16[1536,1152]{1,0:T(8,128)(2,1)S(1)} fusion(bf16[1024,1152]{1,0:T(8,128)(2,1)} %get-tuple-element.138, bf16[1024,1152]{1,0:T(8,128)(2,1)} %get-tuple-element.135, bf16[512,1536]{1,0:T(8,128)(2,1)S(1)} %copy-done.73, bf16[512,1536]{1,0:T(8,128)(2,1)S(1)} %copy-done.71, bf16[512,1536]{1,0:T(8,128)(2,1)} %collective-permute-done.21, ...), kind=kOutput, calls=%fused_computation.1 | convolution fusion | flops 7284129792 | bytes 14548992 | tf_op jit(solution)/shard_map/dot_general | solution.py:26
  422.5 12.0 %convolution_convert_fusion.2.whole = bf16[1536,1152]{1,0:T(8,128)(2,1)S(1)} fusion(bf16[1024,1152]{1,0:T(8,128)(2,1)} %get-tuple-element.137, bf16[1024,1152]{1,0:T(8,128)(2,1)} %get-tuple-element.134, bf16[512,1536]{1,0:T(8,128)(2,1)} %copy-done.72, bf16[512,1536]{1,0:T(8,128)(2,1)S(1)} %copy-done.71, bf16[512,1536]{1,0:T(8,128)(2,1)} %collective-permute-done.21, ...), kind=kOutput, calls=%fused_computation.2 | convolution fusion | flops 7284129792 | bytes 14548992 | tf_op jit(solution)/shard_map/dot_general | solution.py:26
  491.3 19.9 %collective-permute-done.50 = bf16[512,1536]{1,0:T(8,128)(2,1)S(1)} collective-permute-done((bf16[512,1536]{1,0:T(8,128)(2,1)S(1)}, bf16[512,1536]{1,0:T(8,128)(2,1)S(1)}, u32[]{:S(2)}, u32[]{:S(2)}) %collective-permute-start.50) | collective-permute-done | bytes 1572896 | tf_op jit(solution)/shard_map/ppermute | solution.py:319
  515.6 26.2 %collective-permute-done.47 = bf16[512,1536]{1,0:T(8,128)(2,1)S(1)} collective-permute-done((bf16[512,1536]{1,0:T(8,128)(2,1)S(1)}, bf16[512,1536]{1,0:T(8,128)(2,1)S(1)}, u32[]{:S(2)}, u32[]{:S(2)}) %collective-permute-start.47) | collective-permute-done | bytes 1572896 | tf_op jit(solution)/shard_map/ppermute | solution.py:319
  556.8 25.7 %collective-permute-done.77 = bf16[192,1152]{1,0:T(8,128)(2,1)S(1)} collective-permute-done((bf16[192,1152]{1,0:T(8,128)(2,1)S(1)}, bf16[192,1152]{1,0:T(8,128)(2,1)S(1)}, u32[]{:S(2)}, u32[]{:S(2)}) %collective-permute-start.77) | collective-permute-done | bytes 442400 | tf_op jit(solution)/shard_map/ppermute | solution.py:290
  586.2 23.6 %collective-permute-start.89 = (bf16[192,1152]{1,0:T(8,128)(2,1)}, bf16[192,1152]{1,0:T(8,128)(2,1)}, u32[]{:S(2)}, u32[]{:S(2)}) collective-permute-start(bf16[192,1152]{1,0:T(8,128)(2,1)} %add_convert_fusion.2), channel_id=1, source_target_pairs={{0,8},{4,12},{8,0},{12,4},{16,24},{20,28},{24,16},{28,20},{1,9},{5... | collective-permute-start | bytes 1327112 | tf_op jit(solution)/shard_map/ppermute | solution.py:290
  619.2 15.5 %collective-permute-start.93 = (bf16[192,1152]{1,0:T(8,128)(2,1)}, bf16[192,1152]{1,0:T(8,128)(2,1)}, u32[]{:S(2)}, u32[]{:S(2)}) collective-permute-start(bf16[192,1152]{1,0:T(8,128)(2,1)} %add_convert_fusion), channel_id=1, source_target_pairs={{0,24},{4,28},{8,16},{12,20},{16,8},{20,12},{24,0},{28,4},{1,25},{... | collective-permute-start | bytes 1327112 | tf_op jit(solution)/shard_map/ppermute | solution.py:290
  639.4 16.9 %collective-permute-done.91 = bf16[192,1152]{1,0:T(8,128)(2,1)} collective-permute-done((bf16[192,1152]{1,0:T(8,128)(2,1)}, bf16[192,1152]{1,0:T(8,128)(2,1)}, u32[]{:S(2)}, u32[]{:S(2)}) %collective-permute-start.91) | collective-permute-done | bytes 442400 | tf_op jit(solution)/shard_map/ppermute | solution.py:290
  664.0 10.5 %attention_backward.3 = (bf16[1024,384]{1,0:T(8,128)(2,1)S(1)}, f32[2048,128]{1,0:T(8,128)S(1)}, f32[2048,128]{1,0:T(8,128)S(1)}) custom-call(s32[1]{0:T(128)} %bitcast.1.chip_ref, bf16[1024,384]{1,0:T(8,128)(2,1)S(1)} %copy-done.53, bf16[1024,384]{1,0:T(8,128)(2,1)S(1)} %convolution_convert_fusion.6.g_ref, bf16[1024,384]{1,0:T(8,128)(2,1)S(1)} %copy-done.5, ...), custom_call_target="tpu_custom_call" | custom-call | flops 17999998976 | bytes 8000000 | tf_op jit(solution)/shard_map/attention_backward/pallas_call | solution.py:196
  679.3 10.8 %attention_backward.2 = (bf16[1024,384]{1,0:T(8,128)(2,1)S(1)}, f32[2048,128]{1,0:T(8,128)S(1)}, f32[2048,128]{1,0:T(8,128)S(1)}) custom-call(s32[1]{0:T(128)} %bitcast.1.chip_ref, bf16[1024,384]{1,0:T(8,128)(2,1)S(1)} %copy-done.55, bf16[1024,384]{1,0:T(8,128)(2,1)S(1)} %convolution_convert_fusion.7.g_ref, bf16[1024,384]{1,0:T(8,128)(2,1)S(1)} %copy-done.7, ...), custom_call_target="tpu_custom_call" | custom-call | flops 17999998976 | bytes 8000000 | tf_op jit(solution)/shard_map/attention_backward/pallas_call | solution.py:196
  695.2 11.6 %collective-permute-start.55 = (bf16[1536,384]{1,0:T(8,128)(2,1)S(1)}, bf16[1536,384]{1,0:T(8,128)(2,1)S(1)}, u32[]{:S(2)}, u32[]{:S(2)}) collective-permute-start(bf16[1536,384]{1,0:T(8,128)(2,1)S(1)} %convolution_convert_fusion.4), channel_id=1, source_target_pairs={{0,2},{1,3},{2,0},{3,1},{4,6},{5,7},{6,4},{7,5},{8,10},{9,11},{10,... | collective-permute-start | bytes 3538952 | tf_op jit(solution)/shard_map/ppermute | solution.py:319
  718.4 45.9 %collective-permute-done.53 = bf16[1024,128]{1,0:T(8,128)(2,1)S(1)} collective-permute-done((bf16[1024,128]{1,0:T(8,128)(2,1)S(1)}, bf16[1024,128]{1,0:T(8,128)(2,1)S(1)}, u32[]{:S(2)}, u32[]{:S(2)}) %collective-permute-start.53) | collective-permute-done | bytes 262176 | tf_op jit(solution)/shard_map/ppermute | solution.py:476
  814.0 9.8 %collective-permute-done.60 = bf16[192,512]{1,0:T(8,128)(2,1)S(1)} collective-permute-done((bf16[192,512]{1,0:T(8,128)(2,1)S(1)}, bf16[192,512]{1,0:T(8,128)(2,1)S(1)}, u32[]{:S(2)}, u32[]{:S(2)}) %collective-permute-start.60) | collective-permute-done | bytes 196640 | tf_op jit(solution)/shard_map/ppermute | solution.py:290
  (506 shorter events, 459.0 us)
Async XLA Ops:
  6.0 64.6 %collective-permute-start = (bf16[512,1536]{1,0:T(8,128)(2,1)}, bf16[512,1536]{1,0:T(8,128)(2,1)}, u32[]{:S(2)}, u32[]{:S(2)}) collective-permute-start(bf16[512,1536]{1,0:T(8,128)(2,1)} %fusion.32), channel_id=1, source_target_pairs={{0,1},{1,0},{2,3},{3,2},{4,5},{5,4},{6,7},{7,6},{8,9},{9,8},{10,11... | collective-permute-start | bytes 4718600 | tf_op jit(solution)/shard_map/ppermute | solution.py:319
  77.6 43.4 %collective-permute-start.19 = (bf16[1536,384]{1,0:T(8,128)(2,1)S(1)}, bf16[1536,384]{1,0:T(8,128)(2,1)}, u32[]{:S(2)}, u32[]{:S(2)}) collective-permute-start(bf16[1536,384]{1,0:T(8,128)(2,1)S(1)} %assemble_pieces.6), channel_id=1, source_target_pairs={{0,2},{1,3},{2,0},{3,1},{4,6},{5,7},{6,4},{7,5},{8,10},{9,11},{10,... | collective-permute-start | bytes 3538952 | tf_op jit(solution)/shard_map/ppermute | solution.py:319
  132.3 83.0 %collective-permute-start.20 = (bf16[512,1536]{1,0:T(8,128)(2,1)}, bf16[512,1536]{1,0:T(8,128)(2,1)}, u32[]{:S(2)}, u32[]{:S(2)}) collective-permute-start(bf16[512,1536]{1,0:T(8,128)(2,1)} %dynamic-slice_convert_fusion.1), channel_id=1, source_target_pairs={{0,1},{1,0},{2,3},{3,2},{4,5},{5,4},{6,7},{7,6},{8,9},{9,8},{10,11... | collective-permute-start | bytes 4718600 | tf_op jit(solution)/shard_map/ppermute | solution.py:319
  135.0 39.0 %collective-permute-start.23 = (bf16[192,1152]{1,0:T(8,128)(2,1)S(1)}, bf16[192,1152]{1,0:T(8,128)(2,1)S(1)}, u32[]{:S(2)}, u32[]{:S(2)}) collective-permute-start(bf16[192,1152]{1,0:T(8,128)(2,1)S(1)} %get-tuple-element.69.refs_0_), channel_id=1, source_target_pairs={{0,16},{4,20},{8,24},{12,28},{16,0},{20,4},{24,8},{28,12},{1,17},{... | collective-permute-start | bytes 1327112 | tf_op jit(solution)/shard_map/ppermute | solution.py:290
  135.5 38.5 %collective-permute-start.22 = (bf16[192,1152]{1,0:T(8,128)(2,1)S(1)}, bf16[192,1152]{1,0:T(8,128)(2,1)S(1)}, u32[]{:S(2)}, u32[]{:S(2)}) collective-permute-start(bf16[192,1152]{1,0:T(8,128)(2,1)S(1)} %get-tuple-element.69.refs_0_), channel_id=1, source_target_pairs={{0,8},{4,12},{8,0},{12,4},{16,24},{20,28},{24,16},{28,20},{1,9},{5... | collective-permute-start | bytes 1327112 | tf_op jit(solution)/shard_map/ppermute | solution.py:290
  137.5 76.5 %collective-permute-start.25 = (bf16[192,1152]{1,0:T(8,128)(2,1)S(1)}, bf16[192,1152]{1,0:T(8,128)(2,1)S(1)}, u32[]{:S(2)}, u32[]{:S(2)}) collective-permute-start(bf16[192,1152]{1,0:T(8,128)(2,1)S(1)} %get-tuple-element.69.refs_0_), channel_id=1, source_target_pairs={{0,4},{4,0},{8,12},{12,8},{16,20},{20,16},{24,28},{28,24},{1,5},{5... | collective-permute-start | bytes 1327112 | tf_op jit(solution)/shard_map/ppermute | solution.py:295
  189.0 46.4 %collective-permute-start.32 = (bf16[192,1152]{1,0:T(8,128)(2,1)S(1)}, bf16[192,1152]{1,0:T(8,128)(2,1)S(1)}, u32[]{:S(2)}, u32[]{:S(2)}) collective-permute-start(bf16[192,1152]{1,0:T(8,128)(2,1)S(1)} %get-tuple-element.70.refs_0_), channel_id=1, source_target_pairs={{0,4},{4,0},{8,12},{12,8},{16,20},{20,16},{24,28},{28,24},{1,5},{5... | collective-permute-start | bytes 1327112 | tf_op jit(solution)/shard_map/ppermute | solution.py:295
  263.8 54.0 %collective-permute-start.21 = (bf16[512,1536]{1,0:T(8,128)(2,1)}, bf16[512,1536]{1,0:T(8,128)(2,1)}, u32[]{:S(2)}, u32[]{:S(2)}) collective-permute-start(bf16[512,1536]{1,0:T(8,128)(2,1)} %multiply_convert_fusion.4), channel_id=1, source_target_pairs={{0,1},{1,0},{2,3},{3,2},{4,5},{5,4},{6,7},{7,6},{8,9},{9,8},{10,11... | collective-permute-start | bytes 4718600 | tf_op jit(solution)/shard_map/ppermute | solution.py:319
  348.4 166.1 %collective-permute-start.43 = (bf16[512,1536]{1,0:T(8,128)(2,1)}, bf16[512,1536]{1,0:T(8,128)(2,1)}, u32[]{:S(2)}, u32[]{:S(2)}) collective-permute-start(bf16[512,1536]{1,0:T(8,128)(2,1)} %slice.146), channel_id=1, source_target_pairs={{0,1},{1,0},{2,3},{3,2},{4,5},{5,4},{6,7},{7,6},{8,9},{9,8},{10,11... | collective-permute-start | bytes 4718600 | tf_op jit(solution)/shard_map/ppermute | solution.py:319
  365.9 124.0 %collective-permute-start.48 = (bf16[512,1536]{1,0:T(8,128)(2,1)}, bf16[512,1536]{1,0:T(8,128)(2,1)}, u32[]{:S(2)}, u32[]{:S(2)}) collective-permute-start(bf16[512,1536]{1,0:T(8,128)(2,1)} %slice.144), channel_id=1, source_target_pairs={{0,1},{1,0},{2,3},{3,2},{4,5},{5,4},{6,7},{7,6},{8,9},{9,8},{10,11... | collective-permute-start | bytes 4718600 | tf_op jit(solution)/shard_map/ppermute | solution.py:319
  398.5 49.3 %collective-permute-start.88 = (bf16[192,1152]{1,0:T(8,128)(2,1)}, bf16[192,1152]{1,0:T(8,128)(2,1)}, u32[]{:S(2)}, u32[]{:S(2)}) collective-permute-start(bf16[192,1152]{1,0:T(8,128)(2,1)} %get-tuple-element.115), channel_id=1, source_target_pairs={{0,4},{4,0},{8,12},{12,8},{16,20},{20,16},{24,28},{28,24},{1,5},{5... | collective-permute-start | bytes 1327112 | tf_op jit(solution)/shard_map/ppermute | solution.py:295
  399.1 52.5 %collective-permute-start.90 = (bf16[192,1152]{1,0:T(8,128)(2,1)}, bf16[192,1152]{1,0:T(8,128)(2,1)}, u32[]{:S(2)}, u32[]{:S(2)}) collective-permute-start(bf16[192,1152]{1,0:T(8,128)(2,1)} %get-tuple-element.117), channel_id=1, source_target_pairs={{0,4},{4,0},{8,12},{12,8},{16,20},{20,16},{24,28},{28,24},{1,5},{5... | collective-permute-start | bytes 1327112 | tf_op jit(solution)/shard_map/ppermute | solution.py:295
  482.1 59.8 %collective-permute-start.47 = (bf16[512,1536]{1,0:T(8,128)(2,1)S(1)}, bf16[512,1536]{1,0:T(8,128)(2,1)S(1)}, u32[]{:S(2)}, u32[]{:S(2)}) collective-permute-start(bf16[512,1536]{1,0:T(8,128)(2,1)S(1)} %fusion.41), channel_id=1, source_target_pairs={{0,2},{1,3},{2,0},{3,1},{4,6},{5,7},{6,4},{7,5},{8,10},{9,11},{10,... | collective-permute-start | bytes 4718600 | tf_op jit(solution)/shard_map/ppermute | solution.py:319
  489.1 60.3 %collective-permute-start.92 = (bf16[192,1152]{1,0:T(8,128)(2,1)S(1)}, bf16[192,1152]{1,0:T(8,128)(2,1)S(1)}, u32[]{:S(2)}, u32[]{:S(2)}) collective-permute-start(bf16[192,1152]{1,0:T(8,128)(2,1)S(1)} %copy-done.45), channel_id=1, source_target_pairs={{0,4},{4,0},{8,12},{12,8},{16,20},{20,16},{24,28},{28,24},{1,5},{5... | collective-permute-start | bytes 1327112 | tf_op jit(solution)/shard_map/ppermute | solution.py:295
  489.9 60.6 %collective-permute-start.73 = (bf16[192,1152]{1,0:T(8,128)(2,1)S(1)}, bf16[192,1152]{1,0:T(8,128)(2,1)S(1)}, u32[]{:S(2)}, u32[]{:S(2)}) collective-permute-start(bf16[192,1152]{1,0:T(8,128)(2,1)S(1)} %get-tuple-element.97), channel_id=1, source_target_pairs={{0,4},{4,0},{8,12},{12,8},{16,20},{20,16},{24,28},{28,24},{1,5},{5... | collective-permute-start | bytes 1327112 | tf_op jit(solution)/shard_map/ppermute | solution.py:295
  511.2 41.1 %collective-permute-start.80 = (bf16[192,1152]{1,0:T(8,128)(2,1)S(1)}, bf16[192,1152]{1,0:T(8,128)(2,1)S(1)}, u32[]{:S(2)}, u32[]{:S(2)}) collective-permute-start(bf16[192,1152]{1,0:T(8,128)(2,1)S(1)} %copy-done.43), channel_id=1, source_target_pairs={{0,4},{4,0},{8,12},{12,8},{16,20},{20,16},{24,28},{28,24},{1,5},{5... | collective-permute-start | bytes 1327112 | tf_op jit(solution)/shard_map/ppermute | solution.py:295
  550.4 108.5 %collective-permute-start.51 = (bf16[512,1536]{1,0:T(8,128)(2,1)}, bf16[512,1536]{1,0:T(8,128)(2,1)}, u32[]{:S(2)}, u32[]{:S(2)}) collective-permute-start(bf16[512,1536]{1,0:T(8,128)(2,1)} %get-tuple-element.130), channel_id=1, source_target_pairs={{0,1},{1,0},{2,3},{3,2},{4,5},{5,4},{6,7},{7,6},{8,9},{9,8},{10,11... | collective-permute-start | bytes 4718600 | tf_op jit(solution)/shard_map/ppermute | solution.py:319
  553.3 65.9 %collective-permute-start.84 = (bf16[192,1152]{1,0:T(8,128)(2,1)S(1)}, bf16[192,1152]{1,0:T(8,128)(2,1)S(1)}, u32[]{:S(2)}, u32[]{:S(2)}) collective-permute-start(bf16[192,1152]{1,0:T(8,128)(2,1)S(1)} %add_convert_fusion.5), channel_id=1, source_target_pairs={{0,16},{4,20},{8,24},{12,28},{16,0},{20,4},{24,8},{28,12},{1,17},{... | collective-permute-start | bytes 1327112 | tf_op jit(solution)/shard_map/ppermute | solution.py:290
  585.5 54.0 %collective-permute-start.87 = (bf16[192,1152]{1,0:T(8,128)(2,1)S(1)}, bf16[192,1152]{1,0:T(8,128)(2,1)}, u32[]{:S(2)}, u32[]{:S(2)}) collective-permute-start(bf16[192,1152]{1,0:T(8,128)(2,1)S(1)} %copy-done.41), channel_id=1, source_target_pairs={{0,4},{4,0},{8,12},{12,8},{16,20},{20,16},{24,28},{28,24},{1,5},{5... | collective-permute-start | bytes 1327112 | tf_op jit(solution)/shard_map/ppermute | solution.py:295
  586.2 53.2 %collective-permute-start.89 = (bf16[192,1152]{1,0:T(8,128)(2,1)}, bf16[192,1152]{1,0:T(8,128)(2,1)}, u32[]{:S(2)}, u32[]{:S(2)}) collective-permute-start(bf16[192,1152]{1,0:T(8,128)(2,1)} %add_convert_fusion.2), channel_id=1, source_target_pairs={{0,8},{4,12},{8,0},{12,4},{16,24},{20,28},{24,16},{28,20},{1,9},{5... | collective-permute-start | bytes 1327112 | tf_op jit(solution)/shard_map/ppermute | solution.py:290
  695.2 80.7 %collective-permute-start.55 = (bf16[1536,384]{1,0:T(8,128)(2,1)S(1)}, bf16[1536,384]{1,0:T(8,128)(2,1)S(1)}, u32[]{:S(2)}, u32[]{:S(2)}) collective-permute-start(bf16[1536,384]{1,0:T(8,128)(2,1)S(1)} %convolution_convert_fusion.4), channel_id=1, source_target_pairs={{0,2},{1,3},{2,0},{3,1},{4,6},{5,7},{6,4},{7,5},{8,10},{9,11},{10,... | collective-permute-start | bytes 3538952 | tf_op jit(solution)/shard_map/ppermute | solution.py:319
  711.5 58.4 %collective-permute-start.65 = (bf16[1536,384]{1,0:T(8,128)(2,1)S(1)}, bf16[1536,384]{1,0:T(8,128)(2,1)S(1)}, u32[]{:S(2)}, u32[]{:S(2)}) collective-permute-start(bf16[1536,384]{1,0:T(8,128)(2,1)S(1)} %convolution_convert_fusion.3), channel_id=1, source_target_pairs={{0,2},{1,3},{2,0},{3,1},{4,6},{5,7},{6,4},{7,5},{8,10},{9,11},{10,... | collective-permute-start | bytes 3538952 | tf_op jit(solution)/shard_map/ppermute | solution.py:319
  713.8 50.5 %collective-permute-start.53 = (bf16[1024,128]{1,0:T(8,128)(2,1)S(1)}, bf16[1024,128]{1,0:T(8,128)(2,1)S(1)}, u32[]{:S(2)}, u32[]{:S(2)}) collective-permute-start(bf16[1024,128]{1,0:T(8,128)(2,1)S(1)} %slice.147), channel_id=1, source_target_pairs={{2,0},{3,1},{6,4},{7,5},{10,8},{11,9},{14,12},{15,13},{18,16},{19,... | collective-permute-start | bytes 786440 | tf_op jit(solution)/shard_map/ppermute | solution.py:476
  765.7 78.4 %collective-permute-start.54 = (bf16[512,1536]{1,0:T(8,128)(2,1)S(1)}, bf16[512,1536]{1,0:T(8,128)(2,1)S(1)}, u32[]{:S(2)}, u32[]{:S(2)}) collective-permute-start(bf16[512,1536]{1,0:T(8,128)(2,1)S(1)} %dynamic-slice_convert_fusion), channel_id=1, source_target_pairs={{0,1},{1,0},{2,3},{3,2},{4,5},{5,4},{6,7},{7,6},{8,9},{9,8},{10,11... | collective-permute-start | bytes 4718600 | tf_op jit(solution)/shard_map/ppermute | solution.py:319
  (182 other events, 3615.9 us)

commit v2 on v1

--- a/solution.py
+++ b/solution.py
@@ -250,30 +250,327 @@
     )(places, *pieces)
 
 
-def split_kernel(count, place_ref, whole, *pieces):
+def pack_kernel(*refs):
+    packed = refs[-1]
+    depth, width = refs[0].shape[0], packed.shape[1]
+    for i, piece in enumerate(refs[:-1]):
+        packed[pl.ds(i * depth, depth), :] = piece[:, :width]
+
+
+def pack(pieces, width):
     depth = pieces[0].shape[0]
-    for i in range(count):
-        pieces[i][...] = whole[pl.ds(pl.multiple_of(place_ref[i] * depth, depth), depth), :]
-
-
-def split(places, whole, count):
-    depth, width = whole.shape[0] // count, whole.shape[1]
-    piece = pl.BlockSpec((depth, width), lambda i, s: (0, 0), pipeline_mode=pl.Buffered(1))
+    rows = depth * len(pieces)
     return pl.pallas_call(
-        functools.partial(split_kernel, count),
+        pack_kernel,
+        grid=(1,),
+        in_specs=[pl.BlockSpec(piece.shape, lambda i: (0, 0)) for piece in pieces],
+        out_specs=pl.BlockSpec((rows, width), lambda i: (0, 0)),
+        out_shape=jax.ShapeDtypeStruct((rows, width), BF),
+        compiler_params=pltpu.CompilerParams(vmem_limit_bytes=16 << 20),
+        cost_estimate=pl.CostEstimate(flops=0, transcendentals=0, bytes_accessed=4 * rows * width),
+        name="pack_pieces",
+    )(*pieces)
+
+
+def unpack_kernel(half, place_ref, far, near, whole):
+    depth = far.shape[0] // half
+    for i in range(half):
+        rows = pl.ds(i * depth, depth)
+        whole[pl.ds(pl.multiple_of(place_ref[i] * depth, depth), depth), :] = far[rows, :]
+        whole[pl.ds(pl.multiple_of(place_ref[half + i] * depth, depth), depth), :] = near[rows, :]
+
+
+def unpack(places, far, near, half):
+    rows, width = far.shape
+    packed = pl.BlockSpec((rows, width), lambda i, s: (0, 0))
+    return pl.pallas_call(
+        functools.partial(unpack_kernel, half),
+        grid_spec=pltpu.PrefetchScalarGridSpec(
+            num_scalar_prefetch=1,
+            grid=(1,),
+            in_specs=[packed, packed],
+            out_specs=pl.BlockSpec((2 * rows, width), lambda i, s: (0, 0)),
+        ),
+        out_shape=jax.ShapeDtypeStruct((2 * rows, width), BF),
+        compiler_params=pltpu.CompilerParams(vmem_limit_bytes=16 << 20),
+        cost_estimate=pl.CostEstimate(flops=0, transcendentals=0, bytes_accessed=8 * rows * width),
+        name="unpack_pieces",
+    )(places, far, near)
+
+
+def split_kernel(groups, half, place_ref, whole, *refs):
+    depth = refs[0].shape[0] // len(groups[0])
+    for group, kept, sent in zip(groups, refs[: len(groups)], refs[len(groups) :]):
+        for at, i in enumerate(group):
+            rows = pl.ds(at * depth, depth)
+            kept[rows, :] = whole[pl.ds(pl.multiple_of(place_ref[i] * depth, depth), depth), :]
+            sent[rows, :] = whole[
+                pl.ds(pl.multiple_of(place_ref[half + i] * depth, depth), depth), :
+            ]
+
+
+def split(places, whole, half, parts=1):
+    size = half // parts
+    groups = [range(half - (p + 1) * size, half - p * size) for p in range(parts)]
+    rows, width = whole.shape[0] // (2 * parts), whole.shape[1]
+    out = pl.BlockSpec((rows, width), lambda i, s: (0, 0))
+    pieces = pl.pallas_call(
+        functools.partial(split_kernel, groups, half),
         grid_spec=pltpu.PrefetchScalarGridSpec(
             num_scalar_prefetch=1,
             grid=(1,),
             in_specs=[pl.BlockSpec(whole.shape, lambda i, s: (0, 0))],
-            out_specs=[piece] * count,
-        ),
-        out_shape=(jax.ShapeDtypeStruct((depth, width), whole.dtype),) * count,
+            out_specs=[out] * (2 * parts),
+        ),
+        out_shape=(jax.ShapeDtypeStruct((rows, width), whole.dtype),) * (2 * parts),
         compiler_params=pltpu.CompilerParams(vmem_limit_bytes=24 << 20),
         cost_estimate=pl.CostEstimate(
-            flops=0, transcendentals=0, bytes_accessed=4 * count * depth * width
+            flops=0, transcendentals=0, bytes_accessed=8 * parts * rows * width
         ),
         name="split_pieces",
     )(places, whole)
+    return pieces[:parts], pieces[parts:]
+
+
+def fold_kernel(kept, came, *pieces):
+    depth = pieces[0].shape[0]
+    for i, piece in enumerate(pieces):
+        rows = pl.ds(i * depth, depth)
+        piece[...] = (kept[rows, :].astype(F32) + came[rows, :].astype(F32)).astype(BF)
+
+
+def fold(kept, came, half):
+    rows, width = kept.shape
+    depth = rows // half
+    whole = pl.BlockSpec((rows, width), lambda i: (0, 0))
+    return pl.pallas_call(
+        fold_kernel,
+        grid=(1,),
+        in_specs=[whole, whole],
+        out_specs=[pl.BlockSpec((depth, width), lambda i: (0, 0))] * half,
+        out_shape=(jax.ShapeDtypeStruct((depth, width), BF),) * half,
+        compiler_params=pltpu.CompilerParams(vmem_limit_bytes=24 << 20),
+        cost_estimate=pl.CostEstimate(
+            flops=0, transcendentals=0, bytes_accessed=6 * rows * width
+        ),
+        name="fold_pieces",
+    )(kept, came)
+
+
+def gelu_parts(gate):
+    square = gate * gate
+    t = jnp.tanh(gate * (0.7978845608028654 + 0.035677408136300125 * square))
+    half = 0.5 + 0.5 * t
+    value = gate * half
+    slope = half + 0.5 * gate * (1.0 - t * t) * (0.7978845608028654 + 0.10703222440890037 * square)
+    return value, slope
+
+
+def bring(count, place_ref, pieces, whole, sems, out):
+    depth, wide = pieces[0].shape
+    copies = [
+        pltpu.make_async_copy(
+            piece,
+            whole.at[
+                pl.ds(pl.multiple_of(place_ref[i % count] * depth, depth), depth),
+                pl.ds(i // count * wide, wide),
+            ],
+            sems.at[i],
+        )
+        for i, piece in enumerate(pieces)
+    ]
+    save = pltpu.make_async_copy(whole, out, sems.at[len(pieces)])
+
+    @pl.when(pl.program_id(0) == 0)
+    def _():
+        for copy in copies:
+            copy.start()
+        for copy in copies:
+            copy.wait()
+        save.start()
+
+    return save
+
+
+def gate_up_block(norm_ref, whole, product_ref, to_gate_ref, to_up_ref):
+    hidden = product_ref.shape[1]
+    step = 384
+    for start in range(0, hidden, step):
+        cols = slice(start, start + step)
+        gate = dot(norm_ref[...], whole[:, cols])
+        up = dot(norm_ref[...], whole[:, hidden + start : hidden + start + step])
+        value, slope = gelu_parts(gate)
+        product_ref[:, cols] = (value * up).astype(BF)
+        to_gate_ref[:, cols] = (up * slope).astype(BF)
+        to_up_ref[:, cols] = value.astype(BF)
+
+
+def gate_up_first_kernel(count, place_ref, norm_ref, *refs):
+    pieces = refs[: 2 * count]
+    product_ref, to_gate_ref, to_up_ref, out, whole, sems = refs[2 * count :]
+    save = bring(count, place_ref, pieces, whole, sems, out)
+    gate_up_block(norm_ref, whole, product_ref, to_gate_ref, to_up_ref)
+
+    @pl.when(pl.program_id(0) == pl.num_programs(0) - 1)
+    def _():
+        save.wait()
+
+
+def gate_up_first(norm, places, gate_pieces, up_pieces):
+    rows, width = norm.shape
+    count = len(gate_pieces)
+    hidden = gate_pieces[0].shape[1]
+    block = 256
+    out = pl.BlockSpec((block, hidden), lambda i, s: (i, 0))
+    anywhere = pl.BlockSpec(memory_space=pl.ANY)
+    return pl.pallas_call(
+        functools.partial(gate_up_first_kernel, count),
+        grid_spec=pltpu.PrefetchScalarGridSpec(
+            num_scalar_prefetch=1,
+            grid=(rows // block,),
+            in_specs=[pl.BlockSpec((block, width), lambda i, s: (i, 0))] + [anywhere] * (2 * count),
+            out_specs=[out, out, out, anywhere],
+            scratch_shapes=[
+                pltpu.VMEM((width, 2 * hidden), BF),
+                pltpu.SemaphoreType.DMA((2 * count + 1,)),
+            ],
+        ),
+        out_shape=(jax.ShapeDtypeStruct((2 * rows, hidden), BF),) * 3
+        + (jax.ShapeDtypeStruct((width, 2 * hidden), BF),),
+        compiler_params=pltpu.CompilerParams(vmem_limit_bytes=36 << 20),
+        cost_estimate=pl.CostEstimate(
+            flops=4 * rows * width * hidden,
+            transcendentals=rows * hidden,
+            bytes_accessed=2 * rows * width + 6 * rows * hidden + 8 * width * hidden,
+        ),
+        name="gate_up_first",
+    )(places, norm, *gate_pieces, *up_pieces)
+
+
+def gate_up_rest_kernel(norm_ref, whole_ref, a, b, c, product_ref, to_gate_ref, to_up_ref):
+    del a, b, c
+    gate_up_block(norm_ref, whole_ref, product_ref, to_gate_ref, to_up_ref)
+
+
+def gate_up_rest(norm, gate_up, *earlier):
+    rows, width = norm.shape
+    hidden = gate_up.shape[1] // 2
+    block = 256
+    steps = rows // block
+    out = pl.BlockSpec((block, hidden), lambda i: (i + steps, 0))
+    anywhere = pl.BlockSpec(memory_space=pl.ANY)
+    return pl.pallas_call(
+        gate_up_rest_kernel,
+        grid=(steps,),
+        in_specs=[
+            pl.BlockSpec((block, width), lambda i: (i, 0)),
+            pl.BlockSpec(gate_up.shape, lambda i: (0, 0), pipeline_mode=pl.Buffered(1)),
+            anywhere,
+            anywhere,
+            anywhere,
+        ],
+        out_specs=[out, out, out],
+        out_shape=(jax.ShapeDtypeStruct((2 * rows, hidden), BF),) * 3,
+        input_output_aliases={2: 0, 3: 1, 4: 2},
+        compiler_params=pltpu.CompilerParams(vmem_limit_bytes=36 << 20),
+        cost_estimate=pl.CostEstimate(
+            flops=4 * rows * width * hidden,
+            transcendentals=rows * hidden,
+            bytes_accessed=2 * rows * width + 6 * rows * hidden + 4 * width * hidden,
+        ),
+        name="gate_up_rest",
+    )(norm, gate_up, *earlier)
+
+
+def product_gradient_kernel(count, place_ref, cot_ref, to_gate_ref, to_up_ref, *refs):
+    pieces = refs[:count]
+    dgate_ref, dup_ref, out, whole, sems = refs[count:]
+    save = bring(count, place_ref, pieces, whole, sems, out)
+    step = 384
+    for start in range(0, whole.shape[1], step):
+        cols = slice(start, start + step)
+        grad = dot(cot_ref[...], whole[:, cols])
+        dgate_ref[:, cols] = (grad * to_gate_ref[:, cols].astype(F32)).astype(BF)
+        dup_ref[:, cols] = (grad * to_up_ref[:, cols].astype(F32)).astype(BF)
+
+    @pl.when(pl.program_id(0) == pl.num_programs(0) - 1)
+    def _():
+        save.wait()
+
+
+def product_gradient(cot, to_gate, to_up, places, pieces):
+    rows, width = cot.shape
+    count = len(pieces)
+    hidden = to_gate.shape[1]
+    block = 256
+    part = pl.BlockSpec((block, hidden), lambda i, s: (i, 0))
+    anywhere = pl.BlockSpec(memory_space=pl.ANY)
+    return pl.pallas_call(
+        functools.partial(product_gradient_kernel, count),
+        grid_spec=pltpu.PrefetchScalarGridSpec(
+            num_scalar_prefetch=1,
+            grid=(rows // block,),
+            in_specs=[pl.BlockSpec((block, width), lambda i, s: (i, 0)), part, part]
+            + [anywhere] * count,
+            out_specs=[part, part, anywhere],
+            scratch_shapes=[
+                pltpu.VMEM((width, hidden), BF),
+                pltpu.SemaphoreType.DMA((count + 1,)),
+            ],
+        ),
+        out_shape=(jax.ShapeDtypeStruct((rows, hidden), BF),) * 2
+        + (jax.ShapeDtypeStruct((width, hidden), BF),),
+        compiler_params=pltpu.CompilerParams(vmem_limit_bytes=32 << 20),
+        cost_estimate=pl.CostEstimate(
+            flops=2 * rows * width * hidden,
+            transcendentals=0,
+            bytes_accessed=2 * rows * width + 8 * rows * hidden + 4 * width * hidden,
+        ),
+        name="product_gradient",
+    )(places, cot, to_gate, to_up, *pieces)
+
+
+def feed_back_kernel(dgate_ref, dup_ref, gate_up_ref, kept_ref, sent_ref):
+    hidden = dgate_ref.shape[1]
+    total = dot(dgate_ref[...], gate_up_ref[:, :hidden], NT)
+    total = (total + dot(dup_ref[...], gate_up_ref[:, hidden:], NT)).astype(BF)
+
+    @pl.when(pl.program_id(0) < pl.num_programs(0) // 2)
+    def _():
+        kept_ref[...] = total
+
+    @pl.when(pl.program_id(0) >= pl.num_programs(0) // 2)
+    def _():
+        sent_ref[...] = total
+
+
+def feed_back(first, rows, dgate, dup, gate_up):
+    width, hidden = gate_up.shape[0], dgate.shape[1]
+    block = 256
+    steps = rows // block
+    skip = first // block
+    part = pl.BlockSpec((block, hidden), lambda i: (i + skip, 0))
+    return pl.pallas_call(
+        feed_back_kernel,
+        grid=(steps,),
+        in_specs=[
+            part,
+            part,
+            pl.BlockSpec(gate_up.shape, lambda i: (0, 0), pipeline_mode=pl.Buffered(1)),
+        ],
+        out_specs=[
+            pl.BlockSpec((block, width), lambda i: (jnp.minimum(i, steps // 2 - 1), 0)),
+            pl.BlockSpec((block, width), lambda i: (jnp.maximum(i - steps // 2, 0), 0)),
+        ],
+        out_shape=(jax.ShapeDtypeStruct((rows // 2, width), BF),) * 2,
+        compiler_params=pltpu.CompilerParams(vmem_limit_bytes=36 << 20),
+        cost_estimate=pl.CostEstimate(
+            flops=4 * rows * width * hidden,
+            transcendentals=0,
+            bytes_accessed=2 * rows * width + 4 * rows * hidden + 4 * width * hidden,
+        ),
+        name="feed_back",
+    )(dgate, dup, gate_up)
 
 
 class Shards:
@@ -294,39 +591,12 @@
     def near(self, value):
         return lax.ppermute(value, "shard", [(i, i ^ 1) for i in range(self.count)])
 
-    def gather_far(self, piece):
-        return [piece] + [self.far(piece, k) for k in range(1, self.half)]
-
-    def gather_near(self, pieces):
-        return pieces + [self.near(piece) for piece in pieces]
-
     def whole(self, pieces):
         return assemble(self.places, pieces)
 
-    def scatter(self, value):
-        pieces = split(self.places, value, self.count)
-        kept, sent = pieces[: self.half], pieces[self.half :]
-        sums = [
-            (a.astype(F32) + self.near(b).astype(F32)).astype(BF) for a, b in zip(kept, sent)
-        ]
-        total = sums[0].astype(F32)
-        for k in range(1, self.half):
-            total = total + self.far(sums[k], k).astype(F32)
-        return total
-
 
 def tp_swap(value, mask):
     return lax.ppermute(value, "tp", [(i, i ^ mask) for i in range(4)])
-
-
-def gelu_parts(gate):
-    inner = 0.7978845608028654 * (gate + 0.044715 * gate * gate * gate)
-    t = jnp.tanh(inner)
-    value = 0.5 * gate * (1.0 + t)
-    slope = 0.5 * (1.0 + t) + 0.5 * gate * (1.0 - t * t) * 0.7978845608028654 * (
-        1.0 + 3.0 * 0.044715 * gate * gate
-    )
-    return value, slope
 
 
 def local(count, tokens, w_query, w_keyval, w_out, w_gate, w_up, w_down, gain_attn, gain_mlp, cotangent):
@@ -355,117 +625,263 @@
     send_up = (own_up * gain_two).astype(BF)
     send_down = jnp.transpose(w_down).astype(BF)
 
-    far_in = shards.gather_far(send_in)
-    far_out = shards.gather_far(after(send_out, *far_in[1:]))
-    far_gate = shards.gather_far(after(send_gate, *far_out[1:]))
-    far_up = shards.gather_far(after(send_up, *far_gate[1:]))
-    far_down = shards.gather_far(after(send_down, *far_up[1:]))
+    heads = GROUP * HD
+    half_count = shards.half
+    places = shards.places
+    most, part = range(1, half_count - 1), half_count // 2
+    token = places
+
+    def sync(*values):
+        nonlocal token
+        token, *values = lax.optimization_barrier((token, *values))
+        return values
+
+    def far_most(piece):
+        return [shards.far(piece, k) for k in most]
+
+    def far_last(piece):
+        return [shards.far(piece, half_count - 1)]
+
+    def near(pieces):
+        return [shards.near(piece) for piece in pieces]
+
+    def rows_of(value, other):
+        return lax.dynamic_slice_in_dim(value, (core ^ other) * rows, rows, 0)
 
     inputs = tokens.reshape(rows, width).astype(F32)
     scale_one = lax.rsqrt(jnp.mean(inputs * inputs, axis=-1, keepdims=True) + EPS)
     unit_own = (inputs * scale_one).astype(BF)
-    unit = in_order(unit_own, tp_swap(unit_own, 1))
+    far_in = far_most(send_in) + far_last(send_in)
+    unit_other = tp_swap(unit_own, 1)
     cot = cotangent.reshape(4, rows, width)
     cots = [lax.dynamic_index_in_dim(cot, tp ^ k, 0, keepdims=False) for k in range(4)]
-    cot_near = jnp.concatenate(cots[:2], 0)
-    cot_far = jnp.concatenate(cots[2:], 0)
-
-    in_full = shards.whole(shards.gather_near(far_in))
-    in_query = in_full[:, : GROUP * HD]
-    in_key = in_full[:, GROUP * HD :]
-    in_query_b = tp_swap(in_query, 2)
-    out_full = shards.whole(shards.gather_near(far_out))
-    out_full_b = tp_swap(after(out_full, in_query_b), 2)
-
-    half = dot(unit, in_key).astype(BF)
+    cot_all = jnp.concatenate(cots, 0)
+    send_in, cot_all, send_out, unit_other, *far_in = sync(
+        send_in, cot_all, send_out, unit_other, *far_in
+    )
+
+    far_in = [send_in] + far_in
+    near_in = near(far_in)
+    far_out = far_most(send_out) + far_last(send_out)
+    query_far_b = tp_swap(pack(far_in, heads), 2)
+    unit = in_order(unit_own, unit_other)
+    unit, query_far_b, send_gate, send_up, *pieces = sync(
+        unit, query_far_b, send_gate, send_up, *far_in, *near_in, *far_out
+    )
+    far_in, near_in, far_out = (
+        pieces[:half_count],
+        pieces[half_count : 2 * half_count],
+        [send_out] + pieces[2 * half_count :],
+    )
+
+    in_full = shards.whole(far_in + near_in)
+    in_query = in_full[:, :heads]
+    scale = HD ** (-0.5)
+    column = lax.broadcasted_iota(jnp.int32, (1, in_full.shape[1]), 1)
+    query_half = (
+        dot(unit, in_full) * jnp.where(column < heads, scale * LOG2E, 1.0)
+    ).astype(BF)
+    half = query_half[:, heads:]
     half_other = tp_swap(half, 1)
     before = lax.ppermute(half, "tp", [(0, 2), (1, 3)])
     before_other = tp_swap(before, 1)
+    query_near_b = tp_swap(after(pack(near_in, heads), half), 2)
+    near_out = near(far_out)
+    far_gate = far_most(send_gate)
     own_pair = jnp.concatenate([before, half], 0)
     other_pair = jnp.concatenate([before_other, half_other], 0)
     keys = jnp.where(first_core, own_pair, other_pair)
     values = jnp.where(first_core, other_pair, own_pair)
+    query_half, keys, values, query_near_b, send_gate, *pieces = sync(
+        query_half, keys, values, query_near_b, send_gate, *near_out, *far_gate
+    )
+    near_out, far_gate = pieces[:half_count], [send_gate] + pieces[half_count:]
+
     keys_t = jnp.transpose(keys)
     values_t = jnp.transpose(values)
-
-    scale = HD ** (-0.5)
-    query_a = (dot(unit, in_query) * (scale * LOG2E)).astype(BF)
-    mixed_a, lse_a = forward_attention(chip_table, query_a, keys, values_t)
+    far_gate += far_last(send_gate)
+    near_gate = near(far_gate[:part])
+    out_far_b = tp_swap(pack(far_out, heads), 2)
+    mixed_a, lse_a = forward_attention(chip_table, query_half, keys, values_t)
+    in_query_b = unpack(places, query_far_b, query_near_b, half_count)
     query_b = (dot(unit, in_query_b) * (scale * LOG2E)).astype(BF)
+    out_full = shards.whole(far_out + near_out)
+    mixed_a, query_b, out_far_b, send_up, *pieces = sync(
+        mixed_a, query_b, out_far_b, send_up, *far_gate[1:], *near_gate
+    )
+    far_gate, near_gate = [send_gate] + pieces[: half_count - 1], pieces[half_count - 1 :]
+
+    far_up = far_most(send_up)
+    near_gate += near(far_gate[part:])
+    out_near_b = tp_swap(pack(near_out, heads), 2)
     mixed_b, lse_b = forward_attention(chip_table, query_b, keys, values_t)
-
-    branch = dot(mixed_a, out_full, NT) + dot(mixed_b, out_full_b, NT)
-    branch_own = lax.dynamic_slice_in_dim(branch, core * rows, rows, 0)
-    branch_other = lax.dynamic_slice_in_dim(branch, (1 - core) * rows, rows, 0).astype(BF)
-    hidden = inputs + (branch_own + tp_swap(branch_other, 1).astype(F32))
+    branch_other = dot(rows_of(mixed_a, 1), out_full, NT)
+    branch_own = dot(rows_of(mixed_a, 0), out_full, NT)
+    mixed_b, out_near_b, branch_other, branch_own, send_up, *pieces = sync(
+        mixed_b, out_near_b, branch_other, branch_own, send_up, *far_up, *near_gate
+    )
+    far_up, near_gate = [send_up] + pieces[: len(most)], pieces[len(most) :]
+
+    far_up += far_last(send_up)
+    near_up = near(far_up[:part])
+    out_full_b = unpack(places, out_far_b, out_near_b, half_count)
+    branch_other = (branch_other + dot(rows_of(mixed_b, 1), out_full_b, NT)).astype(BF)
+    branch_came = tp_swap(branch_other, 1)
+    branch_own = branch_own + dot(rows_of(mixed_b, 0), out_full_b, NT)
+    hidden = inputs + (branch_own + branch_came.astype(F32))
     scale_two = lax.rsqrt(jnp.mean(hidden * hidden, axis=-1, keepdims=True) + EPS)
     norm_own = (hidden * scale_two).astype(BF)
-    norm_x = tp_swap(norm_own, 2)
-    norm_near = jnp.concatenate([norm_own, tp_swap(norm_own, 1)], 0)
-    norm_far = jnp.concatenate([norm_x, tp_swap(norm_x, 1)], 0)
-
-    gate_full = shards.whole(shards.gather_near(far_gate))
-    up_full = shards.whole(shards.gather_near(far_up))
-    down_full = shards.whole(shards.gather_near(far_down))
-
-    def feed_forward(norm, cot_part):
-        gate = dot(norm, gate_full)
-        up = dot(norm, up_full)
-        value, slope = gelu_parts(gate)
-        product = (value * up).astype(BF)
-        grad_product = dot(cot_part, down_full)
-        grad_gate = (grad_product * up * slope).astype(BF)
-        grad_up = (grad_product * value).astype(BF)
-        return product, grad_gate, grad_up
-
-    product_near, dgate_near, dup_near = feed_forward(norm_near, cot_near)
-    product_far, dgate_far, dup_far = feed_forward(norm_far, cot_far)
-
-    def reduce_rows(near, far):
-        out_far = far[:rows] + tp_swap(far[rows:].astype(BF), 1).astype(F32)
-        mine = near[:rows] + tp_swap(near[rows:].astype(BF), 1).astype(F32)
-        return mine + tp_swap(out_far.astype(BF), 2).astype(F32)
-
-    back_far = dot(dgate_far, gate_full, NT) + dot(dup_far, up_full, NT)
-    back_near = dot(dgate_near, gate_full, NT) + dot(dup_near, up_full, NT)
-    grad_norm = reduce_rows(back_near, back_far)
-
-    down_far = dot(product_far, down_full, NT)
-    down_near = dot(product_near, down_full, NT)
-    output = (hidden + reduce_rows(down_near, down_far)).astype(BF)
-
+    norm_own, send_down, *pieces = sync(norm_own, send_down, *far_up[1:], *near_up)
+    far_up, near_up = [send_up] + pieces[: half_count - 1], pieces[half_count - 1 :]
+
+    cut = rows // 16 * 9
+    far_down = far_most(send_down)
+    near_up += near(far_up[part:])
+    norm_core = tp_swap(norm_own, 1)
+    norm_x1 = tp_swap(norm_own[:cut], 2)
+    norm_near = jnp.concatenate([norm_own, norm_core], 0)
+    norm_near, norm_x1, send_down, *pieces = sync(
+        norm_near, norm_x1, send_down, *far_down, *near_up
+    )
+    far_down, near_up = [send_down] + pieces[: len(most)], pieces[len(most) :]
+
+    far_down += far_last(send_down)
+    near_down = near(far_down[:part])
+    norm_x2 = tp_swap(norm_own[cut:], 2)
+    norm_d1 = tp_swap(norm_x1, 1)
+    product, to_gate, to_up, gate_up_full = gate_up_first(
+        norm_near, places, far_gate + near_gate, far_up + near_up
+    )
+    norm_x2, norm_d1, product, to_gate, to_up, *pieces = sync(
+        norm_x2, norm_d1, product, to_gate, to_up, *far_down[1:], *near_down
+    )
+    far_down, near_down = [send_down] + pieces[: half_count - 1], pieces[half_count - 1 :]
+
+    near_down += near(far_down[part:])
+    norm_d2 = tp_swap(norm_x2, 1)
+    norm_far = jnp.concatenate([norm_x1, norm_x2, norm_d1, norm_d2], 0)
+    product, to_gate, to_up = gate_up_rest(norm_far, gate_up_full, product, to_gate, to_up)
     norm_all = jnp.concatenate([norm_near, norm_far], 0)
-    g_down = dot(
-        jnp.concatenate([cot_near, cot_far], 0), jnp.concatenate([product_near, product_far], 0), TN
-    ).astype(BF)
-    g_gate = dot(norm_all, jnp.concatenate([dgate_near, dgate_far], 0), TN).astype(BF)
-    g_up = dot(norm_all, jnp.concatenate([dup_near, dup_far], 0), TN).astype(BF)
-    grad_w_down = jnp.transpose(shards.scatter(g_down))
-    sum_gate = shards.scatter(g_gate)
-    sum_up = shards.scatter(g_up)
-    grad_w_gate = sum_gate * gain_two
-    grad_w_up = sum_up * gain_two
-    gain_two_part = jnp.sum(own_gate * sum_gate + own_up * sum_up, axis=1)
-
+    g_down = dot(cot_all, product, TN).astype(BF)
+    kept_down, sent_down = split(places, g_down, half_count, 2)
+    cot_all, sent, *near_down = sync(cot_all, sent_down[0], *near_down)
+
+    came = shards.near(sent)
+    dgate, dup, down_full = product_gradient(
+        cot_all, to_gate, to_up, places, far_down + near_down
+    )
+    came_down = [came]
+    dgate, sent, *came_down = sync(dgate, sent_down[1], *came_down)
+
+    came_down.append(shards.near(sent))
+    back_x, back_diagonal = feed_back(2 * rows, 2 * rows, dgate, dup, gate_up_full)
+    sums_down = list(fold(kept_down[0], came_down[0], part))
+    back_diagonal = tp_swap(back_diagonal, 1)
+    back_far = [
+        (a.astype(F32) + b.astype(F32)).astype(BF)
+        for a, b in (
+            (back_x[:cut], back_diagonal[:cut]),
+            (back_x[cut:], back_diagonal[cut:]),
+        )
+    ]
+    dgate, *pieces = sync(dgate, *back_far, came_down[1], *sums_down)
+    back_far, came_down[1], sums_down = pieces[:2], pieces[2], pieces[3:]
+
+    back_came = [tp_swap(back_far[0], 2)]
+    far_sums = [shards.far(sums_down[0], part)]
+    sums_down = list(fold(kept_down[1], came_down[1], part)) + sums_down
+    g_gate = dot(norm_all, dgate, TN).astype(BF)
+    kept_gate, sent_gate = split(places, g_gate, half_count, 2)
+    product_down = product
+    down_x = dot(product_down[2 * rows : 3 * rows], down_full, NT).astype(BF)
+    down_diagonal = dot(product_down[3 * rows :], down_full, NT).astype(BF)
+    dup, back_far[1], sent, down_diagonal, *pieces = sync(
+        dup, back_far[1], sent_gate[0], down_diagonal, *back_came, *far_sums, *sums_down
+    )
+    back_came, far_sums, sums_down = [pieces[0]], [pieces[1]], pieces[2:]
+
+    back_came.append(tp_swap(back_far[1], 2))
+    came_gate = [shards.near(sent)]
+    others = [k for k in range(1, half_count) if k != part]
+    far_sums += [shards.far(sums_down[k], k) for k in others]
+    down_diagonal = tp_swap(down_diagonal, 1)
+    g_up = dot(norm_all, dup, TN).astype(BF)
+    kept_up, sent_up = split(places, g_up, half_count, 2)
+    down_far = (down_x.astype(F32) + down_diagonal.astype(F32)).astype(BF)
+    dgate, sent, down_far, *pieces = sync(
+        dgate, sent_gate[1], down_far, *back_came, *came_gate, *far_sums
+    )
+    back_came, came_gate, far_sums_down = pieces[:2], [pieces[2]], pieces[3:]
+
+    came_gate.append(shards.near(sent))
+    down_came = [tp_swap(down_far[:cut], 2)]
+    back_own, back_core = feed_back(0, 2 * rows, dgate, dup, gate_up_full)
+    back_core = tp_swap(back_core, 1)
+    sums_gate = list(fold(kept_gate[0], came_gate[0], part))
+    back_own, back_core, sent, *pieces = sync(
+        back_own, back_core, sent_up[0], *down_came, came_gate[1], *sums_gate
+    )
+    down_came, came_gate[1], sums_gate = [pieces[0]], pieces[1], pieces[2:]
+
+    came_up = [shards.near(sent)]
+    far_sums = [shards.far(sums_gate[0], part)]
+    sums_gate = list(fold(kept_gate[1], came_gate[1], part)) + sums_gate
+    grad_norm = (
+        back_own.astype(F32)
+        + back_core.astype(F32)
+        + jnp.concatenate(back_came, 0).astype(F32)
+    )
     unit_two = hidden * scale_two
     grad_hidden = cots[0].astype(F32) + scale_two * (
         grad_norm - unit_two * jnp.mean(grad_norm * unit_two, axis=-1, keepdims=True)
     )
-    grad_branch_own = grad_hidden.astype(BF)
-    grad_branch = in_order(grad_branch_own, tp_swap(grad_branch_own, 1))
-
-    grad_mixed_b = dot(grad_branch, out_full_b).astype(BF)
+    branch_own = grad_hidden.astype(BF)
+    branch_other = tp_swap(branch_own, 1)
+    g_out_b = dot(branch_own, rows_of(mixed_b, 0), TN)
+    grad_own = dot(branch_own, out_full_b).astype(BF)
+    branch_other = after(branch_other, g_out_b, grad_own)
+    g_out_b = (g_out_b + dot(branch_other, rows_of(mixed_b, 1), TN)).astype(BF)
+    g_out_came = tp_swap(g_out_b, 2)
+    grad_mixed_b = in_order(grad_own, dot(branch_other, out_full_b).astype(BF))
+    grad_mixed_b, sent, *pieces = sync(
+        grad_mixed_b, sent_up[1], *came_up, *far_sums, *sums_gate
+    )
+    came_up, far_sums, sums_gate = [pieces[0]], [pieces[1]], pieces[2:]
+
+    came_up.append(shards.near(sent))
+    far_sums += [shards.far(sums_gate[k], k) for k in others]
+    sums_up = list(fold(kept_up[0], came_up[0], part))
     dq_b, dk_b, dv_b = backward_attention(
         chip_table, query_b, grad_mixed_b, mixed_b, lse_b, keys, keys_t, values
     )
     g_query_b = dot(unit, dq_b, TN).astype(BF)
-    g_out_b = dot(grad_branch, mixed_b, TN).astype(BF)
-    grad_mixed_a = dot(grad_branch, out_full).astype(BF)
+    dq_b, g_query_b, g_out_came, *pieces = sync(
+        dq_b, g_query_b, g_out_came, came_up[1], *far_sums, *sums_up
+    )
+    came_up[1], far_sums_gate, sums_up = (
+        pieces[0],
+        pieces[1:half_count],
+        pieces[half_count:],
+    )
+
+    g_query_came = tp_swap(g_query_b, 2)
+    far_sums = [shards.far(sums_up[0], part)]
+    sums_up = list(fold(kept_up[1], came_up[1], part)) + sums_up
+    g_out = (
+        dot(branch_own, rows_of(mixed_a, 0), TN)
+        + dot(branch_other, rows_of(mixed_a, 1), TN)
+        + g_out_came.astype(F32)
+    )
+    (kept_out,), (sent_out,) = split(places, g_out.astype(BF), half_count)
+    came_out = shards.near(sent_out)
+    grad_mixed_a = in_order(
+        dot(branch_own, out_full).astype(BF), dot(branch_other, out_full).astype(BF)
+    )
     dq_a, dk_a, dv_a = backward_attention(
-        chip_table, query_a, grad_mixed_a, mixed_a, lse_a, keys, keys_t, values
-    )
-    g_out = dot(grad_branch, mixed_a, TN) + tp_swap(g_out_b, 2).astype(F32)
-    grad_w_out = jnp.transpose(shards.scatter(g_out.astype(BF)))
+        chip_table, query_half, after(grad_mixed_a, sent_out), mixed_a, lse_a, keys, keys_t, values
+    )
+    dq_a, came_out, *pieces = sync(dq_a, came_out, *far_sums, *sums_up)
+    far_sums, sums_up = [pieces[0]], pieces[1:]
 
     grad_keys = (dk_a + dk_b) * LN2
     grad_values = dv_a + dv_b
@@ -473,32 +889,71 @@
     theirs = jnp.where(first_core, grad_values, grad_keys).astype(BF)
     mine = mine + tp_swap(theirs, 1).astype(F32)
     chip_rows = mine.shape[0] // 2
+    g_query = (dot(unit, dq_a, TN) + g_query_came.astype(F32)).astype(BF)
+    (kept_query,), (sent_query,) = split(places, g_query, half_count)
     earlier = lax.ppermute(mine[:chip_rows].astype(BF), "tp", [(2, 0), (3, 1)])
     grad_half = (mine[chip_rows:] + earlier.astype(F32)).astype(BF)
-
-    g_query = dot(unit, dq_a, TN) + tp_swap(g_query_b, 2).astype(F32)
-    g_half = dot(unit, grad_half, TN)
-    g_in = jnp.concatenate([g_query, g_half], 1).astype(BF)
-    sum_in = shards.scatter(g_in)
-
-    back = dot(dq_a, in_query, NT) + dot(dq_b, in_query_b, NT) + dot(grad_half, in_key, NT)
-    back_own = lax.dynamic_slice_in_dim(back, core * rows, rows, 0)
-    back_other = lax.dynamic_slice_in_dim(back, (1 - core) * rows, rows, 0).astype(BF)
-    grad_unit = back_own + tp_swap(back_other, 1).astype(F32)
+    came_query = shards.near(sent_query)
+    far_sums += [shards.far(sums_up[k], k) for k in others]
+    sums_out = fold(kept_out, came_out, half_count)
+    dq_a1, dq_b1 = after(dq_a, sent_query), after(dq_b, sent_query)
+    back_other = dot(rows_of(dq_a1, 1), in_query, NT) + dot(rows_of(dq_b1, 1), in_query_b, NT)
+    back_own = dot(rows_of(dq_a1, 0), in_query, NT) + dot(rows_of(dq_b1, 0), in_query_b, NT)
+    g_half = dot(unit, after(grad_half, back_own), TN).astype(BF)
+    (kept_half,), (sent_half,) = split(places, g_half, half_count)
+    back_other, back_own, grad_half, sent_half, came_query, *pieces = sync(
+        back_other, back_own, grad_half, sent_half, came_query, *far_sums, *sums_out
+    )
+    far_sums_up, sums_out = pieces[: half_count - 1], pieces[half_count - 1 :]
+
+    came_half = shards.near(sent_half)
+    sums_query = fold(kept_query, came_query, half_count)
+    far_query = [shards.far(sums_query[k], k) for k in range(1, half_count)]
+    far_out_sums = [shards.far(sums_out[k], k) for k in range(1, half_count)]
+    in_half = in_full[:, heads:]
+    back_other = (back_other + dot(rows_of(grad_half, 1), in_half, NT)).astype(BF)
+    back_came = tp_swap(back_other, 1)
+    back_own = back_own + dot(rows_of(grad_half, 0), in_half, NT)
+    down_came.append(tp_swap(down_far[cut:], 2))
+    down_own = dot(after(product, back_own)[:rows], down_full, NT).astype(BF)
+    down_core = dot(after(product, back_own)[rows : 2 * rows], down_full, NT).astype(BF)
+    sums_half = fold(kept_half, after(came_half, back_own, *sums_query), half_count)
+    far_half = [shards.far(sums_half[k], k) for k in range(1, half_count)]
+
+    grad_unit = back_own + back_came.astype(F32)
     unit_one = inputs * scale_one
     grad_tokens = grad_hidden + scale_one * (
         grad_unit - unit_one * jnp.mean(grad_unit * unit_one, axis=-1, keepdims=True)
     )
-
-    sum_query = sum_in[:, : GROUP * HD]
-    sum_half = sum_in[:, GROUP * HD :]
-    gain_query_part = jnp.sum(own_query * sum_query, axis=1)
-    gain_half_part = jnp.sum(keyval_half * sum_half, axis=1)
-    gains = jnp.stack([gain_query_part + gain_half_part, gain_two_part], 0)
-    gains = gains + tp_swap(gains, 1)
-    gains = gains + tp_swap(gains, 2)
-    sum_half = sum_half + tp_swap(sum_half, 2)
-    half_swapped = tp_swap(sum_half, 1)
+    output = (
+        hidden
+        + down_own.astype(F32)
+        + tp_swap(down_core, 1).astype(F32)
+        + jnp.concatenate(down_came, 0).astype(F32)
+    ).astype(BF)
+
+    def total(own, others):
+        return functools.reduce(lambda t, o: t + o.astype(F32), others, own.astype(F32))
+
+    sum_gate = total(sums_gate[0], far_sums_gate)
+    sum_up = total(sums_up[0], far_sums_up)
+    grad_w_gate = sum_gate * gain_two
+    grad_w_up = sum_up * gain_two
+    gain_two_part = jnp.sum(own_gate * sum_gate + own_up * sum_up, axis=1)
+    grad_w_down = jnp.transpose(total(sums_down[0], far_sums_down))
+    grad_w_out = jnp.transpose(total(sums_out[0], far_out_sums))
+    sum_query = total(sums_query[0], far_query)
+    sum_half = total(sums_half[0], far_half)
+
+    gain_one_part = jnp.sum(own_query * sum_query, axis=1) + jnp.sum(keyval_half * sum_half, axis=1)
+    small = jnp.concatenate(
+        [jnp.transpose(sum_half), gain_one_part[None], gain_two_part[None], jnp.zeros((6, sum_half.shape[0]), F32)], 0
+    )
+    small = small + tp_swap(small, 2)
+    other = tp_swap(small, 1)
+    gains = small[HD : HD + 2] + other[HD : HD + 2]
+    sum_half = jnp.transpose(small[:HD])
+    half_swapped = jnp.transpose(other[:HD])
     grad_w_keyval = (
         jnp.where(
             first_core,

time: 857 us -> 643 us (0.75)
  waiting for transfers between devices: 369 us -> 211 us
  matrix products: 183 us -> 96 us
  Pallas kernels: 60.8 us -> 132 us
  starting transfers between devices: 152 us -> 110 us
    dot_general x30, matrix products: 183 us -> 96 us  [dot(): return lax.dot_general(a, b, dims, preferred_element_type=F32)]
    pallas_call x5 -> x26, Pallas kernels: 4.65 us -> 79.9 us  [the longest x2 25.6 us: feed_back(): pl.pallas_call(feed_back_kernel, grid=(steps,), in_specs=[part, part, pl....]
    ppermute x40 -> x29, waiting for transfers between devices: 110 us -> 62.5 us  [near(): return lax.ppermute(value, 'shard', [(i, i ^ 1) for i in range(self.count)])]
    ppermute x24 -> x28, waiting for transfers between devices: 54.8 us -> 8.77 us  [tp_swap(): return lax.ppermute(value, 'tp', [(i, i ^ mask) for i in range(4)])]
    ppermute x30 -> x33, starting transfers between devices: 91.8 us -> 47.1 us  [far(): lax.ppermute(value, 'shard', [(i, (i // 2 ^ k) * 2 + i % 2) for i in rang...]
    ppermute x1, waiting for transfers between devices: 45.9 us -> 7.52 us  [local(): earlier = lax.ppermute(mine[:chip_rows].astype(BF), 'tp', [(2, 0), (3, 1)])]
    ppermute x30 -> x33, waiting for transfers between devices: 158 us -> 129 us  [far(): lax.ppermute(value, 'shard', [(i, (i // 2 ^ k) * 2 + i % 2) for i in rang...]
    ppermute x24 -> x28, starting transfers between devices: 17 us -> 30.2 us  [tp_swap(): return lax.ppermute(value, 'tp', [(i, i ^ mask) for i in range(4)])]
  transfers between devices with their start and end apart: 96 -> 92, of which waited for: 42 -> 37; matrix products, arithmetic and copies ran while one was open for 25% -> 21% of each run, Pallas kernels for 5% -> 15%
where the time goes in v2:
time: 643 us; the launch traced here: 638 us
  waiting for transfers between devices  211 us (33%)
  Pallas kernels  132 us (21%)
  starting transfers between devices  110 us (17%)
  matrix products  96 us (15%)
  local copies, waits for them, and re-layouts  43.5 us (7%)
  other arithmetic  41.9 us (7%)
    ppermute x33, waiting for transfers between devices, far(): lax.ppermute(value, 'shard', [(i, (i // 2 ^ k) * 2 + i % 2) for i in rang...  129 us
    dot_general x30, matrix products, dot(): return lax.dot_general(a, b, dims, preferred_element_type=F32)  96 us
    ppermute x29, waiting for transfers between devices, near(): return lax.ppermute(value, 'shard', [(i, i ^ 1) for i in range(self.count)])  62.5 us
    ppermute x33, starting transfers between devices, far(): lax.ppermute(value, 'shard', [(i, (i // 2 ^ k) * 2 + i % 2) for i in rang...  47.1 us
    unnamed x232, local copies, waits for them, and re-layouts  34.5 us
    ppermute x28, starting transfers between devices, tp_swap(): return lax.ppermute(value, 'tp', [(i, i ^ mask) for i in range(4)])  30.2 us
    pallas_call x2, Pallas kernels, forward_attention(): pl.pallas_call(forward_attention_kernel, grid_spec=pltpu.PrefetchScalarGr...  29.4 us
    ppermute x29, starting transfers between devices, near(): return lax.ppermute(value, 'shard', [(i, i ^ 1) for i in range(self.count)])  28.5 us
  transfers between devices with their start and end apart: 92, of which 37 were waited for; matrix products, arithmetic and copies ran while one was open for 21% of the time, Pallas kernels for 15%

profile of v2, /device:TPU:0, one launch (start us, length us, event | category | flops | bytes accessed | tf_op | source)
XLA Modules:
  0.0 638.1 jit_solution(10755769744594577337)
XLA Ops:
  98.8 14.6 %attention_forward.2 = (bf16[1024,384]{1,0:T(8,128)(2,1)S(1)}, f32[8,1024]{1,0:T(8,128)S(1)}) custom-call(s32[1]{0:T(128)} %bitcast.1.chip_ref, bf16[1024,512]{1,0:T(8,128)(2,1)S(1)} %copy-done.27, bf16[2048,128]{1,0:T(8,128)(2,1)S(1)} %get-tuple-element.264.k_ref, bf16[128,2048]{1,0:T(8,128)(2,1)S(1)} %copy-done.22), custom_call_target="tpu_custom_call" | custom-call | flops 8999999488 | bytes 4000000 | tf_op jit(solution)/shard_map/attention_forward/pallas_call | solution.py:92
  118.8 14.8 %attention_forward.3 = (bf16[1024,384]{1,0:T(8,128)(2,1)S(1)}, f32[8,1024]{1,0:T(8,128)S(1)}) custom-call(s32[1]{0:T(128)} %bitcast.1.chip_ref, bf16[1024,384]{1,0:T(8,128)(2,1)S(1)} %multiply_convert_fusion.2.q_ref, bf16[2048,128]{1,0:T(8,128)(2,1)S(1)} %get-tuple-element.264.k_ref, bf16[128,2048]{1,0:T(8,128)(2,1)S(1)} %copy-done.22), custom_call_target="tpu_custom_call" | custom-call | flops 8999999488 | bytes 4000000 | tf_op jit(solution)/shard_map/attention_forward/pallas_call | solution.py:92
  168.6 8.4 %collective-permute-done.34.refs_13_ = bf16[192,1152]{1,0:T(8,128)(2,1)S(1)} collective-permute-done((bf16[192,1152]{1,0:T(8,128)(2,1)S(1)}, bf16[192,1152]{1,0:T(8,128)(2,1)S(1)}, u32[]{:S(2)}, u32[]{:S(2)}) %collective-permute-start.34) | collective-permute-done | bytes 442400 | tf_op jit(solution)/shard_map/ppermute | solution.py:592
  181.8 16.6 %collective-permute-done.37.refs_1_ = bf16[192,1152]{1,0:T(8,128)(2,1)S(1)} collective-permute-done((bf16[192,1152]{1,0:T(8,128)(2,1)S(1)}, bf16[192,1152]{1,0:T(8,128)(2,1)S(1)}, u32[]{:S(2)}, u32[]{:S(2)}) %collective-permute-start.37) | collective-permute-done | bytes 442400 | tf_op jit(solution)/shard_map/ppermute | solution.py:587
  207.0 14.2 %gate_up_first.1 = (bf16[2048,1152]{1,0:T(8,128)(2,1)S(1)}, bf16[2048,1152]{1,0:T(8,128)(2,1)}, bf16[2048,1152]{1,0:T(8,128)(2,1)}, bf16[1536,2304]{1,0:T(8,128)(2,1)}) custom-call(s32[8]{0:T(128)S(1)} %stack.35.place_ref, bf16[1024,1536]{1,0:T(8,128)(2,1)S(1)} %pad_maximum_fusion.1.norm_ref, bf16[192,1152]{1,0:T(8,128)(2,1)} %get-tuple-element.272.refs_0_, ...), custom_call_target="tpu_custom_call" | custom-call | flops 7247757312 | bytes 24379392 | tf_op jit(solution)/shard_map/gate_up_first/pallas_call | solution.py:426
  234.2 14.5 %gate_up_rest.1 = (bf16[2048,1152]{1,0:T(8,128)(2,1)S(1)}, bf16[2048,1152]{1,0:T(8,128)(2,1)S(1)}, bf16[2048,1152]{1,0:T(8,128)(2,1)S(1)}) custom-call(bf16[1024,1536]{1,0:T(8,128)(2,1)S(1)} %pad_maximum_fusion.2.norm_ref, bf16[1536,2304]{1,0:T(8,128)(2,1)} %get-tuple-element.319.whole_ref.gate_up_ref, ...), custom_call_target="tpu_custom_call", output_to_operand_aliasing={{0}: (2, {}), {1}: (3, {}), {2}: (4, {})} | custom-call | flops 7247757312 | bytes 17301504 | tf_op jit(solution)/shard_map/gate_up_rest/pallas_call | solution.py:462
  250.8 15.2 %convolution_convert_fusion.2.whole = bf16[1536,1152]{1,0:T(8,128)(2,1)S(1)} fusion(bf16[2048,1536]{1,0:T(8,128)(2,1)} %pad_maximum_fusion.cot_ref, bf16[2048,1152]{1,0:T(8,128)(2,1)} %copy-done.54), kind=kOutput, calls=%fused_computation.2 | convolution fusion | flops 7249526784 | bytes 14548992 | tf_op jit(solution)/shard_map/dot_general | solution.py:26
  273.3 16.4 %product_gradient.1 = (bf16[2048,1152]{1,0:T(8,128)(2,1)S(1)}, bf16[2048,1152]{1,0:T(8,128)(2,1)S(1)}, bf16[1536,1152]{1,0:T(8,128)(2,1)S(1)}) custom-call(s32[8]{0:T(128)S(1)} %stack.35.place_ref, bf16[2048,1536]{1,0:T(8,128)(2,1)} %pad_maximum_fusion.cot_ref, bf16[2048,1152]{1,0:T(8,128)(2,1)S(1)} %copy-done.57, bf16[2048,1152]{1,0:T(8,128)(2,1)} %copy-done.59, ...), custom_call_target="tpu_custom_call" | custom-call | flops 7247757312 | bytes 32243712 | tf_op jit(solution)/shard_map/product_gradient/pallas_call | solution.py:508
  290.1 13.3 %feed_back.2 = (bf16[512,1536]{1,0:T(8,128)(2,1)S(1)}, bf16[512,1536]{1,0:T(8,128)(2,1)S(1)}) custom-call(bf16[2048,1152]{1,0:T(8,128)(2,1)S(1)} %get-tuple-element.369.dgate_ref, bf16[2048,1152]{1,0:T(8,128)(2,1)S(1)} %get-tuple-element.370.dup_ref, bf16[1536,2304]{1,0:T(8,128)(2,1)} %get-tuple-element.319.whole_ref.gate_up_ref), custom_call_target="tpu_custom_call" | custom-call | flops 7247757312 | bytes 14942208 | tf_op jit(solution)/shard_map/feed_back/pallas_call | solution.py:553
  312.7 19.3 %collective-permute-done.51.came = bf16[384,1152]{1,0:T(8,128)(2,1)S(1)} collective-permute-done((bf16[384,1152]{1,0:T(8,128)(2,1)S(1)}, bf16[384,1152]{1,0:T(8,128)(2,1)S(1)}, u32[]{:S(2)}, u32[]{:S(2)}) %collective-permute-start.51) | collective-permute-done | bytes 884768 | tf_op jit(solution)/shard_map/ppermute | solution.py:592
  332.4 10.7 %convolution_convert_fusion.1.whole = bf16[1536,1152]{1,0:T(8,128)(2,1)S(1)} fusion(bf16[2048,1536]{1,0:T(8,128)(2,1)} %copy-done.94, bf16[2048,1152]{1,0:T(8,128)(2,1)S(1)} %get-tuple-element.369.dgate_ref), kind=kOutput, calls=%fused_computation.1 | convolution fusion | flops 7249526784 | bytes 14548992 | tf_op jit(solution)/shard_map/dot_general | solution.py:26
  345.0 7.8 %collective-permute-done.53 = bf16[192,1152]{1,0:T(8,128)(2,1)S(1)} collective-permute-done((bf16[192,1152]{1,0:T(8,128)(2,1)S(1)}, bf16[192,1152]{1,0:T(8,128)(2,1)S(1)}, u32[]{:S(2)}, u32[]{:S(2)}) %collective-permute-start.53) | collective-permute-done | bytes 442400 | tf_op jit(solution)/shard_map/ppermute | solution.py:587
  362.0 10.2 %collective-permute-done.57 = bf16[192,1152]{1,0:T(8,128)(2,1)S(1)} collective-permute-done((bf16[192,1152]{1,0:T(8,128)(2,1)S(1)}, bf16[192,1152]{1,0:T(8,128)(2,1)S(1)}, u32[]{:S(2)}, u32[]{:S(2)}) %collective-permute-start.57) | collective-permute-done | bytes 442400 | tf_op jit(solution)/shard_map/ppermute | solution.py:587
  372.2 9.1 %collective-permute-done.58 = bf16[192,1152]{1,0:T(8,128)(2,1)S(1)} collective-permute-done((bf16[192,1152]{1,0:T(8,128)(2,1)S(1)}, bf16[192,1152]{1,0:T(8,128)(2,1)S(1)}, u32[]{:S(2)}, u32[]{:S(2)}) %collective-permute-start.58) | collective-permute-done | bytes 442400 | tf_op jit(solution)/shard_map/ppermute | solution.py:587
  382.3 12.3 %feed_back.3 = (bf16[512,1536]{1,0:T(8,128)(2,1)S(1)}, bf16[512,1536]{1,0:T(8,128)(2,1)S(1)}) custom-call(bf16[2048,1152]{1,0:T(8,128)(2,1)S(1)} %get-tuple-element.369.dgate_ref, bf16[2048,1152]{1,0:T(8,128)(2,1)S(1)} %get-tuple-element.370.dup_ref, bf16[1536,2304]{1,0:T(8,128)(2,1)} %get-tuple-element.319.whole_ref.gate_up_ref), custom_call_target="tpu_custom_call" | custom-call | flops 7247757312 | bytes 14942208 | tf_op jit(solution)/shard_map/feed_back/pallas_call | solution.py:553
  395.7 11.0 %convolution_convert_fusion.whole = bf16[1536,1152]{1,0:T(8,128)(2,1)S(1)} fusion(bf16[2048,1536]{1,0:T(8,128)(2,1)} %copy-done.94, bf16[2048,1152]{1,0:T(8,128)(2,1)S(1)} %get-tuple-element.370.dup_ref), kind=kOutput, calls=%fused_computation | convolution fusion | flops 7249526784 | bytes 14548992 | tf_op jit(solution)/shard_map/dot_general | solution.py:26
  440.5 15.2 %collective-permute-done.64 = bf16[192,1152]{1,0:T(8,128)(2,1)S(1)} collective-permute-done((bf16[192,1152]{1,0:T(8,128)(2,1)S(1)}, bf16[192,1152]{1,0:T(8,128)(2,1)S(1)}, u32[]{:S(2)}, u32[]{:S(2)}) %collective-permute-start.64) | collective-permute-done | bytes 442400 | tf_op jit(solution)/shard_map/ppermute | solution.py:587
  458.7 10.8 %attention_backward.2 = (bf16[1024,384]{1,0:T(8,128)(2,1)S(1)}, f32[2048,128]{1,0:T(8,128)S(1)}, f32[2048,128]{1,0:T(8,128)S(1)}) custom-call(s32[1]{0:T(128)} %bitcast.1.chip_ref, bf16[1024,384]{1,0:T(8,128)(2,1)S(1)} %copy-done.64, bf16[1024,384]{1,0:T(8,128)(2,1)S(1)} %maximum_select_fusion.2.g_ref, bf16[1024,384]{1,0:T(8,128)(2,1)S(1)} %get-tuple-element.286.o_ref, ...), custom_call_target="tpu_custom_call" | custom-call | flops 17999998976 | bytes 8000000 | tf_op jit(solution)/shard_map/attention_backward/pallas_call | solution.py:196
  484.7 8.0 %collective-permute-done.68 = bf16[192,1152]{1,0:T(8,128)(2,1)S(1)} collective-permute-done((bf16[192,1152]{1,0:T(8,128)(2,1)S(1)}, bf16[192,1152]{1,0:T(8,128)(2,1)S(1)}, u32[]{:S(2)}, u32[]{:S(2)}) %collective-permute-start.68) | collective-permute-done | bytes 442400 | tf_op jit(solution)/shard_map/ppermute | solution.py:587
  496.0 10.7 %attention_backward.3 = (bf16[1024,384]{1,0:T(8,128)(2,1)S(1)}, f32[2048,128]{1,0:T(8,128)S(1)}, f32[2048,128]{1,0:T(8,128)S(1)}) custom-call(s32[1]{0:T(128)} %bitcast.1.chip_ref, bf16[1024,512]{1,0:T(8,128)(2,1)S(1)} %copy-done.28, bf16[1024,384]{1,0:T(8,128)(2,1)S(1)} %maximum_select_fusion.1.g_ref, bf16[1024,384]{1,0:T(8,128)(2,1)S(1)} %copy-done.5, ...), custom_call_target="tpu_custom_call" | custom-call | flops 17999998976 | bytes 8000000 | tf_op jit(solution)/shard_map/attention_backward/pallas_call | solution.py:196
  507.0 11.2 %collective-permute-start.71 = (bf16[1536,384]{1,0:T(8,128)(2,1)S(1)}, bf16[1536,384]{1,0:T(8,128)(2,1)S(1)}, u32[]{:S(2)}, u32[]{:S(2)}) collective-permute-start(bf16[1536,384]{1,0:T(8,128)(2,1)S(1)} %convolution_convert_fusion.7), channel_id=1, source_target_pairs={{0,2},{1,3},{2,0},{3,1},{4,6},{5,7},{6,4},{7,5},{8,10},{9,11},{10,... | collective-permute-start | bytes 3538952 | tf_op jit(solution)/shard_map/ppermute | solution.py:599
  526.6 14.5 %collective-permute-done.70 = bf16[192,1152]{1,0:T(8,128)(2,1)S(1)} collective-permute-done((bf16[192,1152]{1,0:T(8,128)(2,1)S(1)}, bf16[192,1152]{1,0:T(8,128)(2,1)S(1)}, u32[]{:S(2)}, u32[]{:S(2)}) %collective-permute-start.70) | collective-permute-done | bytes 442400 | tf_op jit(solution)/shard_map/ppermute | solution.py:587
  561.9 8.3 %collective-permute-done.74.came = bf16[768,384]{1,0:T(8,128)(2,1)S(1)} collective-permute-done((bf16[768,384]{1,0:T(8,128)(2,1)S(1)}, bf16[768,384]{1,0:T(8,128)(2,1)S(1)}, u32[]{:S(2)}, u32[]{:S(2)}) %collective-permute-start.74) | collective-permute-done | bytes 589856 | tf_op jit(solution)/shard_map/ppermute | solution.py:592
  593.2 8.5 %collective-permute-done.81 = bf16[192,384]{1,0:T(8,128)(2,1)S(1)} collective-permute-done((bf16[192,384]{1,0:T(8,128)(2,1)S(1)}, bf16[192,384]{1,0:T(8,128)(2,1)S(1)}, u32[]{:S(2)}, u32[]{:S(2)}) %collective-permute-start.81) | collective-permute-done | bytes 147488 | tf_op jit(solution)/shard_map/ppermute | solution.py:587
  (520 shorter events, 339.6 us)
Async XLA Ops:
  75.9 40.1 %collective-permute-start.22 = (bf16[768,384]{1,0:T(8,128)(2,1)}, bf16[768,384]{1,0:T(8,128)(2,1)}, u32[]{:S(2)}, u32[]{:S(2)}) collective-permute-start(bf16[768,384]{1,0:T(8,128)(2,1)} %pack_pieces.6), channel_id=1, source_target_pairs={{0,2},{1,3},{2,0},{3,1},{4,6},{5,7},{6,4},{7,5},{8,10},{9,11},{10,... | collective-permute-start | bytes 1769480 | tf_op jit(solution)/shard_map/ppermute | solution.py:599
  87.8 28.2 %collective-permute-start.23 = (bf16[192,1152]{1,0:T(8,128)(2,1)}, bf16[192,1152]{1,0:T(8,128)(2,1)}, u32[]{:S(2)}, u32[]{:S(2)}) collective-permute-start(bf16[192,1152]{1,0:T(8,128)(2,1)} %get-tuple-element.272.refs_0_), channel_id=1, source_target_pairs={{0,24},{4,28},{8,16},{12,20},{16,8},{20,12},{24,0},{28,4},{1,25},{... | collective-permute-start | bytes 1327112 | tf_op jit(solution)/shard_map/ppermute | solution.py:587
  89.4 26.5 %collective-permute-start.24 = (bf16[192,1152]{1,0:T(8,128)(2,1)}, bf16[192,1152]{1,0:T(8,128)(2,1)}, u32[]{:S(2)}, u32[]{:S(2)}) collective-permute-start(bf16[192,1152]{1,0:T(8,128)(2,1)} %get-tuple-element.272.refs_0_), channel_id=1, source_target_pairs={{0,4},{4,0},{8,12},{12,8},{16,20},{20,16},{24,28},{28,24},{1,5},{5... | collective-permute-start | bytes 1327112 | tf_op jit(solution)/shard_map/ppermute | solution.py:592
  92.5 23.5 %collective-permute-start.25 = (bf16[192,1152]{1,0:T(8,128)(2,1)}, bf16[192,1152]{1,0:T(8,128)(2,1)S(1)}, u32[]{:S(2)}, u32[]{:S(2)}) collective-permute-start(bf16[192,1152]{1,0:T(8,128)(2,1)} %copy-done.32), channel_id=1, source_target_pairs={{0,4},{4,0},{8,12},{12,8},{16,20},{20,16},{24,28},{28,24},{1,5},{5... | collective-permute-start | bytes 1327112 | tf_op jit(solution)/shard_map/ppermute | solution.py:592
  94.0 43.7 %collective-permute-start.26 = (bf16[768,384]{1,0:T(8,128)(2,1)}, bf16[768,384]{1,0:T(8,128)(2,1)S(1)}, u32[]{:S(2)}, u32[]{:S(2)}) collective-permute-start(bf16[768,384]{1,0:T(8,128)(2,1)} %copy-done.20), channel_id=1, source_target_pairs={{0,2},{1,3},{2,0},{3,1},{4,6},{5,7},{6,4},{7,5},{8,10},{9,11},{10,... | collective-permute-start | bytes 1769480 | tf_op jit(solution)/shard_map/ppermute | solution.py:599
  177.1 23.9 %collective-permute-start.36 = (bf16[288,1536]{1,0:T(8,128)(2,1)S(1)}, bf16[288,1536]{1,0:T(8,128)(2,1)S(1)}, u32[]{:S(2)}, u32[]{:S(2)}) collective-permute-start(bf16[288,1536]{1,0:T(8,128)(2,1)S(1)} %slice.79), channel_id=1, source_target_pairs={{0,2},{1,3},{2,0},{3,1},{4,6},{5,7},{6,4},{7,5},{8,10},{9,11},{10,... | collective-permute-start | bytes 2654216 | tf_op jit(solution)/shard_map/ppermute | solution.py:599
  178.0 22.7 %collective-permute-start.38 = (bf16[192,1152]{1,0:T(8,128)(2,1)S(1)}, bf16[192,1152]{1,0:T(8,128)(2,1)S(1)}, u32[]{:S(2)}, u32[]{:S(2)}) collective-permute-start(bf16[192,1152]{1,0:T(8,128)(2,1)S(1)} %convert_bitcast_fusion.refs_0_), channel_id=1, source_target_pairs={{0,16},{4,20},{8,24},{12,28},{16,0},{20,4},{24,8},{28,12},{1,17},{... | collective-permute-start | bytes 1327112 | tf_op jit(solution)/shard_map/ppermute | solution.py:587
  201.0 25.4 %collective-permute-start.42 = (bf16[288,1536]{1,0:T(8,128)(2,1)S(1)}, bf16[288,1536]{1,0:T(8,128)(2,1)S(1)}, u32[]{:S(2)}, u32[]{:S(2)}) collective-permute-start(bf16[288,1536]{1,0:T(8,128)(2,1)S(1)} %collective-permute-done.36), channel_id=1, source_target_pairs={{0,1},{1,0},{2,3},{3,2},{4,5},{5,4},{6,7},{7,6},{8,9},{9,8},{10,11... | collective-permute-start | bytes 2654216 | tf_op jit(solution)/shard_map/ppermute | solution.py:599
  201.1 22.4 %collective-permute-start.41 = (bf16[224,1536]{1,0:T(8,128)(2,1)S(1)}, bf16[224,1536]{1,0:T(8,128)(2,1)S(1)}, u32[]{:S(2)}, u32[]{:S(2)}) collective-permute-start(bf16[224,1536]{1,0:T(8,128)(2,1)S(1)} %slice.80), channel_id=1, source_target_pairs={{0,2},{1,3},{2,0},{3,1},{4,6},{5,7},{6,4},{7,5},{8,10},{9,11},{10,... | collective-permute-start | bytes 2064392 | tf_op jit(solution)/shard_map/ppermute | solution.py:599
  226.5 40.3 %collective-permute-start.47 = (bf16[192,1152]{1,0:T(8,128)(2,1)S(1)}, bf16[192,1152]{1,0:T(8,128)(2,1)S(1)}, u32[]{:S(2)}, u32[]{:S(2)}) collective-permute-start(bf16[192,1152]{1,0:T(8,128)(2,1)S(1)} %collective-permute-done.38.refs_2_), channel_id=1, source_target_pairs={{0,4},{4,0},{8,12},{12,8},{16,20},{20,16},{24,28},{28,24},{1,5},{5... | collective-permute-start | bytes 1327112 | tf_op jit(solution)/shard_map/ppermute | solution.py:592
  227.1 40.6 %collective-permute-start.48 = (bf16[192,1152]{1,0:T(8,128)(2,1)S(1)}, bf16[192,1152]{1,0:T(8,128)(2,1)S(1)}, u32[]{:S(2)}, u32[]{:S(2)}) collective-permute-start(bf16[192,1152]{1,0:T(8,128)(2,1)S(1)} %collective-permute-done.43.refs_3_), channel_id=1, source_target_pairs={{0,4},{4,0},{8,12},{12,8},{16,20},{20,16},{24,28},{28,24},{1,5},{5... | collective-permute-start | bytes 1327112 | tf_op jit(solution)/shard_map/ppermute | solution.py:592
  352.8 28.5 %collective-permute-start.56 = (bf16[384,1152]{1,0:T(8,128)(2,1)S(1)}, bf16[384,1152]{1,0:T(8,128)(2,1)S(1)}, u32[]{:S(2)}, u32[]{:S(2)}) collective-permute-start(bf16[384,1152]{1,0:T(8,128)(2,1)S(1)} %get-tuple-element.365), channel_id=1, source_target_pairs={{0,4},{4,0},{8,12},{12,8},{16,20},{20,16},{24,28},{28,24},{1,5},{5... | collective-permute-start | bytes 2654216 | tf_op jit(solution)/shard_map/ppermute | solution.py:592
  354.4 27.0 %collective-permute-start.55 = (bf16[224,1536]{1,0:T(8,128)(2,1)S(1)}, bf16[224,1536]{1,0:T(8,128)(2,1)S(1)}, u32[]{:S(2)}, u32[]{:S(2)}) collective-permute-start(bf16[224,1536]{1,0:T(8,128)(2,1)S(1)} %add_convert_fusion.5), channel_id=1, source_target_pairs={{0,2},{1,3},{2,0},{3,1},{4,6},{5,7},{6,4},{7,5},{8,10},{9,11},{10,... | collective-permute-start | bytes 2064392 | tf_op jit(solution)/shard_map/ppermute | solution.py:599
  394.6 22.3 %collective-permute-start.59 = (bf16[512,1536]{1,0:T(8,128)(2,1)S(1)}, bf16[512,1536]{1,0:T(8,128)(2,1)S(1)}, u32[]{:S(2)}, u32[]{:S(2)}) collective-permute-start(bf16[512,1536]{1,0:T(8,128)(2,1)S(1)} %get-tuple-element.372), channel_id=1, source_target_pairs={{0,1},{1,0},{2,3},{3,2},{4,5},{5,4},{6,7},{7,6},{8,9},{9,8},{10,11... | collective-permute-start | bytes 4718600 | tf_op jit(solution)/shard_map/ppermute | solution.py:599
  425.0 30.7 %collective-permute-start.63 = (bf16[384,1152]{1,0:T(8,128)(2,1)}, bf16[384,1152]{1,0:T(8,128)(2,1)S(1)}, u32[]{:S(2)}, u32[]{:S(2)}) collective-permute-start(bf16[384,1152]{1,0:T(8,128)(2,1)} %copy-done.31), channel_id=1, source_target_pairs={{0,4},{4,0},{8,12},{12,8},{16,20},{20,16},{24,28},{28,24},{1,5},{5... | collective-permute-start | bytes 2654216 | tf_op jit(solution)/shard_map/ppermute | solution.py:592
  433.0 22.7 %collective-permute-start.64 = (bf16[192,1152]{1,0:T(8,128)(2,1)S(1)}, bf16[192,1152]{1,0:T(8,128)(2,1)S(1)}, u32[]{:S(2)}, u32[]{:S(2)}) collective-permute-start(bf16[192,1152]{1,0:T(8,128)(2,1)S(1)} %copy-done.47), channel_id=1, source_target_pairs={{0,16},{4,20},{8,24},{12,28},{16,0},{20,4},{24,8},{28,12},{1,17},{... | collective-permute-start | bytes 1327112 | tf_op jit(solution)/shard_map/ppermute | solution.py:587
  455.7 37.0 %collective-permute-start.65 = (bf16[1536,384]{1,0:T(8,128)(2,1)S(1)}, bf16[1536,384]{1,0:T(8,128)(2,1)S(1)}, u32[]{:S(2)}, u32[]{:S(2)}) collective-permute-start(bf16[1536,384]{1,0:T(8,128)(2,1)S(1)} %fusion.12), channel_id=1, source_target_pairs={{0,2},{1,3},{2,0},{3,1},{4,6},{5,7},{6,4},{7,5},{8,10},{9,11},{10,... | collective-permute-start | bytes 3538952 | tf_op jit(solution)/shard_map/ppermute | solution.py:599
  457.2 35.6 %collective-permute-start.66 = (bf16[384,1152]{1,0:T(8,128)(2,1)S(1)}, bf16[384,1152]{1,0:T(8,128)(2,1)S(1)}, u32[]{:S(2)}, u32[]{:S(2)}) collective-permute-start(bf16[384,1152]{1,0:T(8,128)(2,1)S(1)} %copy-done.30), channel_id=1, source_target_pairs={{0,4},{4,0},{8,12},{12,8},{16,20},{20,16},{24,28},{28,24},{1,5},{5... | collective-permute-start | bytes 2654216 | tf_op jit(solution)/shard_map/ppermute | solution.py:592
  507.0 43.7 %collective-permute-start.71 = (bf16[1536,384]{1,0:T(8,128)(2,1)S(1)}, bf16[1536,384]{1,0:T(8,128)(2,1)S(1)}, u32[]{:S(2)}, u32[]{:S(2)}) collective-permute-start(bf16[1536,384]{1,0:T(8,128)(2,1)S(1)} %convolution_convert_fusion.7), channel_id=1, source_target_pairs={{0,2},{1,3},{2,0},{3,1},{4,6},{5,7},{6,4},{7,5},{8,10},{9,11},{10,... | collective-permute-start | bytes 3538952 | tf_op jit(solution)/shard_map/ppermute | solution.py:599
  518.2 22.9 %collective-permute-start.69 = (bf16[768,384]{1,0:T(8,128)(2,1)S(1)}, bf16[768,384]{1,0:T(8,128)(2,1)S(1)}, u32[]{:S(2)}, u32[]{:S(2)}) collective-permute-start(bf16[768,384]{1,0:T(8,128)(2,1)S(1)} %get-tuple-element.405), channel_id=1, source_target_pairs={{0,4},{4,0},{8,12},{12,8},{16,20},{20,16},{24,28},{28,24},{1,5},{5... | collective-permute-start | bytes 1769480 | tf_op jit(solution)/shard_map/ppermute | solution.py:592
  518.8 22.3 %collective-permute-start.70 = (bf16[192,1152]{1,0:T(8,128)(2,1)S(1)}, bf16[192,1152]{1,0:T(8,128)(2,1)S(1)}, u32[]{:S(2)}, u32[]{:S(2)}) collective-permute-start(bf16[192,1152]{1,0:T(8,128)(2,1)S(1)} %get-tuple-element.409), channel_id=1, source_target_pairs={{0,16},{4,20},{8,24},{12,28},{16,0},{20,4},{24,8},{28,12},{1,17},{... | collective-permute-start | bytes 1327112 | tf_op jit(solution)/shard_map/ppermute | solution.py:587
  520.9 29.7 %collective-permute-start.73 = (bf16[1024,128]{1,0:T(8,128)(2,1)S(1)}, bf16[1024,128]{1,0:T(8,128)(2,1)S(1)}, u32[]{:S(2)}, u32[]{:S(2)}) collective-permute-start(bf16[1024,128]{1,0:T(8,128)(2,1)S(1)} %slice.150), channel_id=1, source_target_pairs={{2,0},{3,1},{6,4},{7,5},{10,8},{11,9},{14,12},{15,13},{18,16},{19,... | collective-permute-start | bytes 786440 | tf_op jit(solution)/shard_map/ppermute | solution.py:894
  523.7 108.4 %collective-permute-start.78 = (bf16[224,1536]{1,0:T(8,128)(2,1)S(1)}, bf16[224,1536]{1,0:T(8,128)(2,1)}, u32[]{:S(2)}, u32[]{:S(2)}) collective-permute-start(bf16[224,1536]{1,0:T(8,128)(2,1)S(1)} %slice.94), channel_id=1, source_target_pairs={{0,2},{1,3},{2,0},{3,1},{4,6},{5,7},{6,4},{7,5},{8,10},{9,11},{10,... | collective-permute-start | bytes 2064392 | tf_op jit(solution)/shard_map/ppermute | solution.py:599
  572.4 30.2 %collective-permute-start.79 = (bf16[512,1536]{1,0:T(8,128)(2,1)}, bf16[512,1536]{1,0:T(8,128)(2,1)}, u32[]{:S(2)}, u32[]{:S(2)}) collective-permute-start(bf16[512,1536]{1,0:T(8,128)(2,1)} %add_convert_fusion), channel_id=1, source_target_pairs={{0,1},{1,0},{2,3},{3,2},{4,5},{5,4},{6,7},{7,6},{8,9},{9,8},{10,11... | collective-permute-start | bytes 4718600 | tf_op jit(solution)/shard_map/ppermute | solution.py:599
  (181 other events, 1932.5 us)

commit v3 on v2

v3 whole, which is shorter than its diff:
```python
import functools

import jax
import jax.numpy as jnp
from jax import lax
from jax.experimental import pallas as pl
from jax.experimental.pallas import tpu as pltpu
from jax.sharding import PartitionSpec as P

HD = 128
WINDOW = 1024
QB = 256
GROUP = 3
EPS = 1e-06
LOG2E = 1.4426950408889634
LN2 = 0.6931471805599453
NEG = -1e30
LARGE = 1 << 20
SMALL = pl.CostEstimate(flops=0, transcendentals=0, bytes_accessed=0)
BF = jnp.bfloat16
F32 = jnp.float32
NT = (((1,), (1,)), ((), ()))
TN = (((0,), (0,)), ((), ()))
NN = (((1,), (0,)), ((), ()))


def dot(a, b, dims=NN):
    return lax.dot_general(a, b, dims, preferred_element_type=F32)


def after(value, *others):
    return lax.optimization_barrier((value, *others))[0]


def kernel_call(*args, **kwargs):
    call = pl.pallas_call(*args, **kwargs)

    def run(*operands):
        return call(
            *(
                pltpu.with_memory_space_constraint(x, pltpu.HBM) if x.size > LARGE else x
                for x in operands
            )
        )

    return run


def forward_attention_kernel(chip_ref, q_ref, k_ref, vt_ref, o_ref, lse_ref):
    block = pl.program_id(0)
    chunks = WINDOW // QB
    key_row = lax.broadcasted_iota(jnp.int32, (QB, QB), 0)
    query_col = lax.broadcasted_iota(jnp.int32, (QB, QB), 1)

    def rows_of(chunk):
        return pl.ds(pl.multiple_of((block + chunk) * QB, QB), QB)

    def finish(head, top, total, mixed):
        cols = slice(head * HD, (head + 1) * HD)
        o_ref[:, cols] = jnp.transpose(mixed / total).astype(BF)
        lse_ref[head : head + 1, :] = top + jnp.log(total) * LOG2E

    def attend(first):
        for head in range(GROUP):
            query = q_ref[:, head * HD : (head + 1) * HD]
            scores = {}
            for chunk in range(first, chunks + 1):
                scores[chunk] = dot(k_ref[rows_of(chunk), :], query, NT)
                if chunk == 0:
                    scores[chunk] = jnp.where(key_row > query_col, scores[chunk], NEG)
                if chunk == chunks:
                    scores[chunk] = jnp.where(key_row <= query_col, scores[chunk], NEG)
            top = functools.reduce(jnp.maximum, scores.values())
            top = jnp.max(top, axis=0, keepdims=True)
            total = jnp.zeros((1, QB), F32)
            mixed = jnp.zeros((HD, QB), F32)
            for chunk, part in scores.items():
                probs = jnp.exp2(part - top)
                total = total + jnp.sum(probs, axis=0, keepdims=True)
                mixed = mixed + dot(vt_ref[:, rows_of(chunk)], probs.astype(BF))
            finish(head, top, total, mixed)

    pl.when(chip_ref[0] != 0)(functools.partial(attend, 0))
    for at in range(chunks):
        pl.when((chip_ref[0] == 0) & (block == at))(functools.partial(attend, chunks - at))


def forward_attention(chip, query, keys, values_t):
    rows = query.shape[0]
    width = GROUP * HD
    return kernel_call(
        forward_attention_kernel,
        grid_spec=pltpu.PrefetchScalarGridSpec(
            num_scalar_prefetch=1,
            grid=(rows // QB,),
            in_specs=[
                pl.BlockSpec((QB, width), lambda b, s: (b, 0)),
                pl.BlockSpec((2 * rows, HD), lambda b, s: (0, 0)),
                pl.BlockSpec((HD, 2 * rows), lambda b, s: (0, 0)),
            ],
            out_specs=[
                pl.BlockSpec((QB, width), lambda b, s: (b, 0)),
                pl.BlockSpec((8, QB), lambda b, s: (0, b)),
            ],
        ),
        out_shape=(
            jax.ShapeDtypeStruct((rows, width), BF),
            jax.ShapeDtypeStruct((8, rows), F32),
        ),
        compiler_params=pltpu.CompilerParams(vmem_limit_bytes=40 << 20),
        cost_estimate=SMALL,
        name="attention_forward",
    )(chip, query, keys, values_t)


def backward_attention_kernel(
    chip_ref, q_ref, g_ref, o_ref, lse_ref, k_ref, kt_ref, v_ref, dq_ref, dk_ref, dv_ref
):
    block = pl.program_id(0)
    chunks = WINDOW // QB
    key_row = lax.broadcasted_iota(jnp.int32, (QB, QB), 0)
    query_col = lax.broadcasted_iota(jnp.int32, (QB, QB), 1)

    @pl.when(block == 0)
    def _():
        dk_ref[...] = jnp.zeros_like(dk_ref)
        dv_ref[...] = jnp.zeros_like(dv_ref)

    def rows_of(chunk):
        return pl.ds(pl.multiple_of((block + chunk) * QB, QB), QB)

    deltas = []
    for head in range(GROUP):
        cols = slice(head * HD, (head + 1) * HD)
        both = g_ref[:, cols].astype(F32) * o_ref[:, cols].astype(F32)
        deltas.append(jnp.sum(jnp.transpose(both), axis=0, keepdims=True))

    def one_chunk(chunk, keep, totals):
        rows = rows_of(chunk)
        keys = k_ref[rows, :]
        values = v_ref[rows, :]
        keys_t = kt_ref[:, rows]
        grad_keys = jnp.zeros((QB, HD), F32)
        grad_values = jnp.zeros((QB, HD), F32)
        new = []
        for head in range(GROUP):
            cols = slice(head * HD, (head + 1) * HD)
            query = q_ref[:, cols]
            grad = g_ref[:, cols]
            probs = jnp.exp2(dot(keys, query, NT) - lse_ref[head : head + 1, :])
            if keep is not None:
                probs = jnp.where(keep, probs, 0.0)
            grad_scores = (probs * (dot(values, grad, NT) - deltas[head])).astype(BF)
            grad_values = grad_values + dot(probs.astype(BF), grad)
            grad_keys = grad_keys + dot(grad_scores, query)
            new.append(totals[head] + dot(keys_t, grad_scores))
        dk_ref[rows, :] += grad_keys
        dv_ref[rows, :] += grad_values
        return tuple(new)

    def finish(totals):
        for head in range(GROUP):
            cols = slice(head * HD, (head + 1) * HD)
            dq_ref[:, cols] = (jnp.transpose(totals[head]) * HD ** (-0.5)).astype(BF)

    zeros = tuple(jnp.zeros((HD, QB), F32) for _ in range(GROUP))

    @pl.when(chip_ref[0] != 0)
    def _():
        totals = zeros
        for chunk in range(chunks + 1):
            keep = None
            if chunk == 0:
                keep = key_row > query_col
            if chunk == chunks:
                keep = key_row <= query_col
            totals = one_chunk(chunk, keep, totals)
        finish(totals)

    @pl.when(chip_ref[0] == 0)
    def _():
        def step(chunk, totals):
            return one_chunk(chunk, (key_row <= query_col) | (chunk < chunks), totals)

        finish(lax.fori_loop(chunks - block, chunks + 1, step, zeros))


def backward_attention(chip, query, grad, mixed, lse, keys, keys_t, values):
    rows = query.shape[0]
    width = GROUP * HD
    wide = pl.BlockSpec((QB, width), lambda b, s: (b, 0))
    whole = pl.BlockSpec((2 * rows, HD), lambda b, s: (0, 0))
    return kernel_call(
        backward_attention_kernel,
        grid_spec=pltpu.PrefetchScalarGridSpec(
            num_scalar_prefetch=1,
            grid=(rows // QB,),
            in_specs=[
                wide,
                wide,
                wide,
                pl.BlockSpec((8, QB), lambda b, s: (0, b)),
                whole,
                pl.BlockSpec((HD, 2 * rows), lambda b, s: (0, 0)),
                whole,
            ],
            out_specs=[wide, whole, whole],
        ),
        out_shape=(
            jax.ShapeDtypeStruct((rows, width), BF),
            jax.ShapeDtypeStruct((2 * rows, HD), F32),
            jax.ShapeDtypeStruct((2 * rows, HD), F32),
        ),
        compiler_params=pltpu.CompilerParams(vmem_limit_bytes=40 << 20),
        cost_estimate=SMALL,
        name="attention_backward",
    )(chip, query, grad, mixed, lse, keys, keys_t, values)


def pack_kernel(*refs):
    packed = refs[-1]
    depth, width = refs[0].shape[0], packed.shape[1]
    for i, piece in enumerate(refs[:-1]):
        packed[pl.ds(i * depth, depth), :] = piece[:, :width]


def pack(pieces, width):
    depth = pieces[0].shape[0]
    rows = depth * len(pieces)
    return kernel_call(
        pack_kernel,
        grid=(1,),
        in_specs=[pl.BlockSpec(piece.shape, lambda i: (0, 0)) for piece in pieces],
        out_specs=pl.BlockSpec((rows, width), lambda i: (0, 0)),
        out_shape=jax.ShapeDtypeStruct((rows, width), BF),
        compiler_params=pltpu.CompilerParams(vmem_limit_bytes=16 << 20),
        cost_estimate=SMALL,
        name="pack_pieces",
    )(*pieces)


def unpack_kernel(half, place_ref, far, near, whole):
    depth = far.shape[0] // half
    for i in range(half):
        rows = pl.ds(i * depth, depth)
        whole[pl.ds(pl.multiple_of(place_ref[i] * depth, depth), depth), :] = far[rows, :]
        whole[pl.ds(pl.multiple_of(place_ref[half + i] * depth, depth), depth), :] = near[rows, :]


def unpack(places, far, near, half):
    rows, width = far.shape
    packed = pl.BlockSpec((rows, width), lambda i, s: (0, 0))
    return kernel_call(
        functools.partial(unpack_kernel, half),
        grid_spec=pltpu.PrefetchScalarGridSpec(
            num_scalar_prefetch=1,
            grid=(1,),
            in_specs=[packed, packed],
            out_specs=pl.BlockSpec((2 * rows, width), lambda i, s: (0, 0)),
        ),
        out_shape=jax.ShapeDtypeStruct((2 * rows, width), BF),
        compiler_params=pltpu.CompilerParams(vmem_limit_bytes=16 << 20),
        cost_estimate=SMALL,
        name="unpack_pieces",
    )(places, far, near)


def split_kernel(groups, half, place_ref, whole, *refs):
    depth = refs[0].shape[0] // len(groups[0])
    for group, kept, sent in zip(groups, refs[: len(groups)], refs[len(groups) :]):
        for at, i in enumerate(group):
            rows = pl.ds(at * depth, depth)
            kept[rows, :] = whole[pl.ds(pl.multiple_of(place_ref[i] * depth, depth), depth), :]
            sent[rows, :] = whole[
                pl.ds(pl.multiple_of(place_ref[half + i] * depth, depth), depth), :
            ]


def split(places, whole, half, parts=1):
    size = half // parts
    groups = [range(half - (p + 1) * size, half - p * size) for p in range(parts)]
    rows, width = whole.shape[0] // (2 * parts), whole.shape[1]
    out = pl.BlockSpec((rows, width), lambda i, s: (0, 0))
    pieces = kernel_call(
        functools.partial(split_kernel, groups, half),
        grid_spec=pltpu.PrefetchScalarGridSpec(
            num_scalar_prefetch=1,
            grid=(1,),
            in_specs=[pl.BlockSpec(whole.shape, lambda i, s: (0, 0))],
            out_specs=[out] * (2 * parts),
        ),
        out_shape=(jax.ShapeDtypeStruct((rows, width), whole.dtype),) * (2 * parts),
        compiler_params=pltpu.CompilerParams(vmem_limit_bytes=24 << 20),
        cost_estimate=SMALL,
        name="split_pieces",
    )(places, whole)
    return pieces[:parts], pieces[parts:]


def fold_kernel(kept, came, *pieces):
    depth = pieces[0].shape[0]
    for i, piece in enumerate(pieces):
        rows = pl.ds(i * depth, depth)
        piece[...] = (kept[rows, :].astype(F32) + came[rows, :].astype(F32)).astype(BF)


def fold(kept, came, half):
    rows, width = kept.shape
    depth = rows // half
    whole = pl.BlockSpec((rows, width), lambda i: (0, 0))
    return kernel_call(
        fold_kernel,
        grid=(1,),
        in_specs=[whole, whole],
        out_specs=[pl.BlockSpec((depth, width), lambda i: (0, 0))] * half,
        out_shape=(jax.ShapeDtypeStruct((depth, width), BF),) * half,
        compiler_params=pltpu.CompilerParams(vmem_limit_bytes=24 << 20),
        cost_estimate=SMALL,
        name="fold_pieces",
    )(kept, came)


def weight_gradient_kernel(half, slot_ref, near_ref, far_ref, grad_ref, *refs):
    part = half // 2
    rows = near_ref.shape[0]
    depth = refs[0].shape[0] // part
    total = dot(near_ref[...], grad_ref[:rows, :], TN) + dot(far_ref[...], grad_ref[rows:, :], TN)
    total = total.astype(BF)
    count = total.shape[0] // depth
    for at in range(count):
        slot = slot_ref[pl.program_id(0) * count + at]
        k = lax.rem(slot, half)
        target = 2 * (slot // half) + 1 - k // part
        place = pl.ds(pl.multiple_of(lax.rem(k, part) * depth, depth), depth)
        for i, ref in enumerate(refs):

            @pl.when(target == i)
            def _(ref=ref, place=place, at=at):
                ref[place, :] = total[at * depth : (at + 1) * depth, :]


def weight_gradient(slots, near, far, grad):
    half = slots.shape[0] // 2
    rows, width = near.shape
    hidden = grad.shape[1]
    block = 384
    tall = pl.BlockSpec((rows, block), lambda i, s: (0, i))
    out = pl.BlockSpec((width // 4, hidden), lambda i, s: (0, 0))
    pieces = kernel_call(
        functools.partial(weight_gradient_kernel, half),
        grid_spec=pltpu.PrefetchScalarGridSpec(
            num_scalar_prefetch=1,
            grid=(width // block,),
            in_specs=[
                tall,
                tall,
                pl.BlockSpec(grad.shape, lambda i, s: (0, 0), pipeline_mode=pl.Buffered(1)),
            ],
            out_specs=[out] * 4,
        ),
        out_shape=(jax.ShapeDtypeStruct((width // 4, hidden), BF),) * 4,
        compiler_params=pltpu.CompilerParams(vmem_limit_bytes=40 << 20),
        cost_estimate=SMALL,
        name="weight_gradient",
    )(slots, near, far, grad)
    return pieces[:2], pieces[2:]


def gelu_parts(gate):
    square = gate * gate
    t = jnp.tanh(gate * (0.7978845608028654 + 0.035677408136300125 * square))
    half = 0.5 + 0.5 * t
    value = gate * half
    slope = half + 0.5 * gate * (1.0 - t * t) * (0.7978845608028654 + 0.10703222440890037 * square)
    return value, slope


def gate_up_block(norm_ref, whole, product_ref, to_gate_ref, to_up_ref):
    hidden = product_ref.shape[1]
    step = 384
    for start in range(0, hidden, step):
        cols = slice(start, start + step)
        gate = dot(norm_ref[...], whole[:, cols])
        up = dot(norm_ref[...], whole[:, hidden + start : hidden + start + step])
        value, slope = gelu_parts(gate)
        product_ref[:, cols] = (value * up).astype(BF)
        to_gate_ref[:, cols] = (up * slope).astype(BF)
        to_up_ref[:, cols] = value.astype(BF)


def gate_up_kernel(norm_ref, whole_ref, *refs):
    gate_up_block(norm_ref, whole_ref, *refs[-3:])


def apply_gate_up(norm, gate_up, *earlier):
    rows, width = norm.shape
    hidden = gate_up.shape[1] // 2
    block = 256
    steps = rows // block
    skip = steps if earlier else 0
    out = pl.BlockSpec((block, hidden), lambda i: (i + skip, 0))
    return kernel_call(
        gate_up_kernel,
        grid=(steps,),
        in_specs=[
            pl.BlockSpec((block, width), lambda i: (i, 0)),
            pl.BlockSpec(gate_up.shape, lambda i: (0, 0), pipeline_mode=pl.Buffered(1)),
        ]
        + [pl.BlockSpec(memory_space=pl.ANY)] * len(earlier),
        out_specs=[out, out, out],
        out_shape=(jax.ShapeDtypeStruct((2 * rows, hidden), BF),) * 3,
        input_output_aliases={2 + i: i for i in range(len(earlier))},
        compiler_params=pltpu.CompilerParams(vmem_limit_bytes=36 << 20),
        cost_estimate=SMALL,
        name="gate_up_rest" if earlier else "gate_up_first",
    )(norm, gate_up, *earlier)


def product_gradient_kernel(near_ref, far_ref, to_gate_ref, to_up_ref, down_ref, dgate_ref, dup_ref):
    step = 384

    def block(cot_ref):
        for start in range(0, down_ref.shape[1], step):
            cols = slice(start, start + step)
            grad = dot(cot_ref[...], down_ref[:, cols])
            dgate_ref[:, cols] = (grad * to_gate_ref[:, cols].astype(F32)).astype(BF)
            dup_ref[:, cols] = (grad * to_up_ref[:, cols].astype(F32)).astype(BF)

    first = pl.program_id(0) < pl.num_programs(0) // 2
    pl.when(first)(functools.partial(block, near_ref))
    pl.when(jnp.logical_not(first))(functools.partial(block, far_ref))


def product_gradient(near, far, to_gate, to_up, down):
    rows, width = near.shape
    hidden = to_gate.shape[1]
    block = 256
    steps = rows // block
    part = pl.BlockSpec((block, hidden), lambda i: (i, 0))
    return kernel_call(
        product_gradient_kernel,
        grid=(2 * steps,),
        in_specs=[
            pl.BlockSpec((block, width), lambda i: (jnp.minimum(i, steps - 1), 0)),
            pl.BlockSpec((block, width), lambda i: (jnp.maximum(i - steps, 0), 0)),
            part,
            part,
            pl.BlockSpec(down.shape, lambda i: (0, 0), pipeline_mode=pl.Buffered(1)),
        ],
        out_specs=[part, part],
        out_shape=(jax.ShapeDtypeStruct((2 * rows, hidden), BF),) * 2,
        compiler_params=pltpu.CompilerParams(vmem_limit_bytes=32 << 20),
        cost_estimate=SMALL,
        name="product_gradient",
    )(near, far, to_gate, to_up, down)


def down_project_kernel(product_ref, down_ref, *outs):
    for i, out in enumerate(outs):

        @pl.when(pl.program_id(0) // 2 == i)
        def _(out=out):
            out[...] = dot(product_ref[...], down_ref[...], NT).astype(BF)


def down_project(product, down):
    rows, hidden = product.shape
    width = down.shape[0]
    block = rows // 8

    def spec(i):
        return pl.BlockSpec((block, width), lambda at: (jnp.clip(at - 2 * i, 0, 1), 0))

    return kernel_call(
        down_project_kernel,
        grid=(8,),
        in_specs=[
            pl.BlockSpec((block, hidden), lambda at: (at, 0)),
            pl.BlockSpec(down.shape, lambda at: (0, 0), pipeline_mode=pl.Buffered(1)),
        ],
        out_specs=[spec(i) for i in range(4)],
        out_shape=(jax.ShapeDtypeStruct((rows // 4, width), BF),) * 4,
        compiler_params=pltpu.CompilerParams(vmem_limit_bytes=24 << 20),
        cost_estimate=SMALL,
        name="down_project",
    )(product, down)


def feed_back_kernel(dgate_ref, dup_ref, gate_up_ref, kept_ref, sent_ref):
    hidden = dgate_ref.shape[1]
    total = dot(dgate_ref[...], gate_up_ref[:, :hidden], NT)
    total = (total + dot(dup_ref[...], gate_up_ref[:, hidden:], NT)).astype(BF)

    @pl.when(pl.program_id(0) < pl.num_programs(0) // 2)
    def _():
        kept_ref[...] = total

    @pl.when(pl.program_id(0) >= pl.num_programs(0) // 2)
    def _():
        sent_ref[...] = total


def feed_back(first, rows, dgate, dup, gate_up):
    width, hidden = gate_up.shape[0], dgate.shape[1]
    block = 256
    steps = rows // block
    skip = first // block
    part = pl.BlockSpec((block, hidden), lambda i: (i + skip, 0))
    return kernel_call(
        feed_back_kernel,
        grid=(steps,),
        in_specs=[
            part,
            part,
            pl.BlockSpec(gate_up.shape, lambda i: (0, 0), pipeline_mode=pl.Buffered(1)),
        ],
        out_specs=[
            pl.BlockSpec((block, width), lambda i: (jnp.minimum(i, steps // 2 - 1), 0)),
            pl.BlockSpec((block, width), lambda i: (jnp.maximum(i - steps // 2, 0), 0)),
        ],
        out_shape=(jax.ShapeDtypeStruct((rows // 2, width), BF),) * 2,
        compiler_params=pltpu.CompilerParams(vmem_limit_bytes=36 << 20),
        cost_estimate=SMALL,
        name="feed_back",
    )(dgate, dup, gate_up)


class Shards:
    def __init__(self, count):
        self.count = count
        self.half = count // 2
        index = lax.axis_index("shard").astype(jnp.int32)
        hi, lo = index // 2, index % 2
        mine = [(hi ^ k) * 2 + lo for k in range(self.half)]
        partner = [(hi ^ k) * 2 + (1 - lo) for k in range(self.half)]
        self.places = jnp.stack(mine + partner)
        owner = jnp.arange(count, dtype=jnp.int32)
        self.slots = (owner // 2 ^ hi) + self.half * (owner % 2 ^ lo)

    def far(self, value, k):
        return lax.ppermute(
            value, "shard", [(i, ((i // 2) ^ k) * 2 + i % 2) for i in range(self.count)]
        )

    def near(self, value):
        return lax.ppermute(value, "shard", [(i, i ^ 1) for i in range(self.count)])


def tp_swap(value, mask):
    return lax.ppermute(value, "tp", [(i, i ^ mask) for i in range(4)])


def local(count, tokens, w_query, w_keyval, w_out, w_gate, w_up, w_down, gain_attn, gain_mlp, cotangent):
    rows, width = tokens.shape[0], tokens.shape[2]
    tp = lax.axis_index("tp").astype(jnp.int32)
    core, chip = tp % 2, tp // 2
    first_core = core == 0
    chip_table = jnp.reshape(chip, (1,))
    shards = Shards(count)

    def in_order(own, other):
        return jnp.where(
            first_core, jnp.concatenate([own, other], 0), jnp.concatenate([other, own], 0)
        )

    gain_one = gain_attn.astype(BF).astype(F32)[:, None]
    gain_two = gain_mlp.astype(BF).astype(F32)[:, None]
    own_query = w_query.astype(BF).astype(F32)
    own_keyval = w_keyval.astype(BF).astype(F32)
    own_gate = w_gate.astype(BF).astype(F32)
    own_up = w_up.astype(BF).astype(F32)
    keyval_half = jnp.where(first_core, own_keyval[:, :HD], own_keyval[:, HD:])
    send_in = (jnp.concatenate([own_query, keyval_half], 1) * gain_one).astype(BF)
    send_out = jnp.transpose(w_out).astype(BF)
    send_gate_up = (jnp.concatenate([own_gate, own_up], 1) * gain_two).astype(BF)
    send_down = jnp.transpose(w_down).astype(BF)

    heads = GROUP * HD
    half_count = shards.half
    places = shards.places
    part = half_count // 2
    token = places

    def sync(*values):
        nonlocal token
        token, *values = lax.optimization_barrier((token, *values))
        return values

    def far_all(piece):
        return [shards.far(piece, k) for k in range(1, half_count)]

    def rows_of(value, other):
        return lax.dynamic_slice_in_dim(value, (core ^ other) * rows, rows, 0)

    inputs = tokens.reshape(rows, width).astype(F32)
    scale_one = lax.rsqrt(jnp.mean(inputs * inputs, axis=-1, keepdims=True) + EPS)
    unit_own = (inputs * scale_one).astype(BF)
    far_in = far_all(send_in)
    unit_other = tp_swap(unit_own, 1)
    cot = cotangent.reshape(4, rows, width)
    cots = [lax.dynamic_index_in_dim(cot, tp ^ k, 0, keepdims=False) for k in range(4)]
    cot_near, cot_far = jnp.concatenate(cots[:2], 0), jnp.concatenate(cots[2:], 0)
    send_in, cot_near, cot_far, send_out, send_gate_up, send_down, unit_other, *far_in = sync(
        send_in, cot_near, cot_far, send_out, send_gate_up, send_down, unit_other, *far_in
    )

    gate_up_full = lax.all_gather(send_gate_up, "shard", axis=0, tiled=True)
    far_out = far_all(send_out)
    far_in = pack([send_in] + far_in, send_in.shape[1])
    near_in = shards.near(far_in)
    query_far_b = tp_swap(far_in[:, :heads], 2)
    unit = in_order(unit_own, unit_other)
    unit, query_far_b, near_in, far_in, *far_out = sync(
        unit, query_far_b, near_in, far_in, *far_out
    )

    in_full = unpack(places, far_in, near_in, half_count)
    in_query = in_full[:, :heads]
    scale = HD ** (-0.5)
    column = lax.broadcasted_iota(jnp.int32, (1, in_full.shape[1]), 1)
    query_half = (
        dot(unit, in_full) * jnp.where(column < heads, scale * LOG2E, 1.0)
    ).astype(BF)
    half, query_half, in_query, query_near, *far_out = sync(
        query_half[:, heads:], query_half, in_query, near_in[:, :heads], *far_out
    )

    half_other = tp_swap(half, 1)
    before = lax.ppermute(half, "tp", [(0, 2), (1, 3)])
    far_out = pack([send_out] + far_out, heads)
    near_out = shards.near(far_out)
    half, half_other, before, far_out, query_near = sync(
        half, half_other, before, far_out, query_near
    )

    query_near_b = tp_swap(query_near, 2)
    before_other = tp_swap(before, 1)
    own_pair = jnp.concatenate([before, half], 0)
    other_pair = jnp.concatenate([before_other, half_other], 0)
    keys = jnp.where(first_core, own_pair, other_pair)
    values = jnp.where(first_core, other_pair, own_pair)
    keys_t = jnp.transpose(keys)
    values_t = jnp.transpose(values)
    mixed_a, lse_a = forward_attention(chip_table, query_half, keys, values_t)
    mixed_a, query_near_b, far_out, near_out, send_down = sync(
        mixed_a, query_near_b, far_out, near_out, send_down
    )

    down_full = lax.all_gather(send_down, "shard", axis=0, tiled=True)
    out_far_b = tp_swap(far_out, 2)
    in_query_b = unpack(places, query_far_b, query_near_b, half_count)
    query_b = (dot(unit, in_query_b) * (scale * LOG2E)).astype(BF)
    mixed_b, lse_b = forward_attention(chip_table, query_b, keys, values_t)
    mixed_a, mixed_b, out_far_b, near_out = sync(mixed_a, mixed_b, out_far_b, near_out)

    out_near_b = tp_swap(near_out, 2)
    out_full = unpack(places, far_out, near_out, half_count)
    branch_other = dot(rows_of(mixed_a, 1), out_full, NT)
    branch_own = dot(rows_of(mixed_a, 0), out_full, NT)
    branch_other, branch_own, mixed_b, out_near_b = sync(
        branch_other, branch_own, mixed_b, out_near_b
    )

    out_full_b = unpack(places, out_far_b, out_near_b, half_count)
    branch_other = (branch_other + dot(rows_of(mixed_b, 1), out_full_b, NT)).astype(BF)
    branch_came = tp_swap(branch_other, 1)
    branch_own = branch_own + dot(rows_of(mixed_b, 0), out_full_b, NT)
    hidden = inputs + (branch_own + branch_came.astype(F32))
    scale_two = lax.rsqrt(jnp.mean(hidden * hidden, axis=-1, keepdims=True) + EPS)
    norm_own = (hidden * scale_two).astype(BF)
    (norm_own,) = sync(norm_own)

    cut = rows // 2
    norm_core = tp_swap(norm_own, 1)
    norm_x1 = tp_swap(norm_own[:cut], 2)
    norm_near = jnp.concatenate([norm_own, norm_core], 0)
    norm_own, norm_near, norm_x1 = sync(norm_own, norm_near, norm_x1)

    norm_x2 = tp_swap(norm_own[cut:], 2)
    norm_d1 = tp_swap(norm_x1, 1)
    product, to_gate, to_up = apply_gate_up(norm_near, gate_up_full)
    norm_x2, norm_d1, product, to_gate, to_up = sync(norm_x2, norm_d1, product, to_gate, to_up)

    norm_d2 = tp_swap(norm_x2, 1)
    norm_far = jnp.concatenate([norm_x1, norm_x2, norm_d1, norm_d2], 0)
    product, to_gate, to_up = apply_gate_up(norm_far, gate_up_full, product, to_gate, to_up)
    product, to_gate, to_up, norm_far = sync(product, to_gate, to_up, norm_far)
    kept_down, sent_down = weight_gradient(shards.slots, cot_near, cot_far, product)
    cot_near, cot_far, sent, product, norm_far = sync(
        cot_near, cot_far, sent_down[0], product, norm_far
    )

    came_down = [shards.near(sent)]
    dgate, dup = product_gradient(cot_near, cot_far, to_gate, to_up, down_full)
    dgate, dup, sent, product, *came_down = sync(dgate, dup, sent_down[1], product, *came_down)

    came_down.append(shards.near(sent))
    sums_down = list(fold(kept_down[0], came_down[0], part))
    kept_gate, sent_gate = weight_gradient(shards.slots, norm_near, norm_far, dgate)
    dgate, dup, sent, product, came_down[1], *sums_down = sync(
        dgate, dup, sent_gate[0], product, came_down[1], *sums_down
    )

    came_gate = [shards.near(sent)]
    far_sums = [shards.far(sums_down[0], part)]
    sums_down = list(fold(kept_down[1], came_down[1], part)) + sums_down
    back_x, back_diagonal = feed_back(2 * rows, 2 * rows, dgate, dup, gate_up_full)
    back_x, back_diagonal, dup, dgate, sent, *pieces = sync(
        back_x, back_diagonal, dup, dgate, sent_gate[1], *came_gate, *far_sums, *sums_down
    )
    came_gate, far_sums, sums_down = pieces[:1], pieces[1:2], pieces[2:]

    others = [k for k in range(1, half_count) if k != part]
    came_gate.append(shards.near(sent))
    far_sums += [shards.far(sums_down[k], k) for k in others]
    back_diagonal = tp_swap(back_diagonal, 1)
    sums_gate = list(fold(kept_gate[0], came_gate[0], part))
    back_far = [
        (a.astype(F32) + b.astype(F32)).astype(BF)
        for a, b in (
            (back_x[:cut], back_diagonal[:cut]),
            (back_x[cut:], back_diagonal[cut:]),
        )
    ]
    kept_up, sent_up = weight_gradient(shards.slots, norm_near, norm_far, after(dup, *back_far))
    dgate, dup, sent, *pieces = sync(
        dgate, dup, sent_up[0], *back_far, came_gate[1], *sums_gate, *far_sums
    )
    back_far, came_gate[1], sums_gate, far_sums_down = (
        pieces[:2],
        pieces[2],
        pieces[3 : 3 + part],
        pieces[3 + part :],
    )

    back_came = [tp_swap(back_far[0], 2)]
    came_up = [shards.near(sent)]
    far_sums = [shards.far(sums_gate[0], part)]
    sums_gate = list(fold(kept_gate[1], came_gate[1], part)) + sums_gate
    back_own, back_core = feed_back(0, 2 * rows, dgate, dup, gate_up_full)
    back_own, back_core, product, sent, back_far[1], *pieces = sync(
        back_own, back_core, product, sent_up[1], back_far[1], *back_came, *came_up, *far_sums, *sums_gate
    )
    back_came, came_up, far_sums, sums_gate = pieces[:1], pieces[1:2], pieces[2:3], pieces[3:]

    back_came.append(tp_swap(back_far[1], 2))
    came_up.append(shards.near(sent))
    far_sums += [shards.far(sums_gate[k], k) for k in others]
    back_core = tp_swap(back_core, 1)
    sums_up = list(fold(kept_up[0], came_up[0], part))
    down_parts = down_project(product, down_full)
    back_own, back_core, *pieces = sync(
        back_own, back_core, *back_came, came_up[1], *sums_up, *far_sums, *down_parts
    )
    back_came, came_up[1], sums_up, far_sums_gate, down_parts = (
        pieces[:2],
        pieces[2],
        pieces[3 : 3 + part],
        pieces[3 + part : 2 + part + half_count],
        pieces[2 + part + half_count :],
    )

    sums_up = list(fold(kept_up[1], came_up[1], part)) + sums_up
    down_diagonal = tp_swap(down_parts[3], 1)
    grad_norm = (
        back_own.astype(F32)
        + back_core.astype(F32)
        + jnp.concatenate(back_came, 0).astype(F32)
    )
    unit_two = hidden * scale_two
    grad_hidden = cots[0].astype(F32) + scale_two * (
        grad_norm - unit_two * jnp.mean(grad_norm * unit_two, axis=-1, keepdims=True)
    )
    branch_own = grad_hidden.astype(BF)
    branch_other = tp_swap(branch_own, 1)
    g_out_b = dot(branch_own, rows_of(mixed_b, 0), TN)
    grad_own = dot(branch_own, out_full_b).astype(BF)
    down_far = (down_parts[2].astype(F32) + down_diagonal.astype(F32)).astype(BF)
    branch_other = after(branch_other, g_out_b, grad_own, down_far)
    g_out_b = (g_out_b + dot(branch_other, rows_of(mixed_b, 1), TN)).astype(BF)
    grad_mixed_b = in_order(grad_own, dot(branch_other, out_full_b).astype(BF))
    grad_mixed_b, g_out_b, down_far, branch_own, branch_other, *sums_up = sync(
        grad_mixed_b, g_out_b, down_far, branch_own, branch_other, *sums_up
    )

    g_out_came = tp_swap(g_out_b, 2)
    far_sums = [shards.far(sums_up[part], part)]
    dq_b, dk_b, dv_b = backward_attention(
        chip_table, query_b, grad_mixed_b, mixed_b, lse_b, keys, keys_t, values
    )
    dq_b, dk_b, dv_b, g_out_came, branch_own, branch_other, *pieces = sync(
        dq_b, dk_b, dv_b, g_out_came, branch_own, branch_other, *far_sums, *sums_up
    )
    far_sums, sums_up = pieces[:1], pieces[1:]

    g_query_b = dot(unit, dq_b, TN).astype(BF)
    g_out = (
        dot(branch_own, rows_of(mixed_a, 0), TN)
        + dot(branch_other, rows_of(mixed_a, 1), TN)
        + g_out_came.astype(F32)
    )
    (kept_out,), (sent_out,) = split(places, g_out.astype(BF), half_count)
    grad_mixed_a = in_order(
        dot(branch_own, out_full).astype(BF), dot(branch_other, out_full).astype(BF)
    )
    g_query_b, sent_out, grad_mixed_a, kept_out, *sums_up = sync(
        g_query_b, sent_out, grad_mixed_a, kept_out, *sums_up
    )

    g_query_came = tp_swap(g_query_b, 2)
    far_sums += [shards.far(sums_up[k], k) for k in others]
    came_out = shards.near(sent_out)
    dq_a, dk_a, dv_a = backward_attention(
        chip_table, query_half, grad_mixed_a, mixed_a, lse_a, keys, keys_t, values
    )
    dq_a, dk_a, dv_a, g_query_came, came_out, *far_sums_up = sync(
        dq_a, dk_a, dv_a, g_query_came, came_out, *far_sums
    )

    grad_keys = (dk_a + dk_b) * LN2
    grad_values = dv_a + dv_b
    mine = jnp.where(first_core, grad_keys, grad_values)
    theirs = jnp.where(first_core, grad_values, grad_keys).astype(BF)
    theirs = tp_swap(theirs, 1)
    cuts = [0, rows // 16 * 5, rows // 32 * 21, rows]
    down_far = [down_far[a:b] for a, b in zip(cuts[:-1], cuts[1:])]
    down_came = [tp_swap(down_far[0], 2)]
    g_query = (dot(unit, dq_a, TN) + g_query_came.astype(F32)).astype(BF)
    (kept_query,), (sent_query,) = split(places, g_query, half_count)
    sums_out = fold(kept_out, came_out, half_count)
    mine = mine + theirs.astype(F32)
    chip_rows = mine.shape[0] // 2
    mine, own = mine[chip_rows:], mine[:chip_rows].astype(BF)
    mine, own, sent_query, dq_a, dq_b, down_came[0], down_far[1], down_far[2], *sums_out = sync(
        mine, own, sent_query, dq_a, dq_b, down_came[0], down_far[1], down_far[2], *sums_out
    )

    earlier = lax.ppermute(own, "tp", [(2, 0), (3, 1)])
    came_query = shards.near(sent_query)
    far_out_sums = [shards.far(sums_out[k], k) for k in range(1, half_count)]
    back_other = dot(rows_of(dq_a, 1), in_query, NT) + dot(rows_of(dq_b, 1), in_query_b, NT)
    back_own = dot(rows_of(dq_a, 0), in_query, NT) + dot(rows_of(dq_b, 0), in_query_b, NT)
    back_own, back_other, earlier, came_query, down_far[1], *far_out_sums = sync(
        back_own, back_other, earlier, came_query, down_far[1], *far_out_sums
    )

    down_came.append(tp_swap(down_far[1], 2))
    grad_half = (mine + earlier.astype(F32)).astype(BF)
    g_half = dot(unit, grad_half, TN).astype(BF)
    (kept_half,), (sent_half,) = split(places, g_half, half_count)
    sums_query = fold(kept_query, came_query, half_count)
    in_half = in_full[:, heads:]
    back_other = (back_other + dot(rows_of(grad_half, 1), in_half, NT)).astype(BF)
    back_own = back_own + dot(rows_of(grad_half, 0), in_half, NT)
    back_other, back_own, kept_half, sent_half, down_came[1], down_far[2], *sums_query = sync(
        back_other, back_own, kept_half, sent_half, down_came[1], down_far[2], *sums_query
    )

    came_half = shards.near(sent_half)
    back_came = tp_swap(back_other, 1)
    far_query = [shards.far(sums_query[k], k) for k in range(1, half_count)]
    down_came.append(tp_swap(down_far[2], 2))
    down_core = tp_swap(down_parts[1], 1)
    grad_unit = back_own + back_came.astype(F32)
    unit_one = inputs * scale_one
    grad_tokens = grad_hidden + scale_one * (
        grad_unit - unit_one * jnp.mean(grad_unit * unit_one, axis=-1, keepdims=True)
    )
    came_half, grad_tokens, down_core, *pieces = sync(
        came_half, grad_tokens, down_core, *down_came, *far_query
    )
    down_came, far_query = pieces[:3], pieces[3:]

    sums_half = fold(kept_half, came_half, half_count)
    far_half = [shards.far(sums_half[k], k) for k in range(1, half_count)]
    output = (
        hidden
        + down_parts[0].astype(F32)
        + down_core.astype(F32)
        + jnp.concatenate(down_came, 0).astype(F32)
    ).astype(BF)

    def total(own, others):
        return functools.reduce(lambda t, o: t + o.astype(F32), others, own.astype(F32))

    sum_gate = total(sums_gate[0], far_sums_gate)
    sum_up = total(sums_up[0], far_sums_up)
    grad_w_gate = sum_gate * gain_two
    grad_w_up = sum_up * gain_two
    gain_two_part = jnp.sum(own_gate * sum_gate + own_up * sum_up, axis=1)
    grad_w_down = jnp.transpose(total(sums_down[0], far_sums_down))
    grad_w_out = jnp.transpose(total(sums_out[0], far_out_sums))
    sum_query = total(sums_query[0], far_query)
    sum_half = total(sums_half[0], far_half)

    gain_one_part = jnp.sum(own_query * sum_query, axis=1) + jnp.sum(keyval_half * sum_half, axis=1)
    small = jnp.concatenate(
        [jnp.transpose(sum_half), gain_one_part[None], gain_two_part[None], jnp.zeros((6, sum_half.shape[0]), F32)], 0
    )
    small = small + tp_swap(small, 2)
    other = tp_swap(small, 1)
    gains = small[HD : HD + 2] + other[HD : HD + 2]
    sum_half = jnp.transpose(small[:HD])
    half_swapped = jnp.transpose(other[:HD])
    grad_w_keyval = (
        jnp.where(
            first_core,
            jnp.concatenate([sum_half, half_swapped], 1),
            jnp.concatenate([half_swapped, sum_half], 1),
        )
        * gain_one
    )
    return (
        output.reshape(rows, 1, width),
        grad_tokens.reshape(rows, 1, width),
        sum_query * gain_one,
        grad_w_keyval,
        grad_w_out,
        grad_w_gate,
        grad_w_up,
        grad_w_down,
        gains[0],
        gains[1],
    )


def solution(mesh):
    in_specs = (
        P("tp", "shard", None),
        P("shard", "tp"),
        P("shard", None),
        P("tp", "shard"),
        P("shard", "tp"),
        P("shard", "tp"),
        P("tp", "shard"),
        P("shard"),
        P("shard"),
        P(None, "shard", None),
    )
    out_specs = (
        P("tp", "shard", None),
        P("tp", "shard", None),
        P("shard", "tp"),
        P("shard", None),
        P("tp", "shard"),
        P("shard", "tp"),
        P("shard", "tp"),
        P("tp", "shard"),
        P("shard"),
        P("shard"),
    )
    return jax.shard_map(
        functools.partial(local, mesh.shape["shard"]),
        mesh=mesh,
        in_specs=in_specs,
        out_specs=out_specs,
        check_vma=False,
    )
```

time: 643 us -> 546 us (0.85)
  waiting for transfers between devices: 211 us -> 128 us
  matrix products: 96 us -> 33.4 us
  Pallas kernels: 132 us -> 168 us
  starting transfers between devices: 110 us -> 93.3 us
  between operations: 3.04 us -> 15.7 us
  other arithmetic: 41.9 us -> 53.5 us
    ppermute x33 -> x24, waiting for transfers between devices: 129 us -> 55.1 us  [far(): lax.ppermute(value, 'shard', [(i, (i // 2 ^ k) * 2 + i % 2) for i in rang...]
    dot_general x30 -> x23, matrix products: 96 us -> 33.4 us  [dot(): return lax.dot_general(a, b, dims, preferred_element_type=F32)]
    ppermute x29 -> x11, waiting for transfers between devices: 62.5 us -> 10.3 us  [near(): return lax.ppermute(value, 'shard', [(i, i ^ 1) for i in range(self.count)])]
    ppermute x28 -> x29, waiting for transfers between devices: 8.77 us -> 50.9 us  [tp_swap(): return lax.ppermute(value, 'tp', [(i, i ^ mask) for i in range(4)])]
    pallas_call x32 -> x31, Pallas kernels: 132 us -> 168 us  [run(): call(*(pltpu.with_memory_space_constraint(x, pltpu.HBM) if x.size > LARGE...]
    ppermute x29 -> x11, starting transfers between devices: 28.5 us -> 11.9 us  [near(): return lax.ppermute(value, 'shard', [(i, i ^ 1) for i in range(self.count)])]
    all_gather x0 -> x2, waiting for transfers between devices: none -> 9.04 us  [the longest x1 9.04 us: local(): down_full = lax.all_gather(send_down, 'shard', axis=0, tiled=True)]
    ppermute x1, waiting for transfers between devices: 7.52 us -> 0.01 us  [local(): earlier = lax.ppermute(own, 'tp', [(2, 0), (3, 1)])]
  transfers between devices with their start and end apart: 92 -> 68, of which waited for: 37 -> 28; matrix products, arithmetic and copies ran while one was open for 21% -> 16% of each run, Pallas kernels for 15% -> 31%
where the time goes in v3:
time: 546 us; the launch traced here: 541 us
  Pallas kernels  168 us (31%)
  waiting for transfers between devices  128 us (23%)
  starting transfers between devices  93.3 us (17%)
  other arithmetic  53.5 us (10%)
  local copies, waits for them, and re-layouts  48.5 us (9%)
  matrix products  33.4 us (6%)
  between operations  15.7 us (3%)
    pallas_call x31, Pallas kernels, run(): call(*(pltpu.with_memory_space_constraint(x, pltpu.HBM) if x.size > LARGE...  168 us
    ppermute x24, waiting for transfers between devices, far(): lax.ppermute(value, 'shard', [(i, (i // 2 ^ k) * 2 + i % 2) for i in rang...  55.1 us
    ppermute x24, starting transfers between devices, far(): lax.ppermute(value, 'shard', [(i, (i // 2 ^ k) * 2 + i % 2) for i in rang...  52.6 us
    ppermute x29, waiting for transfers between devices, tp_swap(): return lax.ppermute(value, 'tp', [(i, i ^ mask) for i in range(4)])  50.9 us
    unnamed x208, local copies, waits for them, and re-layouts  38 us
    dot_general x23, matrix products, dot(): return lax.dot_general(a, b, dims, preferred_element_type=F32)  33.4 us
    ppermute x29, starting transfers between devices, tp_swap(): return lax.ppermute(value, 'tp', [(i, i ^ mask) for i in range(4)])  23.6 us
    ppermute x11, starting transfers between devices, near(): return lax.ppermute(value, 'shard', [(i, i ^ 1) for i in range(self.count)])  11.9 us
  transfers between devices with their start and end apart: 68, of which 28 were waited for; matrix products, arithmetic and copies ran while one was open for 16% of the time, Pallas kernels for 31%

profile of v3, /device:TPU:0, one launch (start us, length us, event | category | flops | bytes accessed | tf_op | source)
XLA Modules:
  0.0 541.3 jit_solution(11019636307013078700)
XLA Ops:
  43.4 11.4 %collective-permute-done.7.refs_2_ = bf16[192,384]{1,0:T(8,128)(2,1)S(1)} collective-permute-done((bf16[192,384]{1,0:T(8,128)(2,1)S(1)}, bf16[192,384]{1,0:T(8,128)(2,1)S(1)}, u32[]{:S(2)}, u32[]{:S(2)}) %collective-permute-start.7) | collective-permute-done | bytes 147488 | tf_op jit(solution)/shard_map/ppermute | solution.py:541
  72.6 5.8 %attention_forward.2 = (bf16[1024,384]{1,0:T(8,128)(2,1)S(1)}, f32[8,1024]{1,0:T(8,128)S(1)}) custom-call(s32[1]{0:T(128)} %bitcast.1.chip_ref, bf16[1024,512]{1,0:T(8,128)(2,1)S(1)} %multiply_convert_fusion.1.q_ref, bf16[2048,128]{1,0:T(8,128)(2,1)S(1)} %get-tuple-element.592.k_ref, bf16[128,2048]{1,0:T(8,128)(2,1)S(1)} %copy.28.vt_ref), custom_call_target="tpu_custom_call" | custom-call | tf_op jit(solution)/shard_map/attention_forward/pallas_call | solution.py:39
  94.5 5.9 %attention_forward.3 = (bf16[1024,384]{1,0:T(8,128)(2,1)S(1)}, f32[8,1024]{1,0:T(8,128)S(1)}) custom-call(s32[1]{0:T(128)} %bitcast.1.chip_ref, bf16[1024,384]{1,0:T(8,128)(2,1)S(1)} %multiply_convert_fusion.2.q_ref, bf16[2048,128]{1,0:T(8,128)(2,1)S(1)} %get-tuple-element.592.k_ref, bf16[128,2048]{1,0:T(8,128)(2,1)S(1)} %copy.28.vt_ref), custom_call_target="tpu_custom_call" | custom-call | tf_op jit(solution)/shard_map/attention_forward/pallas_call | solution.py:39
  108.9 9.4 %collective-permute-done.15.near = bf16[768,384]{1,0:T(8,128)(2,1)S(1)} collective-permute-done((bf16[768,384]{1,0:T(8,128)(2,1)}, bf16[768,384]{1,0:T(8,128)(2,1)S(1)}, u32[]{:S(2)}, u32[]{:S(2)}) %collective-permute-start.15) | collective-permute-done | bytes 589856 | tf_op jit(solution)/shard_map/ppermute | solution.py:550
  135.2 14.9 %collective-permute-done.18 = bf16[256,1536]{1,0:T(8,128)(2,1)} collective-permute-done((bf16[256,1536]{1,0:T(8,128)(2,1)S(1)}, bf16[256,1536]{1,0:T(8,128)(2,1)}, u32[]{:S(2)}, u32[]{:S(2)}) %collective-permute-start.18) | collective-permute-done | bytes 786464 | tf_op jit(solution)/shard_map/ppermute | solution.py:550
  152.8 14.3 %gate_up_first.1 = (bf16[2048,1152]{1,0:T(8,128)(2,1)S(1)}, bf16[2048,1152]{1,0:T(8,128)(2,1)S(1)}, bf16[2048,1152]{1,0:T(8,128)(2,1)S(1)}) custom-call(bf16[1024,1536]{1,0:T(8,128)(2,1)} %pad_maximum_fusion.2.norm_ref.near_ref, bf16[1536,2304]{1,0:T(8,128)(2,1)} %all-gather.3.cloned.1.call-done.whole_ref.gate_up_ref), custom_call_target="tpu_custom_call" | custom-call | tf_op jit(solution)/shard_map/gate_up_first/pallas_call | solution.py:39
  177.9 15.3 %gate_up_rest.1 = (bf16[2048,1152]{1,0:T(8,128)(2,1)}, bf16[2048,1152]{1,0:T(8,128)(2,1)}, bf16[2048,1152]{1,0:T(8,128)(2,1)}) custom-call(bf16[1024,1536]{1,0:T(8,128)(2,1)} %copy-done.51, bf16[1536,2304]{1,0:T(8,128)(2,1)} %all-gather.3.cloned.1.call-done.whole_ref.gate_up_ref, ...), custom_call_target="tpu_custom_call", output_to_operand_aliasing={{0}: (2, {}), {1}: (3, {}), {2}: (4, {})} | custom-call | tf_op jit(solution)/shard_map/gate_up_rest/pallas_call | solution.py:39
  193.2 13.8 %weight_gradient.3 = (bf16[384,1152]{1,0:T(8,128)(2,1)S(1)}, bf16[384,1152]{1,0:T(8,128)(2,1)S(1)}, bf16[384,1152]{1,0:T(8,128)(2,1)}, bf16[384,1152]{1,0:T(8,128)(2,1)S(1)}) custom-call(s32[8]{0:T(128)S(1)} %fusion.60.slot_ref, bf16[1024,1536]{1,0:T(8,128)(2,1)} %get-tuple-element.353.near_ref, bf16[1024,1536]{1,0:T(8,128)(2,1)} %get-tuple-element.354.far_ref, ...), custom_call_target="tpu_custom_call" | custom-call | tf_op jit(solution)/shard_map/weight_gradient/pallas_call | solution.py:39
  210.2 9.0 %all-gather.5.cloned.1.call-done.down_ref = bf16[1536,1152]{1,0:T(8,128)(2,1)} async-done(((bf16[192,1152]{1,0:T(8,128)(2,1)}), bf16[1536,1152]{1,0:T(8,128)(2,1)}) %all-gather.5.cloned.1.call-update) | async-done | bytes 3538960 | tf_op jit(solution)/shard_map/all_gather | solution.py:649
  219.3 14.6 %product_gradient.1 = (bf16[2048,1152]{1,0:T(8,128)(2,1)S(1)}, bf16[2048,1152]{1,0:T(8,128)(2,1)S(1)}) custom-call(bf16[1024,1536]{1,0:T(8,128)(2,1)} %get-tuple-element.353.near_ref, bf16[1024,1536]{1,0:T(8,128)(2,1)} %get-tuple-element.354.far_ref, bf16[2048,1152]{1,0:T(8,128)(2,1)} %get-tuple-element.355.to_gate_ref, ...), custom_call_target="tpu_custom_call" | custom-call | tf_op jit(solution)/shard_map/product_gradient/pallas_call | solution.py:39
  240.2 13.3 %weight_gradient.4 = (bf16[384,1152]{1,0:T(8,128)(2,1)S(1)}, bf16[384,1152]{1,0:T(8,128)(2,1)S(1)}, bf16[384,1152]{1,0:T(8,128)(2,1)S(1)}, bf16[384,1152]{1,0:T(8,128)(2,1)S(1)}) custom-call(s32[8]{0:T(128)S(1)} %fusion.60.slot_ref, bf16[1024,1536]{1,0:T(8,128)(2,1)} %pad_maximum_fusion.2.norm_ref.near_ref, bf16[1024,1536]{1,0:T(8,128)(2,1)} %copy-done.51, ...), custom_call_target="tpu_custom_call" | custom-call | tf_op jit(solution)/shard_map/weight_gradient/pallas_call | solution.py:39
  253.5 5.2 collective-permute-done.23.came
  259.3 9.9 %collective-permute-start.25 = (bf16[192,1152]{1,0:T(8,128)(2,1)S(1)}, bf16[192,1152]{1,0:T(8,128)(2,1)S(1)}, u32[]{:S(2)}, u32[]{:S(2)}) collective-permute-start(bf16[192,1152]{1,0:T(8,128)(2,1)S(1)} %get-tuple-element.379), channel_id=1, source_target_pairs={{0,16},{4,20},{8,24},{12,28},{16,0},{20,4},{24,8},{28,12},{1,17},{... | collective-permute-start | bytes 1327112 | tf_op jit(solution)/shard_map/ppermute | solution.py:541
  269.4 12.8 %feed_back.2 = (bf16[512,1536]{1,0:T(8,128)(2,1)S(1)}, bf16[512,1536]{1,0:T(8,128)(2,1)S(1)}) custom-call(bf16[2048,1152]{1,0:T(8,128)(2,1)} %copy-done.1, bf16[2048,1152]{1,0:T(8,128)(2,1)} %copy-done.2, bf16[1536,2304]{1,0:T(8,128)(2,1)} %all-gather.3.cloned.1.call-done.whole_ref.gate_up_ref), custom_call_target="tpu_custom_call" | custom-call | tf_op jit(solution)/shard_map/feed_back/pallas_call | solution.py:39
  291.3 12.9 %weight_gradient.5 = (bf16[384,1152]{1,0:T(8,128)(2,1)S(1)}, bf16[384,1152]{1,0:T(8,128)(2,1)S(1)}, bf16[384,1152]{1,0:T(8,128)(2,1)S(1)}, bf16[384,1152]{1,0:T(8,128)(2,1)S(1)}) custom-call(s32[8]{0:T(128)S(1)} %fusion.60.slot_ref, bf16[1024,1536]{1,0:T(8,128)(2,1)} %pad_maximum_fusion.2.norm_ref.near_ref, bf16[1024,1536]{1,0:T(8,128)(2,1)} %copy-done.51, ...), custom_call_target="tpu_custom_call" | custom-call | tf_op jit(solution)/shard_map/weight_gradient/pallas_call | solution.py:39
  304.2 6.2 %collective-permute-done.29 = bf16[192,1152]{1,0:T(8,128)(2,1)S(1)} collective-permute-done((bf16[192,1152]{1,0:T(8,128)(2,1)S(1)}, bf16[192,1152]{1,0:T(8,128)(2,1)S(1)}, u32[]{:S(2)}, u32[]{:S(2)}) %collective-permute-start.29) | collective-permute-done | bytes 442400 | tf_op jit(solution)/shard_map/ppermute | solution.py:541
  314.3 12.7 %feed_back.3 = (bf16[512,1536]{1,0:T(8,128)(2,1)S(1)}, bf16[512,1536]{1,0:T(8,128)(2,1)S(1)}) custom-call(bf16[2048,1152]{1,0:T(8,128)(2,1)} %copy-done.1, bf16[2048,1152]{1,0:T(8,128)(2,1)} %copy-done.2, bf16[1536,2304]{1,0:T(8,128)(2,1)} %all-gather.3.cloned.1.call-done.whole_ref.gate_up_ref), custom_call_target="tpu_custom_call" | custom-call | tf_op jit(solution)/shard_map/feed_back/pallas_call | solution.py:39
  337.9 12.7 %down_project.1 = (bf16[512,1536]{1,0:T(8,128)(2,1)S(1)}, bf16[512,1536]{1,0:T(8,128)(2,1)S(1)}, bf16[512,1536]{1,0:T(8,128)(2,1)S(1)}, bf16[512,1536]{1,0:T(8,128)(2,1)S(1)}) custom-call(bf16[2048,1152]{1,0:T(8,128)(2,1)} %get-tuple-element.426.grad_ref.product_ref, bf16[1536,1152]{1,0:T(8,128)(2,1)} %all-gather.5.cloned.1.call-done.down_ref), custom_call_target="tpu_custom_call" | custom-call | tf_op jit(solution)/shard_map/down_project/pallas_call | solution.py:39
  380.2 10.8 %attention_backward.2 = (bf16[1024,384]{1,0:T(8,128)(2,1)S(1)}, f32[2048,128]{1,0:T(8,128)S(1)}, f32[2048,128]{1,0:T(8,128)S(1)}) custom-call(s32[1]{0:T(128)} %bitcast.1.chip_ref, bf16[1024,384]{1,0:T(8,128)(2,1)S(1)} %copy-done.20, bf16[1024,384]{1,0:T(8,128)(2,1)S(1)} %copy-done.21, bf16[1024,384]{1,0:T(8,128)(2,1)S(1)} %copy-done.11, ...), custom_call_target="tpu_custom_call" | custom-call | tf_op jit(solution)/shard_map/attention_backward/pallas_call | solution.py:39
  414.0 11.0 %attention_backward.3 = (bf16[1024,384]{1,0:T(8,128)(2,1)S(1)}, f32[2048,128]{1,0:T(8,128)S(1)}, f32[2048,128]{1,0:T(8,128)S(1)}) custom-call(s32[1]{0:T(128)} %bitcast.1.chip_ref, bf16[1024,512]{1,0:T(8,128)(2,1)S(1)} %copy-done.16, bf16[1024,384]{1,0:T(8,128)(2,1)S(1)} %maximum_select_fusion.2.g_ref, bf16[1024,384]{1,0:T(8,128)(2,1)S(1)} %copy-done.14, ...), custom_call_target="tpu_custom_call" | custom-call | tf_op jit(solution)/shard_map/attention_backward/pallas_call | solution.py:39
  425.1 7.3 %collective-permute-done.45 = bf16[192,1152]{1,0:T(8,128)(2,1)S(1)} collective-permute-done((bf16[192,1152]{1,0:T(8,128)(2,1)S(1)}, bf16[192,1152]{1,0:T(8,128)(2,1)S(1)}, u32[]{:S(2)}, u32[]{:S(2)}) %collective-permute-start.45) | collective-permute-done | bytes 442400 | tf_op jit(solution)/shard_map/ppermute | solution.py:541
  443.0 8.2 %collective-permute-done.47 = bf16[160,1536]{1,0:T(8,128)(2,1)S(1)} collective-permute-done((bf16[160,1536]{1,0:T(8,128)(2,1)S(1)}, bf16[160,1536]{1,0:T(8,128)(2,1)S(1)}, u32[]{:S(2)}, u32[]{:S(2)}) %collective-permute-start.47) | collective-permute-done | bytes 491552 | tf_op jit(solution)/shard_map/ppermute | solution.py:550
  462.1 5.8 %collective-permute-done.51 = bf16[192,384]{1,0:T(8,128)(2,1)S(1)} collective-permute-done((bf16[192,384]{1,0:T(8,128)(2,1)S(1)}, bf16[192,384]{1,0:T(8,128)(2,1)S(1)}, u32[]{:S(2)}, u32[]{:S(2)}) %collective-permute-start.51) | collective-permute-done | bytes 147488 | tf_op jit(solution)/shard_map/ppermute | solution.py:541
  491.3 5.2 collective-permute-start.58
  (450 shorter events, 277.4 us)
Async XLA Ops:
  7.2 145.6 %all-gather.3.cloned.1.call-start = ((), (), s32[]{:S(2)}) async-start(), calls=%async_computation | async-start | bytes 7962624 | tf_op jit(solution)/shard_map/all_gather | solution.py:607
  30.4 188.9 %all-gather.5.cloned.1.call-start = ((), (), s32[]{:S(2)}) async-start(), calls=%async_computation.1 | async-start | bytes 3981312 | tf_op jit(solution)/shard_map/all_gather | solution.py:649
  30.5 24.9 %collective-permute-start.5 = (bf16[768,512]{1,0:T(8,128)(2,1)S(1)}, bf16[768,512]{1,0:T(8,128)(2,1)S(1)}, u32[]{:S(2)}, u32[]{:S(2)}) collective-permute-start(bf16[768,512]{1,0:T(8,128)(2,1)S(1)} %pack_pieces.2.far), channel_id=1, source_target_pairs={{0,4},{4,0},{8,12},{12,8},{16,20},{20,16},{24,28},{28,24},{1,5},{5... | collective-permute-start | bytes 2359304 | tf_op jit(solution)/shard_map/ppermute | solution.py:546
  32.2 22.6 %collective-permute-start.4 = (bf16[768,384]{1,0:T(8,128)(2,1)S(1)}, bf16[768,384]{1,0:T(8,128)(2,1)S(1)}, u32[]{:S(2)}, u32[]{:S(2)}) collective-permute-start(bf16[768,384]{1,0:T(8,128)(2,1)S(1)} %slice.99), channel_id=1, source_target_pairs={{0,2},{1,3},{2,0},{3,1},{4,6},{5,7},{6,4},{7,5},{8,10},{9,11},{10,... | collective-permute-start | bytes 1769480 | tf_op jit(solution)/shard_map/ppermute | solution.py:550
  130.2 20.0 %collective-permute-start.18 = (bf16[256,1536]{1,0:T(8,128)(2,1)S(1)}, bf16[256,1536]{1,0:T(8,128)(2,1)}, u32[]{:S(2)}, u32[]{:S(2)}) collective-permute-start(bf16[256,1536]{1,0:T(8,128)(2,1)S(1)} %slice.79), channel_id=1, source_target_pairs={{0,2},{1,3},{2,0},{3,1},{4,6},{5,7},{6,4},{7,5},{8,10},{9,11},{10,... | collective-permute-start | bytes 2359304 | tf_op jit(solution)/shard_map/ppermute | solution.py:550
  151.1 20.4 %collective-permute-start.19 = (bf16[256,1536]{1,0:T(8,128)(2,1)}, bf16[256,1536]{1,0:T(8,128)(2,1)}, u32[]{:S(2)}, u32[]{:S(2)}) collective-permute-start(bf16[256,1536]{1,0:T(8,128)(2,1)} %slice.80), channel_id=1, source_target_pairs={{0,2},{1,3},{2,0},{3,1},{4,6},{5,7},{6,4},{7,5},{8,10},{9,11},{10,... | collective-permute-start | bytes 2359304 | tf_op jit(solution)/shard_map/ppermute | solution.py:550
  209.8 28.5 %collective-permute-start.22 = (bf16[384,1152]{1,0:T(8,128)(2,1)}, bf16[384,1152]{1,0:T(8,128)(2,1)}, u32[]{:S(2)}, u32[]{:S(2)}) collective-permute-start(bf16[384,1152]{1,0:T(8,128)(2,1)} %get-tuple-element.362), channel_id=1, source_target_pairs={{0,4},{4,0},{8,12},{12,8},{16,20},{20,16},{24,28},{28,24},{1,5},{5... | collective-permute-start | bytes 2654216 | tf_op jit(solution)/shard_map/ppermute | solution.py:546
  238.3 20.4 %collective-permute-start.23 = (bf16[384,1152]{1,0:T(8,128)(2,1)S(1)}, bf16[384,1152]{1,0:T(8,128)(2,1)S(1)}, u32[]{:S(2)}, u32[]{:S(2)}) collective-permute-start(bf16[384,1152]{1,0:T(8,128)(2,1)S(1)} %copy-done.41), channel_id=1, source_target_pairs={{0,4},{4,0},{8,12},{12,8},{16,20},{20,16},{24,28},{28,24},{1,5},{5... | collective-permute-start | bytes 2654216 | tf_op jit(solution)/shard_map/ppermute | solution.py:546
  258.7 26.6 %collective-permute-start.24 = (bf16[384,1152]{1,0:T(8,128)(2,1)S(1)}, bf16[384,1152]{1,0:T(8,128)(2,1)S(1)}, u32[]{:S(2)}, u32[]{:S(2)}) collective-permute-start(bf16[384,1152]{1,0:T(8,128)(2,1)S(1)} %get-tuple-element.378), channel_id=1, source_target_pairs={{0,4},{4,0},{8,12},{12,8},{16,20},{20,16},{24,28},{28,24},{1,5},{5... | collective-permute-start | bytes 2654216 | tf_op jit(solution)/shard_map/ppermute | solution.py:546
  259.3 26.0 %collective-permute-start.25 = (bf16[192,1152]{1,0:T(8,128)(2,1)S(1)}, bf16[192,1152]{1,0:T(8,128)(2,1)S(1)}, u32[]{:S(2)}, u32[]{:S(2)}) collective-permute-start(bf16[192,1152]{1,0:T(8,128)(2,1)S(1)} %get-tuple-element.379), channel_id=1, source_target_pairs={{0,16},{4,20},{8,24},{12,28},{16,0},{20,4},{24,8},{28,12},{1,17},{... | collective-permute-start | bytes 1327112 | tf_op jit(solution)/shard_map/ppermute | solution.py:541
  286.1 24.3 %collective-permute-start.27 = (bf16[384,1152]{1,0:T(8,128)(2,1)S(1)}, bf16[384,1152]{1,0:T(8,128)(2,1)S(1)}, u32[]{:S(2)}, u32[]{:S(2)}) collective-permute-start(bf16[384,1152]{1,0:T(8,128)(2,1)S(1)} %get-tuple-element.391), channel_id=1, source_target_pairs={{0,4},{4,0},{8,12},{12,8},{16,20},{20,16},{24,28},{28,24},{1,5},{5... | collective-permute-start | bytes 2654216 | tf_op jit(solution)/shard_map/ppermute | solution.py:546
  287.3 23.1 %collective-permute-start.29 = (bf16[192,1152]{1,0:T(8,128)(2,1)S(1)}, bf16[192,1152]{1,0:T(8,128)(2,1)S(1)}, u32[]{:S(2)}, u32[]{:S(2)}) collective-permute-start(bf16[192,1152]{1,0:T(8,128)(2,1)S(1)} %get-tuple-element.398), channel_id=1, source_target_pairs={{0,24},{4,28},{8,16},{12,20},{16,8},{20,12},{24,0},{28,4},{1,25},{... | collective-permute-start | bytes 1327112 | tf_op jit(solution)/shard_map/ppermute | solution.py:541
  310.4 21.7 %collective-permute-start.31 = (bf16[384,1152]{1,0:T(8,128)(2,1)S(1)}, bf16[384,1152]{1,0:T(8,128)(2,1)S(1)}, u32[]{:S(2)}, u32[]{:S(2)}) collective-permute-start(bf16[384,1152]{1,0:T(8,128)(2,1)S(1)} %get-tuple-element.407), channel_id=1, source_target_pairs={{0,4},{4,0},{8,12},{12,8},{16,20},{20,16},{24,28},{28,24},{1,5},{5... | collective-permute-start | bytes 2654216 | tf_op jit(solution)/shard_map/ppermute | solution.py:546
  311.5 20.6 %collective-permute-start.30 = (bf16[256,1536]{1,0:T(8,128)(2,1)S(1)}, bf16[256,1536]{1,0:T(8,128)(2,1)S(1)}, u32[]{:S(2)}, u32[]{:S(2)}) collective-permute-start(bf16[256,1536]{1,0:T(8,128)(2,1)S(1)} %get-tuple-element.406), channel_id=1, source_target_pairs={{0,2},{1,3},{2,0},{3,1},{4,6},{5,7},{6,4},{7,5},{8,10},{9,11},{10,... | collective-permute-start | bytes 2359304 | tf_op jit(solution)/shard_map/ppermute | solution.py:550
  332.0 24.8 %collective-permute-start.33 = (bf16[512,1536]{1,0:T(8,128)(2,1)S(1)}, bf16[512,1536]{1,0:T(8,128)(2,1)S(1)}, u32[]{:S(2)}, u32[]{:S(2)}) collective-permute-start(bf16[512,1536]{1,0:T(8,128)(2,1)S(1)} %get-tuple-element.415), channel_id=1, source_target_pairs={{0,1},{1,0},{2,3},{3,2},{4,5},{5,4},{6,7},{7,6},{8,9},{9,8},{10,11... | collective-permute-start | bytes 4718600 | tf_op jit(solution)/shard_map/ppermute | solution.py:550
  332.1 24.7 %collective-permute-start.35 = (bf16[384,1152]{1,0:T(8,128)(2,1)S(1)}, bf16[384,1152]{1,0:T(8,128)(2,1)S(1)}, u32[]{:S(2)}, u32[]{:S(2)}) collective-permute-start(bf16[384,1152]{1,0:T(8,128)(2,1)S(1)} %get-tuple-element.418), channel_id=1, source_target_pairs={{0,4},{4,0},{8,12},{12,8},{16,20},{20,16},{24,28},{28,24},{1,5},{5... | collective-permute-start | bytes 2654216 | tf_op jit(solution)/shard_map/ppermute | solution.py:546
  333.6 23.2 %collective-permute-start.34 = (bf16[256,1536]{1,0:T(8,128)(2,1)S(1)}, bf16[256,1536]{1,0:T(8,128)(2,1)S(1)}, u32[]{:S(2)}, u32[]{:S(2)}) collective-permute-start(bf16[256,1536]{1,0:T(8,128)(2,1)S(1)} %get-tuple-element.417), channel_id=1, source_target_pairs={{0,2},{1,3},{2,0},{3,1},{4,6},{5,7},{6,4},{7,5},{8,10},{9,11},{10,... | collective-permute-start | bytes 2359304 | tf_op jit(solution)/shard_map/ppermute | solution.py:550
  334.4 22.4 %collective-permute-start.37 = (bf16[192,1152]{1,0:T(8,128)(2,1)S(1)}, bf16[192,1152]{1,0:T(8,128)(2,1)S(1)}, u32[]{:S(2)}, u32[]{:S(2)}) collective-permute-start(bf16[192,1152]{1,0:T(8,128)(2,1)S(1)} %get-tuple-element.425), channel_id=1, source_target_pairs={{0,24},{4,28},{8,16},{12,20},{16,8},{20,12},{24,0},{28,4},{1,25},{... | collective-permute-start | bytes 1327112 | tf_op jit(solution)/shard_map/ppermute | solution.py:541
  371.6 28.4 %collective-permute-start.40 = (bf16[1536,384]{1,0:T(8,128)(2,1)}, bf16[1536,384]{1,0:T(8,128)(2,1)}, u32[]{:S(2)}, u32[]{:S(2)}) collective-permute-start(bf16[1536,384]{1,0:T(8,128)(2,1)} %fusion.11), channel_id=1, source_target_pairs={{0,2},{1,3},{2,0},{3,1},{4,6},{5,7},{6,4},{7,5},{8,10},{9,11},{10,... | collective-permute-start | bytes 3538952 | tf_op jit(solution)/shard_map/ppermute | solution.py:550
  372.9 22.7 %collective-permute-start.41 = (bf16[192,1152]{1,0:T(8,128)(2,1)}, bf16[192,1152]{1,0:T(8,128)(2,1)}, u32[]{:S(2)}, u32[]{:S(2)}) collective-permute-start(bf16[192,1152]{1,0:T(8,128)(2,1)} %get-tuple-element.453), channel_id=1, source_target_pairs={{0,16},{4,20},{8,24},{12,28},{16,0},{20,4},{24,8},{28,12},{1,17},{... | collective-permute-start | bytes 1327112 | tf_op jit(solution)/shard_map/ppermute | solution.py:541
  408.9 27.3 %collective-permute-start.42 = (bf16[1536,384]{1,0:T(8,128)(2,1)S(1)}, bf16[1536,384]{1,0:T(8,128)(2,1)S(1)}, u32[]{:S(2)}, u32[]{:S(2)}) collective-permute-start(bf16[1536,384]{1,0:T(8,128)(2,1)S(1)} %convolution_convert_fusion), channel_id=1, source_target_pairs={{0,2},{1,3},{2,0},{3,1},{4,6},{5,7},{6,4},{7,5},{8,10},{9,11},{10,... | collective-permute-start | bytes 3538952 | tf_op jit(solution)/shard_map/ppermute | solution.py:550
  410.2 22.1 %collective-permute-start.43 = (bf16[768,384]{1,0:T(8,128)(2,1)S(1)}, bf16[768,384]{1,0:T(8,128)(2,1)S(1)}, u32[]{:S(2)}, u32[]{:S(2)}) collective-permute-start(bf16[768,384]{1,0:T(8,128)(2,1)S(1)} %get-tuple-element.472), channel_id=1, source_target_pairs={{0,4},{4,0},{8,12},{12,8},{16,20},{20,16},{24,28},{28,24},{1,5},{5... | collective-permute-start | bytes 1769480 | tf_op jit(solution)/shard_map/ppermute | solution.py:546
  411.6 20.7 %collective-permute-start.45 = (bf16[192,1152]{1,0:T(8,128)(2,1)S(1)}, bf16[192,1152]{1,0:T(8,128)(2,1)S(1)}, u32[]{:S(2)}, u32[]{:S(2)}) collective-permute-start(bf16[192,1152]{1,0:T(8,128)(2,1)S(1)} %copy-done.43), channel_id=1, source_target_pairs={{0,24},{4,28},{8,16},{12,20},{16,8},{20,12},{24,0},{28,4},{1,25},{... | collective-permute-start | bytes 1327112 | tf_op jit(solution)/shard_map/ppermute | solution.py:541
  488.3 21.4 %collective-permute-start.57 = (bf16[176,1536]{1,0:T(8,128)(2,1)}, bf16[176,1536]{1,0:T(8,128)(2,1)S(1)}, u32[]{:S(2)}, u32[]{:S(2)}) collective-permute-start(bf16[176,1536]{1,0:T(8,128)(2,1)} %get-tuple-element.519), channel_id=1, source_target_pairs={{0,2},{1,3},{2,0},{3,1},{4,6},{5,7},{6,4},{7,5},{8,10},{9,11},{10,... | collective-permute-start | bytes 1622024 | tf_op jit(solution)/shard_map/ppermute | solution.py:550
  (146 other events, 1202.0 us)
Sparse Core Ops, SparseCore 0:
  30.5 120.2 all-gather.2
  153.1 66.1 all-gather.4

commit v4 on v3

--- a/solution.py
+++ b/solution.py
@@ -16,6 +16,7 @@
 LN2 = 0.6931471805599453
 NEG = -1e30
 LARGE = 1 << 20
+OUT = pltpu.HBM
 SMALL = pl.CostEstimate(flops=0, transcendentals=0, bytes_accessed=0)
 BF = jnp.bfloat16
 F32 = jnp.float32
@@ -313,18 +314,87 @@
         grid=(1,),
         in_specs=[whole, whole],
         out_specs=[pl.BlockSpec((depth, width), lambda i: (0, 0))] * half,
-        out_shape=(jax.ShapeDtypeStruct((depth, width), BF),) * half,
+        out_shape=(OUT((depth, width), BF),) * half,
         compiler_params=pltpu.CompilerParams(vmem_limit_bytes=24 << 20),
         cost_estimate=SMALL,
         name="fold_pieces",
     )(kept, came)
 
 
-def weight_gradient_kernel(half, slot_ref, near_ref, far_ref, grad_ref, *refs):
+def token_gradient_kernel(own_ref, came_ref, token_ref, through_ref, out_ref):
+    grad = own_ref[...] + came_ref[...].astype(F32)
+    unit = token_ref[...].astype(F32)
+    scale = lax.rsqrt(jnp.mean(unit * unit, axis=-1, keepdims=True) + EPS)
+    unit = unit * scale
+    inner = jnp.mean(grad * unit, axis=-1, keepdims=True)
+    out_ref[:, 0, :] = through_ref[...] + scale * (grad - unit * inner)
+
+
+def token_gradient(own, came, tokens, through):
+    rows, width = own.shape
+    block = 128
+    part = pl.BlockSpec((block, width), lambda i: (i, 0))
+    return kernel_call(
+        token_gradient_kernel,
+        grid=(rows // block,),
+        in_specs=[part] * 4,
+        out_specs=pl.BlockSpec((block, 1, width), lambda i: (i, 0, 0)),
+        out_shape=jax.ShapeDtypeStruct((rows, 1, width), F32),
+        compiler_params=pltpu.CompilerParams(vmem_limit_bytes=24 << 20),
+        cost_estimate=SMALL,
+        name="token_gradient",
+    )(own, came, tokens, through)
+
+
+def query_back_kernel(core_ref, a_ref, b_ref, weight_a_ref, weight_b_ref, own_ref, other_ref):
+    rows = own_ref.shape[0]
+    for out, core in ((other_ref, 1 - core_ref[0]), (own_ref, core_ref[0])):
+        place = pl.ds(pl.multiple_of(core * rows, rows), rows)
+        total = dot(a_ref[place, :], weight_a_ref[...], NT)
+        out[...] = total + dot(b_ref[place, :], weight_b_ref[...], NT)
+
+
+def query_back(core, a, b, weight_a, weight_b):
+    rows, width = a.shape[0] // 2, weight_a.shape[0]
+    whole = [pl.BlockSpec(x.shape, lambda i, s: (0, 0)) for x in (a, b, weight_a, weight_b)]
+    return kernel_call(
+        query_back_kernel,
+        grid_spec=pltpu.PrefetchScalarGridSpec(
+            num_scalar_prefetch=1,
+            grid=(1,),
+            in_specs=whole,
+            out_specs=[pl.BlockSpec((rows, width), lambda i, s: (0, 0))] * 2,
+        ),
+        out_shape=(jax.ShapeDtypeStruct((rows, width), F32),) * 2,
+        compiler_params=pltpu.CompilerParams(vmem_limit_bytes=36 << 20),
+        cost_estimate=SMALL,
+        name="query_back",
+    )(core, a, b, weight_a, weight_b)
+
+
+def spans(parts, block):
+    counts = [part.shape[0] // block for part in parts]
+    return [(sum(counts[:i]), count) for i, count in enumerate(counts)]
+
+
+def part_specs(parts, block, width):
+    def spec(first, count):
+        return pl.BlockSpec((block, width), lambda i: (jnp.clip(i - first, 0, count - 1), 0))
+
+    return [spec(first, count) for first, count in spans(parts, block)]
+
+
+def weight_gradient_kernel(half, slot_ref, *refs):
     part = half // 2
-    rows = near_ref.shape[0]
-    depth = refs[0].shape[0] // part
-    total = dot(near_ref[...], grad_ref[:rows, :], TN) + dot(far_ref[...], grad_ref[rows:, :], TN)
+    outs, grad_ref, parts = refs[-4:], refs[-5], refs[:-5]
+    depth = outs[0].shape[0] // part
+    first = 0
+    total = None
+    for ref in parts:
+        rows = ref.shape[0]
+        term = dot(ref[...], grad_ref[first : first + rows, :], TN)
+        total = term if total is None else total + term
+        first += rows
     total = total.astype(BF)
     count = total.shape[0] // depth
     for at in range(count):
@@ -332,38 +402,56 @@
         k = lax.rem(slot, half)
         target = 2 * (slot // half) + 1 - k // part
         place = pl.ds(pl.multiple_of(lax.rem(k, part) * depth, depth), depth)
-        for i, ref in enumerate(refs):
+        for i, ref in enumerate(outs):
 
             @pl.when(target == i)
             def _(ref=ref, place=place, at=at):
                 ref[place, :] = total[at * depth : (at + 1) * depth, :]
 
 
-def weight_gradient(slots, near, far, grad):
+def weight_gradient(slots, parts, grad):
     half = slots.shape[0] // 2
-    rows, width = near.shape
+    width = parts[0].shape[1]
     hidden = grad.shape[1]
     block = 384
-    tall = pl.BlockSpec((rows, block), lambda i, s: (0, i))
-    out = pl.BlockSpec((width // 4, hidden), lambda i, s: (0, 0))
     pieces = kernel_call(
         functools.partial(weight_gradient_kernel, half),
         grid_spec=pltpu.PrefetchScalarGridSpec(
             num_scalar_prefetch=1,
             grid=(width // block,),
-            in_specs=[
-                tall,
-                tall,
-                pl.BlockSpec(grad.shape, lambda i, s: (0, 0), pipeline_mode=pl.Buffered(1)),
-            ],
-            out_specs=[out] * 4,
+            in_specs=[pl.BlockSpec((part.shape[0], block), lambda i, s: (0, i)) for part in parts]
+            + [pl.BlockSpec(grad.shape, lambda i, s: (0, 0), pipeline_mode=pl.Buffered(1))],
+            out_specs=[pl.BlockSpec((width // 4, hidden), lambda i, s: (0, 0))] * 4,
         ),
-        out_shape=(jax.ShapeDtypeStruct((width // 4, hidden), BF),) * 4,
+        out_shape=(OUT((width // 4, hidden), BF),) * 4,
         compiler_params=pltpu.CompilerParams(vmem_limit_bytes=40 << 20),
         cost_estimate=SMALL,
         name="weight_gradient",
-    )(slots, near, far, grad)
+    )(slots, *parts, grad)
     return pieces[:2], pieces[2:]
+
+
+def combine_kernel(a_ref, b_ref, *outs):
+    first = 0
+    for out in outs:
+        rows = slice(first, first + out.shape[0])
+        out[...] = (a_ref[rows, :].astype(F32) + b_ref[rows, :].astype(F32)).astype(BF)
+        first += out.shape[0]
+
+
+def combine(a, b):
+    rows, width = a.shape
+    whole = pl.BlockSpec((rows, width), lambda i: (0, 0))
+    return kernel_call(
+        combine_kernel,
+        grid=(1,),
+        in_specs=[whole, whole],
+        out_specs=[pl.BlockSpec((rows // 2, width), lambda i: (0, 0))] * 2,
+        out_shape=(jax.ShapeDtypeStruct((rows // 2, width), BF),) * 2,
+        compiler_params=pltpu.CompilerParams(vmem_limit_bytes=16 << 20),
+        cost_estimate=SMALL,
+        name="combine",
+    )(a, b)
 
 
 def gelu_parts(gate):
@@ -375,129 +463,184 @@
     return value, slope
 
 
-def gate_up_block(norm_ref, whole, product_ref, to_gate_ref, to_up_ref):
+def stream(source, whole, sems, cuts, use, axis=1):
+    def at(ref, cut):
+        where = pl.ds(cut[0], cut[1] - cut[0])
+        return ref.at[:, where] if axis else ref.at[where, :]
+
+    copies = [
+        pltpu.make_async_copy(at(source, cut), at(whole, cut), sems.at[i])
+        for i, cut in enumerate(cuts)
+    ]
+
+    @pl.when(pl.program_id(0) == 0)
+    def _():
+        for copy in copies:
+            copy.start()
+        for cut, copy in zip(cuts, copies):
+            copy.wait()
+            use(cut)
+
+    @pl.when(pl.program_id(0) > 0)
+    def _():
+        use((0, cuts[-1][1]))
+
+
+def thirds(width):
+    return [(i * width // 3, (i + 1) * width // 3) for i in range(3)]
+
+
+def gate_up_block(norm_ref, whole, cut, product_ref, to_gate_ref, to_up_ref):
     hidden = product_ref.shape[1]
-    step = 384
-    for start in range(0, hidden, step):
-        cols = slice(start, start + step)
-        gate = dot(norm_ref[...], whole[:, cols])
-        up = dot(norm_ref[...], whole[:, hidden + start : hidden + start + step])
-        value, slope = gelu_parts(gate)
-        product_ref[:, cols] = (value * up).astype(BF)
-        to_gate_ref[:, cols] = (up * slope).astype(BF)
-        to_up_ref[:, cols] = value.astype(BF)
-
-
-def gate_up_kernel(norm_ref, whole_ref, *refs):
-    gate_up_block(norm_ref, whole_ref, *refs[-3:])
-
-
-def apply_gate_up(norm, gate_up, *earlier):
-    rows, width = norm.shape
-    hidden = gate_up.shape[1] // 2
+    cols = slice(*cut)
+    gate = dot(norm_ref[...], whole[:, cols])
+    up = dot(norm_ref[...], whole[:, hidden + cut[0] : hidden + cut[1]])
+    value, slope = gelu_parts(gate)
+    product_ref[:, cols] = (value * up).astype(BF)
+    to_gate_ref[:, cols] = (up * slope).astype(BF)
+    to_up_ref[:, cols] = value.astype(BF)
+
+
+def gate_up_kernel(places, *refs):
+    parts, source = refs[: len(places)], refs[len(places)]
+    outs, whole, sems = refs[-5:-2], refs[-2], refs[-1]
+    hidden = outs[0].shape[1]
+    step = pl.program_id(0)
+    cuts = thirds(hidden)
+    copies = [
+        [
+            pltpu.make_async_copy(
+                source.at[:, pl.ds(side + a, b - a)],
+                whole.at[:, pl.ds(side + a, b - a)],
+                sems.at[2 * i + side // hidden],
+            )
+            for side in (0, hidden)
+        ]
+        for i, (a, b) in enumerate(cuts)
+    ]
+
+    @pl.when(step == 0)
+    def _():
+        for pair in copies:
+            for copy in pair:
+                copy.start()
+        for cut, pair in zip(cuts, copies):
+            for copy in pair:
+                copy.wait()
+            gate_up_block(parts[0], whole, cut, *outs)
+
+    for (first, count), ref in zip(places, parts):
+        inside = (step > 0) & (step >= first) & (step < first + count)
+        pl.when(inside)(functools.partial(gate_up_block, ref, whole, (0, hidden), *outs))
+
+
+def apply_gate_up(parts, gate_up, *earlier):
+    width, hidden = gate_up.shape[0], gate_up.shape[1] // 2
     block = 256
-    steps = rows // block
+    places = spans(parts, block)
+    steps = sum(count for _, count in places)
     skip = steps if earlier else 0
     out = pl.BlockSpec((block, hidden), lambda i: (i + skip, 0))
-    return kernel_call(
-        gate_up_kernel,
+    anywhere = pl.BlockSpec(memory_space=pl.ANY)
+    return kernel_call(
+        functools.partial(gate_up_kernel, places),
         grid=(steps,),
-        in_specs=[
-            pl.BlockSpec((block, width), lambda i: (i, 0)),
-            pl.BlockSpec(gate_up.shape, lambda i: (0, 0), pipeline_mode=pl.Buffered(1)),
-        ]
-        + [pl.BlockSpec(memory_space=pl.ANY)] * len(earlier),
+        in_specs=part_specs(parts, block, width) + [anywhere] * (1 + len(earlier)),
         out_specs=[out, out, out],
-        out_shape=(jax.ShapeDtypeStruct((2 * rows, hidden), BF),) * 3,
-        input_output_aliases={2 + i: i for i in range(len(earlier))},
-        compiler_params=pltpu.CompilerParams(vmem_limit_bytes=36 << 20),
+        out_shape=(OUT((2 * steps * block, hidden), BF),) * 3,
+        scratch_shapes=[pltpu.VMEM(gate_up.shape, BF), pltpu.SemaphoreType.DMA((6,))],
+        input_output_aliases={len(parts) + 1 + i: i for i in range(len(earlier))},
+        compiler_params=pltpu.CompilerParams(vmem_limit_bytes=40 << 20),
         cost_estimate=SMALL,
         name="gate_up_rest" if earlier else "gate_up_first",
-    )(norm, gate_up, *earlier)
-
-
-def product_gradient_kernel(near_ref, far_ref, to_gate_ref, to_up_ref, down_ref, dgate_ref, dup_ref):
-    step = 384
-
-    def block(cot_ref):
-        for start in range(0, down_ref.shape[1], step):
-            cols = slice(start, start + step)
-            grad = dot(cot_ref[...], down_ref[:, cols])
+    )(*parts, gate_up, *earlier)
+
+
+def product_gradient_kernel(places, *refs):
+    parts = refs[: len(places)]
+    to_gate_ref, to_up_ref, source, dgate_ref, dup_ref, whole, sems = refs[len(places) :]
+    at = pl.program_id(0)
+
+    def use(cut):
+        cols = slice(*cut)
+
+        def block(cot_ref):
+            grad = dot(cot_ref[...], whole[:, cols])
             dgate_ref[:, cols] = (grad * to_gate_ref[:, cols].astype(F32)).astype(BF)
             dup_ref[:, cols] = (grad * to_up_ref[:, cols].astype(F32)).astype(BF)
 
-    first = pl.program_id(0) < pl.num_programs(0) // 2
-    pl.when(first)(functools.partial(block, near_ref))
-    pl.when(jnp.logical_not(first))(functools.partial(block, far_ref))
-
-
-def product_gradient(near, far, to_gate, to_up, down):
-    rows, width = near.shape
-    hidden = to_gate.shape[1]
+        if cut[1] - cut[0] < whole.shape[1]:
+            block(parts[0])
+        else:
+            for (first, count), ref in zip(places, parts):
+                pl.when((at >= first) & (at < first + count))(functools.partial(block, ref))
+
+    stream(source, whole, sems, thirds(whole.shape[1]), use)
+
+
+def product_gradient(parts, to_gate, to_up, down):
+    rows, hidden = to_gate.shape
     block = 256
-    steps = rows // block
+    places = spans(parts, block)
     part = pl.BlockSpec((block, hidden), lambda i: (i, 0))
     return kernel_call(
-        product_gradient_kernel,
-        grid=(2 * steps,),
-        in_specs=[
-            pl.BlockSpec((block, width), lambda i: (jnp.minimum(i, steps - 1), 0)),
-            pl.BlockSpec((block, width), lambda i: (jnp.maximum(i - steps, 0), 0)),
-            part,
-            part,
-            pl.BlockSpec(down.shape, lambda i: (0, 0), pipeline_mode=pl.Buffered(1)),
-        ],
+        functools.partial(product_gradient_kernel, places),
+        grid=(rows // block,),
+        in_specs=part_specs(parts, block, down.shape[0])
+        + [part, part, pl.BlockSpec(memory_space=pl.ANY)],
         out_specs=[part, part],
-        out_shape=(jax.ShapeDtypeStruct((2 * rows, hidden), BF),) * 2,
+        out_shape=(OUT((rows, hidden), BF),) * 2,
+        scratch_shapes=[pltpu.VMEM(down.shape, BF), pltpu.SemaphoreType.DMA((3,))],
         compiler_params=pltpu.CompilerParams(vmem_limit_bytes=32 << 20),
         cost_estimate=SMALL,
         name="product_gradient",
-    )(near, far, to_gate, to_up, down)
-
-
-def down_project_kernel(product_ref, down_ref, *outs):
-    for i, out in enumerate(outs):
-
-        @pl.when(pl.program_id(0) // 2 == i)
-        def _(out=out):
-            out[...] = dot(product_ref[...], down_ref[...], NT).astype(BF)
-
-
-def down_project(product, down):
-    rows, hidden = product.shape
-    width = down.shape[0]
-    block = rows // 8
-
-    def spec(i):
-        return pl.BlockSpec((block, width), lambda at: (jnp.clip(at - 2 * i, 0, 1), 0))
-
-    return kernel_call(
-        down_project_kernel,
-        grid=(8,),
-        in_specs=[
-            pl.BlockSpec((block, hidden), lambda at: (at, 0)),
-            pl.BlockSpec(down.shape, lambda at: (0, 0), pipeline_mode=pl.Buffered(1)),
-        ],
-        out_specs=[spec(i) for i in range(4)],
-        out_shape=(jax.ShapeDtypeStruct((rows // 4, width), BF),) * 4,
-        compiler_params=pltpu.CompilerParams(vmem_limit_bytes=24 << 20),
-        cost_estimate=SMALL,
-        name="down_project",
-    )(product, down)
-
-
-def feed_back_kernel(dgate_ref, dup_ref, gate_up_ref, kept_ref, sent_ref):
+    )(*parts, to_gate, to_up, down)
+
+
+def branch_gradients_kernel(branch_ref, mixed_ref, weight_ref, *refs):
+    g_ref, grad_ref = refs[-2:]
+    total = dot(branch_ref[...], mixed_ref[...], TN)
+    if len(refs) > 2:
+        total = total + refs[0][...]
+    g_ref[...] = total.astype(g_ref.dtype)
+    grad_ref[...] = dot(branch_ref[...], weight_ref[...]).astype(BF)
+
+
+def branch_gradients(branch, mixed, weight, *earlier):
+    operands = (branch, mixed, weight, *earlier)
+    whole = [pl.BlockSpec(x.shape, lambda i: (0, 0)) for x in operands]
+    return kernel_call(
+        branch_gradients_kernel,
+        grid=(1,),
+        in_specs=whole,
+        out_specs=[whole[2], whole[1]],
+        out_shape=(
+            jax.ShapeDtypeStruct(weight.shape, BF if earlier else F32),
+            jax.ShapeDtypeStruct(mixed.shape, BF),
+        ),
+        compiler_params=pltpu.CompilerParams(vmem_limit_bytes=32 << 20),
+        cost_estimate=SMALL,
+        name="branch_gradients",
+    )(*operands)
+
+
+def feed_back_kernel(dgate_ref, dup_ref, source, kept_ref, sent_ref, whole, sems):
     hidden = dgate_ref.shape[1]
-    total = dot(dgate_ref[...], gate_up_ref[:, :hidden], NT)
-    total = (total + dot(dup_ref[...], gate_up_ref[:, hidden:], NT)).astype(BF)
-
-    @pl.when(pl.program_id(0) < pl.num_programs(0) // 2)
-    def _():
-        kept_ref[...] = total
-
-    @pl.when(pl.program_id(0) >= pl.num_programs(0) // 2)
-    def _():
-        sent_ref[...] = total
+
+    def use(cut):
+        cols = slice(*cut)
+        total = dot(dgate_ref[...], whole[cols, :hidden], NT)
+        total = (total + dot(dup_ref[...], whole[cols, hidden:], NT)).astype(BF)
+
+        @pl.when(pl.program_id(0) < pl.num_programs(0) // 2)
+        def _():
+            kept_ref[:, cols] = total
+
+        @pl.when(pl.program_id(0) >= pl.num_programs(0) // 2)
+        def _():
+            sent_ref[:, cols] = total
+
+    stream(source, whole, sems, thirds(whole.shape[0]), use, 0)
 
 
 def feed_back(first, rows, dgate, dup, gate_up):
@@ -509,17 +652,14 @@
     return kernel_call(
         feed_back_kernel,
         grid=(steps,),
-        in_specs=[
-            part,
-            part,
-            pl.BlockSpec(gate_up.shape, lambda i: (0, 0), pipeline_mode=pl.Buffered(1)),
-        ],
+        in_specs=[part, part, pl.BlockSpec(memory_space=pl.ANY)],
         out_specs=[
             pl.BlockSpec((block, width), lambda i: (jnp.minimum(i, steps // 2 - 1), 0)),
             pl.BlockSpec((block, width), lambda i: (jnp.maximum(i - steps // 2, 0), 0)),
         ],
         out_shape=(jax.ShapeDtypeStruct((rows // 2, width), BF),) * 2,
-        compiler_params=pltpu.CompilerParams(vmem_limit_bytes=36 << 20),
+        scratch_shapes=[pltpu.VMEM(gate_up.shape, BF), pltpu.SemaphoreType.DMA((3,))],
+        compiler_params=pltpu.CompilerParams(vmem_limit_bytes=40 << 20),
         cost_estimate=SMALL,
         name="feed_back",
     )(dgate, dup, gate_up)
@@ -599,12 +739,12 @@
     unit_other = tp_swap(unit_own, 1)
     cot = cotangent.reshape(4, rows, width)
     cots = [lax.dynamic_index_in_dim(cot, tp ^ k, 0, keepdims=False) for k in range(4)]
-    cot_near, cot_far = jnp.concatenate(cots[:2], 0), jnp.concatenate(cots[2:], 0)
-    send_in, cot_near, cot_far, send_out, send_gate_up, send_down, unit_other, *far_in = sync(
-        send_in, cot_near, cot_far, send_out, send_gate_up, send_down, unit_other, *far_in
-    )
-
+    send_in, send_out, send_down, send_gate_up, unit_other, *pieces = sync(
+        send_in, send_out, send_down, send_gate_up, unit_other, *cots, *far_in
+    )
+    cots, far_in = pieces[:4], pieces[4:]
     gate_up_full = lax.all_gather(send_gate_up, "shard", axis=0, tiled=True)
+
     far_out = far_all(send_out)
     far_in = pack([send_in] + far_in, send_in.shape[1])
     near_in = shards.near(far_in)
@@ -673,95 +813,85 @@
     cut = rows // 2
     norm_core = tp_swap(norm_own, 1)
     norm_x1 = tp_swap(norm_own[:cut], 2)
-    norm_near = jnp.concatenate([norm_own, norm_core], 0)
-    norm_own, norm_near, norm_x1 = sync(norm_own, norm_near, norm_x1)
+    norm_own, norm_core, norm_x1 = sync(norm_own, norm_core, norm_x1)
+    norms = [norm_own, norm_core]
 
     norm_x2 = tp_swap(norm_own[cut:], 2)
     norm_d1 = tp_swap(norm_x1, 1)
-    product, to_gate, to_up = apply_gate_up(norm_near, gate_up_full)
-    norm_x2, norm_d1, product, to_gate, to_up = sync(norm_x2, norm_d1, product, to_gate, to_up)
+    product, to_gate, to_up = apply_gate_up(norms, gate_up_full)
+    norm_x1, norm_x2, norm_d1, product, to_gate, to_up = sync(
+        norm_x1, norm_x2, norm_d1, product, to_gate, to_up
+    )
 
     norm_d2 = tp_swap(norm_x2, 1)
-    norm_far = jnp.concatenate([norm_x1, norm_x2, norm_d1, norm_d2], 0)
-    product, to_gate, to_up = apply_gate_up(norm_far, gate_up_full, product, to_gate, to_up)
-    product, to_gate, to_up, norm_far = sync(product, to_gate, to_up, norm_far)
-    kept_down, sent_down = weight_gradient(shards.slots, cot_near, cot_far, product)
-    cot_near, cot_far, sent, product, norm_far = sync(
-        cot_near, cot_far, sent_down[0], product, norm_far
-    )
-
-    came_down = [shards.near(sent)]
-    dgate, dup = product_gradient(cot_near, cot_far, to_gate, to_up, down_full)
-    dgate, dup, sent, product, *came_down = sync(dgate, dup, sent_down[1], product, *came_down)
-
+    norms += [norm_x1, norm_x2, norm_d1, norm_d2]
+    product, to_gate, to_up = apply_gate_up(norms[2:], gate_up_full, product, to_gate, to_up)
+    kept_down, sent_down = weight_gradient(shards.slots, cots, product)
+    product, to_gate, to_up, *pieces = sync(product, to_gate, to_up, *sent_down, *cots)
+    sent_down, cots = pieces[:2], pieces[2:]
+
+    came_down = [shards.near(sent_down[0])]
+    down_parts = [
+        dot(product[at * rows : (at + 1) * rows], down_full, NT).astype(BF) for at in (3, 2, 1, 0)
+    ][::-1]
+    down_diagonal = tp_swap(down_parts[3], 1)
+    dgate, dup = product_gradient(cots, after(to_gate, *down_parts), to_up, down_full)
+    down_far = combine(down_parts[2], down_diagonal)
+    dgate, dup, *pieces = sync(dgate, dup, sent_down[1], *down_parts, *down_far, *came_down)
+    sent, down_parts, down_far, came_down = pieces[0], pieces[1:5], pieces[5:7], pieces[7:]
+
+    others = [k for k in range(1, half_count) if k != part]
     came_down.append(shards.near(sent))
+    down_came = [tp_swap(down_far[0], 2)]
     sums_down = list(fold(kept_down[0], came_down[0], part))
-    kept_gate, sent_gate = weight_gradient(shards.slots, norm_near, norm_far, dgate)
-    dgate, dup, sent, product, came_down[1], *sums_down = sync(
-        dgate, dup, sent_gate[0], product, came_down[1], *sums_down
-    )
-
-    came_gate = [shards.near(sent)]
     far_sums = [shards.far(sums_down[0], part)]
+    kept_gate, sent_gate = weight_gradient(shards.slots, norms, dgate)
+    back_x, back_diagonal = feed_back(2 * rows, 2 * rows, dgate, dup, gate_up_full)
+    dgate, dup, back_x, back_diagonal, came_down[1], *pieces = sync(
+        dgate, dup, back_x, back_diagonal, came_down[1],
+        *sent_gate, *down_came, *far_sums, *sums_down, *norms
+    )
+    sent_gate, down_came, far_sums, sums_down, norms = (
+        pieces[:2],
+        pieces[2:3],
+        pieces[3:4],
+        pieces[4 : 4 + part],
+        pieces[4 + part :],
+    )
+
+    came_gate = [shards.near(sent_gate[0])]
     sums_down = list(fold(kept_down[1], came_down[1], part)) + sums_down
-    back_x, back_diagonal = feed_back(2 * rows, 2 * rows, dgate, dup, gate_up_full)
-    back_x, back_diagonal, dup, dgate, sent, *pieces = sync(
-        back_x, back_diagonal, dup, dgate, sent_gate[1], *came_gate, *far_sums, *sums_down
-    )
-    came_gate, far_sums, sums_down = pieces[:1], pieces[1:2], pieces[2:]
-
-    others = [k for k in range(1, half_count) if k != part]
+    far_sums += [shards.far(sums_down[k], k) for k in others]
+    back_far = combine(back_x, tp_swap(back_diagonal, 1))
+    back_came = [tp_swap(back_far[0], 2)]
+    kept_up, sent_up = weight_gradient(shards.slots, norms, after(dup, *back_far))
+    dgate, dup, *pieces = sync(
+        dgate, dup, sent_gate[1], back_far[1], *back_came, *came_gate, *sent_up, *far_sums
+    )
+    sent, back_far, back_came, came_gate, sent_up, far_sums_down = (
+        pieces[0],
+        pieces[1],
+        pieces[2:3],
+        pieces[3:4],
+        pieces[4:6],
+        pieces[6:],
+    )
+
     came_gate.append(shards.near(sent))
-    far_sums += [shards.far(sums_down[k], k) for k in others]
-    back_diagonal = tp_swap(back_diagonal, 1)
     sums_gate = list(fold(kept_gate[0], came_gate[0], part))
-    back_far = [
-        (a.astype(F32) + b.astype(F32)).astype(BF)
-        for a, b in (
-            (back_x[:cut], back_diagonal[:cut]),
-            (back_x[cut:], back_diagonal[cut:]),
-        )
-    ]
-    kept_up, sent_up = weight_gradient(shards.slots, norm_near, norm_far, after(dup, *back_far))
-    dgate, dup, sent, *pieces = sync(
-        dgate, dup, sent_up[0], *back_far, came_gate[1], *sums_gate, *far_sums
-    )
-    back_far, came_gate[1], sums_gate, far_sums_down = (
-        pieces[:2],
-        pieces[2],
-        pieces[3 : 3 + part],
-        pieces[3 + part :],
-    )
-
-    back_came = [tp_swap(back_far[0], 2)]
-    came_up = [shards.near(sent)]
     far_sums = [shards.far(sums_gate[0], part)]
+    back_came.append(tp_swap(back_far, 2))
+    back_own, back_core = feed_back(0, 2 * rows, dgate, dup, gate_up_full)
+    back_own, back_core, came_gate[1], down_far[1], *pieces = sync(
+        back_own, back_core, came_gate[1], down_far[1], *back_came, *sent_up, *far_sums, *sums_gate
+    )
+    back_came, sent_up, far_sums, sums_gate = pieces[:2], pieces[2:4], pieces[4:5], pieces[5:]
+
+    came_up = [shards.near(sent_up[0])]
     sums_gate = list(fold(kept_gate[1], came_gate[1], part)) + sums_gate
-    back_own, back_core = feed_back(0, 2 * rows, dgate, dup, gate_up_full)
-    back_own, back_core, product, sent, back_far[1], *pieces = sync(
-        back_own, back_core, product, sent_up[1], back_far[1], *back_came, *came_up, *far_sums, *sums_gate
-    )
-    back_came, came_up, far_sums, sums_gate = pieces[:1], pieces[1:2], pieces[2:3], pieces[3:]
-
-    back_came.append(tp_swap(back_far[1], 2))
-    came_up.append(shards.near(sent))
     far_sums += [shards.far(sums_gate[k], k) for k in others]
+    down_came.append(tp_swap(down_far[1], 2))
     back_core = tp_swap(back_core, 1)
-    sums_up = list(fold(kept_up[0], came_up[0], part))
-    down_parts = down_project(product, down_full)
-    back_own, back_core, *pieces = sync(
-        back_own, back_core, *back_came, came_up[1], *sums_up, *far_sums, *down_parts
-    )
-    back_came, came_up[1], sums_up, far_sums_gate, down_parts = (
-        pieces[:2],
-        pieces[2],
-        pieces[3 : 3 + part],
-        pieces[3 + part : 2 + part + half_count],
-        pieces[2 + part + half_count :],
-    )
-
-    sums_up = list(fold(kept_up[1], came_up[1], part)) + sums_up
-    down_diagonal = tp_swap(down_parts[3], 1)
     grad_norm = (
         back_own.astype(F32)
         + back_core.astype(F32)
@@ -773,25 +903,26 @@
     )
     branch_own = grad_hidden.astype(BF)
     branch_other = tp_swap(branch_own, 1)
-    g_out_b = dot(branch_own, rows_of(mixed_b, 0), TN)
-    grad_own = dot(branch_own, out_full_b).astype(BF)
-    down_far = (down_parts[2].astype(F32) + down_diagonal.astype(F32)).astype(BF)
-    branch_other = after(branch_other, g_out_b, grad_own, down_far)
-    g_out_b = (g_out_b + dot(branch_other, rows_of(mixed_b, 1), TN)).astype(BF)
-    grad_mixed_b = in_order(grad_own, dot(branch_other, out_full_b).astype(BF))
-    grad_mixed_b, g_out_b, down_far, branch_own, branch_other, *sums_up = sync(
-        grad_mixed_b, g_out_b, down_far, branch_own, branch_other, *sums_up
-    )
-
+    g_own, grad_own = branch_gradients(branch_own, rows_of(mixed_b, 0), out_full_b)
+    branch_other = after(branch_other, g_own, grad_own)
+    g_out_b, grad_other = branch_gradients(branch_other, rows_of(mixed_b, 1), out_full_b, g_own)
+    grad_mixed_b = in_order(grad_own, grad_other)
+    grad_mixed_b, g_out_b, branch_own, branch_other, sent, *pieces = sync(
+        grad_mixed_b, g_out_b, branch_own, branch_other, sent_up[1], *came_up, *down_came, *far_sums
+    )
+    came_up, down_came, far_sums_gate = pieces[:1], pieces[1:3], pieces[3:]
+
+    came_up.append(shards.near(sent))
+    sums_up = list(fold(kept_up[0], came_up[0], part))
+    far_sums = [shards.far(sums_up[0], part)]
     g_out_came = tp_swap(g_out_b, 2)
-    far_sums = [shards.far(sums_up[part], part)]
     dq_b, dk_b, dv_b = backward_attention(
         chip_table, query_b, grad_mixed_b, mixed_b, lse_b, keys, keys_t, values
     )
-    dq_b, dk_b, dv_b, g_out_came, branch_own, branch_other, *pieces = sync(
-        dq_b, dk_b, dv_b, g_out_came, branch_own, branch_other, *far_sums, *sums_up
-    )
-    far_sums, sums_up = pieces[:1], pieces[1:]
+    dq_b, dk_b, dv_b, g_out_came, branch_own, branch_other, came_up[1], *pieces = sync(
+        dq_b, dk_b, dv_b, g_out_came, branch_own, branch_other, came_up[1], *far_sums, *sums_up
+    )
+    far_sums, sums_up = pieces[:1], list(fold(kept_up[1], came_up[1], part)) + pieces[1:]
 
     g_query_b = dot(unit, dq_b, TN).astype(BF)
     g_out = (
@@ -822,29 +953,37 @@
     mine = jnp.where(first_core, grad_keys, grad_values)
     theirs = jnp.where(first_core, grad_values, grad_keys).astype(BF)
     theirs = tp_swap(theirs, 1)
-    cuts = [0, rows // 16 * 5, rows // 32 * 21, rows]
-    down_far = [down_far[a:b] for a, b in zip(cuts[:-1], cuts[1:])]
-    down_came = [tp_swap(down_far[0], 2)]
     g_query = (dot(unit, dq_a, TN) + g_query_came.astype(F32)).astype(BF)
     (kept_query,), (sent_query,) = split(places, g_query, half_count)
     sums_out = fold(kept_out, came_out, half_count)
     mine = mine + theirs.astype(F32)
     chip_rows = mine.shape[0] // 2
     mine, own = mine[chip_rows:], mine[:chip_rows].astype(BF)
-    mine, own, sent_query, dq_a, dq_b, down_came[0], down_far[1], down_far[2], *sums_out = sync(
-        mine, own, sent_query, dq_a, dq_b, down_came[0], down_far[1], down_far[2], *sums_out
-    )
+    mine, own, sent_query, dq_a, dq_b, *pieces = sync(
+        mine, own, sent_query, dq_a, dq_b, *sums_out, *far_sums_gate, *far_sums_up, *far_sums_down
+    )
+    sums_out, pieces = pieces[:half_count], pieces[half_count:]
+    far_sums_gate, far_sums_up, far_sums_down = (
+        pieces[at * (half_count - 1) : (at + 1) * (half_count - 1)] for at in range(3)
+    )
+
+    def total(own, others):
+        return functools.reduce(lambda t, o: t + o.astype(F32), others, own.astype(F32))
 
     earlier = lax.ppermute(own, "tp", [(2, 0), (3, 1)])
     came_query = shards.near(sent_query)
     far_out_sums = [shards.far(sums_out[k], k) for k in range(1, half_count)]
-    back_other = dot(rows_of(dq_a, 1), in_query, NT) + dot(rows_of(dq_b, 1), in_query_b, NT)
-    back_own = dot(rows_of(dq_a, 0), in_query, NT) + dot(rows_of(dq_b, 0), in_query_b, NT)
-    back_own, back_other, earlier, came_query, down_far[1], *far_out_sums = sync(
-        back_own, back_other, earlier, came_query, down_far[1], *far_out_sums
-    )
-
-    down_came.append(tp_swap(down_far[1], 2))
+    back_own, back_other = query_back(jnp.reshape(core, (1,)), dq_a, dq_b, in_query, in_query_b)
+    down_core = tp_swap(down_parts[1], 1)
+    sum_gate = total(sums_gate[0], far_sums_gate)
+    sum_up = total(sums_up[0], far_sums_up)
+    grad_w_gate = sum_gate * gain_two
+    grad_w_up = sum_up * gain_two
+    gain_two_part = jnp.sum(own_gate * sum_gate + own_up * sum_up, axis=1)
+    back_own, back_other, earlier, came_query, down_core, grad_w_gate, grad_w_up, gain_two_part, *far_out_sums = sync(
+        back_own, back_other, earlier, came_query, down_core, grad_w_gate, grad_w_up, gain_two_part, *far_out_sums
+    )
+
     grad_half = (mine + earlier.astype(F32)).astype(BF)
     g_half = dot(unit, grad_half, TN).astype(BF)
     (kept_half,), (sent_half,) = split(places, g_half, half_count)
@@ -852,44 +991,27 @@
     in_half = in_full[:, heads:]
     back_other = (back_other + dot(rows_of(grad_half, 1), in_half, NT)).astype(BF)
     back_own = back_own + dot(rows_of(grad_half, 0), in_half, NT)
-    back_other, back_own, kept_half, sent_half, down_came[1], down_far[2], *sums_query = sync(
-        back_other, back_own, kept_half, sent_half, down_came[1], down_far[2], *sums_query
+    back_other, back_own, kept_half, sent_half, *sums_query = sync(
+        back_other, back_own, kept_half, sent_half, *sums_query
     )
 
     came_half = shards.near(sent_half)
     back_came = tp_swap(back_other, 1)
     far_query = [shards.far(sums_query[k], k) for k in range(1, half_count)]
-    down_came.append(tp_swap(down_far[2], 2))
-    down_core = tp_swap(down_parts[1], 1)
-    grad_unit = back_own + back_came.astype(F32)
-    unit_one = inputs * scale_one
-    grad_tokens = grad_hidden + scale_one * (
-        grad_unit - unit_one * jnp.mean(grad_unit * unit_one, axis=-1, keepdims=True)
-    )
-    came_half, grad_tokens, down_core, *pieces = sync(
-        came_half, grad_tokens, down_core, *down_came, *far_query
-    )
-    down_came, far_query = pieces[:3], pieces[3:]
-
-    sums_half = fold(kept_half, came_half, half_count)
-    far_half = [shards.far(sums_half[k], k) for k in range(1, half_count)]
+    grad_tokens = token_gradient(back_own, back_came, tokens.reshape(rows, width), grad_hidden)
+    grad_w_down = jnp.transpose(total(sums_down[0], far_sums_down))
+    grad_w_out = jnp.transpose(total(sums_out[0], far_out_sums))
     output = (
         hidden
         + down_parts[0].astype(F32)
         + down_core.astype(F32)
         + jnp.concatenate(down_came, 0).astype(F32)
     ).astype(BF)
-
-    def total(own, others):
-        return functools.reduce(lambda t, o: t + o.astype(F32), others, own.astype(F32))
-
-    sum_gate = total(sums_gate[0], far_sums_gate)
-    sum_up = total(sums_up[0], far_sums_up)
-    grad_w_gate = sum_gate * gain_two
-    grad_w_up = sum_up * gain_two
-    gain_two_part = jnp.sum(own_gate * sum_gate + own_up * sum_up, axis=1)
-    grad_w_down = jnp.transpose(total(sums_down[0], far_sums_down))
-    grad_w_out = jnp.transpose(total(sums_out[0], far_out_sums))
+    came_half, grad_tokens, output, *far_query = sync(came_half, grad_tokens, output, *far_query)
+
+    sums_half = fold(kept_half, came_half, half_count)
+    far_half = [shards.far(sums_half[k], k) for k in range(1, half_count)]
+
     sum_query = total(sums_query[0], far_query)
     sum_half = total(sums_half[0], far_half)
 
@@ -912,7 +1034,7 @@
     )
     return (
         output.reshape(rows, 1, width),
-        grad_tokens.reshape(rows, 1, width),
+        grad_tokens,
         sum_query * gain_one,
         grad_w_keyval,
         grad_w_out,

time: 546 us -> 526 us (0.963)
  other arithmetic: 53.5 us -> 36.7 us
  starting transfers between devices: 93.3 us -> 78.8 us
  local copies, waits for them, and re-layouts: 48.5 us -> 36.3 us
  Pallas kernels: 168 us -> 180 us
  waiting for transfers between devices: 128 us -> 137 us
    ppermute x24, starting transfers between devices: 52.6 us -> 37.7 us  [far(): lax.ppermute(value, 'shard', [(i, (i // 2 ^ k) * 2 + i % 2) for i in rang...]
    unnamed x208 -> x228, local copies, waits for them, and re-layouts: 38 us -> 23.4 us
    pallas_call x31 -> x36, Pallas kernels: 168 us -> 180 us  [run(): call(*(pltpu.with_memory_space_constraint(x, pltpu.HBM) if x.size > LARGE...]
    ppermute x24, waiting for transfers between devices: 55.1 us -> 60.6 us  [far(): lax.ppermute(value, 'shard', [(i, (i // 2 ^ k) * 2 + i % 2) for i in rang...]
    dot_general x23 -> x19, matrix products: 33.4 us -> 36.1 us  [dot(): return lax.dot_general(a, b, dims, preferred_element_type=F32)]
    ppermute x29 -> x28, waiting for transfers between devices: 50.9 us -> 52.1 us  [tp_swap(): return lax.ppermute(value, 'tp', [(i, i ^ mask) for i in range(4)])]
    ppermute x29 -> x28, starting transfers between devices: 23.6 us -> 23.9 us  [tp_swap(): return lax.ppermute(value, 'tp', [(i, i ^ mask) for i in range(4)])]
  transfers between devices with their start and end apart: 68 -> 67, of which waited for: 28 -> 27; matrix products, arithmetic and copies ran while one was open for 16% -> 11% of each run, Pallas kernels for 31% -> 33%
where the time goes in v4:
time: 526 us; the launch traced here: 520 us
  Pallas kernels  180 us (34%)
  waiting for transfers between devices  137 us (26%)
  starting transfers between devices  78.8 us (15%)
  other arithmetic  36.7 us (7%)
  local copies, waits for them, and re-layouts  36.3 us (7%)
  matrix products  36.1 us (7%)
  between operations  15.7 us (3%)
    pallas_call x36, Pallas kernels, run(): call(*(pltpu.with_memory_space_constraint(x, pltpu.HBM) if x.size > LARGE...  180 us
    ppermute x24, waiting for transfers between devices, far(): lax.ppermute(value, 'shard', [(i, (i // 2 ^ k) * 2 + i % 2) for i in rang...  60.6 us
    ppermute x28, waiting for transfers between devices, tp_swap(): return lax.ppermute(value, 'tp', [(i, i ^ mask) for i in range(4)])  52.1 us
    ppermute x24, starting transfers between devices, far(): lax.ppermute(value, 'shard', [(i, (i // 2 ^ k) * 2 + i % 2) for i in rang...  37.7 us
    dot_general x19, matrix products, dot(): return lax.dot_general(a, b, dims, preferred_element_type=F32)  36.1 us
    ppermute x28, starting transfers between devices, tp_swap(): return lax.ppermute(value, 'tp', [(i, i ^ mask) for i in range(4)])  23.9 us
    unnamed x228, local copies, waits for them, and re-layouts  23.4 us
    all_gather x1, waiting for transfers between devices, local(): down_full = lax.all_gather(send_down, 'shard', axis=0, tiled=True)  13.9 us
  transfers between devices with their start and end apart: 67, of which 27 were waited for; matrix products, arithmetic and copies ran while one was open for 11% of the time, Pallas kernels for 33%

profile of v4, /device:TPU:0, one launch (start us, length us, event | category | flops | bytes accessed | tf_op | source)
XLA Modules:
  0.0 520.4 jit_solution(207178436497878013)
XLA Ops:
  18.6 5.6 %dynamic-slice_bitcast_fusion = (bf16[512,1536]{1,0:T(8,128)(2,1)}, bf16[512,1536]{1,0:T(8,128)(2,1)}, bf16[512,1536]{1,0:T(8,128)(2,1)}, bf16[512,1536]{1,0:T(8,128)(2,1)}) fusion(bf16[4,512,1536]{2,1,0:T(8,128)(2,1)} %bitcast.72, s32[]{:T(128)S(6)} %select_n.133, s32[]{:T(128)S(6)} %select_n.132, s32[]{:T(128)S(6)} %select_n.131, s32[]{:T(128)S(6)} %select_n.130), kind=kLoop, calls=%fused_computation.30 | loop fusion | bytes 12582928 | tf_op jit(solution)/shard_map/jit(dynamic_index_in_dim)/squeeze | solution.py:741
  43.4 11.4 %collective-permute-done.7.refs_2_ = bf16[192,384]{1,0:T(8,128)(2,1)S(1)} collective-permute-done((bf16[192,384]{1,0:T(8,128)(2,1)S(1)}, bf16[192,384]{1,0:T(8,128)(2,1)S(1)}, u32[]{:S(2)}, u32[]{:S(2)}) %collective-permute-start.7) | collective-permute-done | bytes 147488 | tf_op jit(solution)/shard_map/ppermute | solution.py:681
  65.0 5.1 collective-permute-done.10
  78.7 5.8 %attention_forward.2 = (bf16[1024,384]{1,0:T(8,128)(2,1)S(1)}, f32[8,1024]{1,0:T(8,128)S(1)}) custom-call(s32[1]{0:T(128)} %bitcast.1.chip_ref, bf16[1024,512]{1,0:T(8,128)(2,1)S(1)} %copy-done.29, bf16[2048,128]{1,0:T(8,128)(2,1)S(1)} %get-tuple-element.566.k_ref, bf16[128,2048]{1,0:T(8,128)(2,1)S(1)} %copy-done.34), custom_call_target="tpu_custom_call" | custom-call | tf_op jit(solution)/shard_map/attention_forward/pallas_call | solution.py:40
  99.9 5.9 %attention_forward.3 = (bf16[1024,384]{1,0:T(8,128)(2,1)S(1)}, f32[8,1024]{1,0:T(8,128)S(1)}) custom-call(s32[1]{0:T(128)} %bitcast.1.chip_ref, bf16[1024,384]{1,0:T(8,128)(2,1)S(1)} %multiply_convert_fusion.2.q_ref, bf16[2048,128]{1,0:T(8,128)(2,1)S(1)} %get-tuple-element.566.k_ref, bf16[128,2048]{1,0:T(8,128)(2,1)S(1)} %copy-done.35), custom_call_target="tpu_custom_call" | custom-call | tf_op jit(solution)/shard_map/attention_forward/pallas_call | solution.py:40
  114.3 10.6 %collective-permute-done.15.near = bf16[768,384]{1,0:T(8,128)(2,1)S(1)} collective-permute-done((bf16[768,384]{1,0:T(8,128)(2,1)}, bf16[768,384]{1,0:T(8,128)(2,1)S(1)}, u32[]{:S(2)}, u32[]{:S(2)}) %collective-permute-start.15) | collective-permute-done | bytes 589856 | tf_op jit(solution)/shard_map/ppermute | solution.py:690
  136.8 18.2 %collective-permute-done.18.refs_0_.refs_2_ = bf16[256,1536]{1,0:T(8,128)(2,1)} collective-permute-done((bf16[256,1536]{1,0:T(8,128)(2,1)S(1)}, bf16[256,1536]{1,0:T(8,128)(2,1)}, u32[]{:S(2)}, u32[]{:S(2)}) %collective-permute-start.18) | collective-permute-done | bytes 786464 | tf_op jit(solution)/shard_map/ppermute | solution.py:690
  160.2 13.6 %gate_up_first.1 = (bf16[2048,1152]{1,0:T(8,128)(2,1)}, bf16[2048,1152]{1,0:T(8,128)(2,1)}, bf16[2048,1152]{1,0:T(8,128)(2,1)}) custom-call(bf16[512,1536]{1,0:T(8,128)(2,1)S(1)} %multiply_convert_fusion.refs_0_, bf16[512,1536]{1,0:T(8,128)(2,1)S(1)} %copy-done.11, bf16[1536,2304]{1,0:T(8,128)(2,1)} %all-gather.3.cloned.1.call-done.refs_2_.refs_4_.source), custom_call_target="tpu_custom_call" | custom-call | tf_op jit(solution)/shard_map/gate_up_first/pallas_call | solution.py:40
  178.9 14.9 %gate_up_rest.1 = (bf16[2048,1152]{1,0:T(8,128)(2,1)}, bf16[2048,1152]{1,0:T(8,128)(2,1)}, bf16[2048,1152]{1,0:T(8,128)(2,1)}) custom-call(bf16[256,1536]{1,0:T(8,128)(2,1)} %collective-permute-done.18.refs_0_.refs_2_, bf16[256,1536]{1,0:T(8,128)(2,1)} %collective-permute-done.19.refs_1_.refs_3_, ...), custom_call_target="tpu_custom_call", output_to_operand_aliasing={{0}: (5, {}), {1}: (6, {}), {2}: (7, {})} | custom-call | tf_op jit(solution)/shard_map/gate_up_rest/pallas_call | solution.py:40
  193.9 14.9 %weight_gradient.3 = (bf16[384,1152]{1,0:T(8,128)(2,1)}, bf16[384,1152]{1,0:T(8,128)(2,1)}, bf16[384,1152]{1,0:T(8,128)(2,1)}, bf16[384,1152]{1,0:T(8,128)(2,1)}) custom-call(s32[8]{0:T(128)S(1)} %fusion.35.slot_ref, bf16[512,1536]{1,0:T(8,128)(2,1)S(1)} %copy-done.2, bf16[512,1536]{1,0:T(8,128)(2,1)S(1)} %copy-done.8, bf16[512,1536]{1,0:T(8,128)(2,1)S(1)} %copy-done.6, ...), custom_call_target="tpu_custom_call" | custom-call | tf_op jit(solution)/shard_map/weight_gradient/pallas_call | solution.py:40
  208.8 13.9 %all-gather.5.cloned.1.call-done.refs_6_ = bf16[1536,1152]{1,0:T(8,128)(2,1)} async-done(((bf16[192,1152]{1,0:T(8,128)(2,1)}), bf16[1536,1152]{1,0:T(8,128)(2,1)}) %all-gather.5.cloned.1.call-update) | async-done | bytes 3538960 | tf_op jit(solution)/shard_map/all_gather | solution.py:789
  228.1 5.0 convolution_convert_fusion.3
  239.4 16.3 %product_gradient.1 = (bf16[2048,1152]{1,0:T(8,128)(2,1)}, bf16[2048,1152]{1,0:T(8,128)(2,1)}) custom-call(bf16[512,1536]{1,0:T(8,128)(2,1)S(1)} %copy-done.3, bf16[512,1536]{1,0:T(8,128)(2,1)S(1)} %copy-done.9, bf16[512,1536]{1,0:T(8,128)(2,1)S(1)} %copy-done.7, bf16[512,1536]{1,0:T(8,128)(2,1)S(1)} %copy-done.5, ...), custom_call_target="tpu_custom_call" | custom-call | tf_op jit(solution)/shard_map/product_gradient/pallas_call | solution.py:40
  259.8 5.7 %collective-permute-start.26 = (bf16[192,1152]{1,0:T(8,128)(2,1)}, bf16[192,1152]{1,0:T(8,128)(2,1)S(1)}, u32[]{:S(2)}, u32[]{:S(2)}) collective-permute-start(bf16[192,1152]{1,0:T(8,128)(2,1)} %get-tuple-element.376), channel_id=1, source_target_pairs={{0,16},{4,20},{8,24},{12,28},{16,0},{20,4},{24,8},{28,12},{1,17},{... | collective-permute-start | bytes 1327112 | tf_op jit(solution)/shard_map/ppermute | solution.py:681
  265.5 14.9 %weight_gradient.4 = (bf16[384,1152]{1,0:T(8,128)(2,1)}, bf16[384,1152]{1,0:T(8,128)(2,1)}, bf16[384,1152]{1,0:T(8,128)(2,1)}, bf16[384,1152]{1,0:T(8,128)(2,1)}) custom-call(s32[8]{0:T(128)S(1)} %fusion.35.slot_ref, bf16[512,1536]{1,0:T(8,128)(2,1)S(1)} %multiply_convert_fusion.refs_0_, bf16[512,1536]{1,0:T(8,128)(2,1)S(1)} %copy-done.12, ...), custom_call_target="tpu_custom_call" | custom-call | tf_op jit(solution)/shard_map/weight_gradient/pallas_call | solution.py:40
  280.3 12.9 %feed_back.2 = (bf16[512,1536]{1,0:T(8,128)(2,1)S(1)}, bf16[512,1536]{1,0:T(8,128)(2,1)S(1)}) custom-call(bf16[2048,1152]{1,0:T(8,128)(2,1)} %get-tuple-element.400.dgate_ref.refs_6_, bf16[2048,1152]{1,0:T(8,128)(2,1)} %get-tuple-element.401.dup_ref.refs_6_, bf16[1536,2304]{1,0:T(8,128)(2,1)} %all-gather.3.cloned.1.call-done.refs_2_.refs_4_.source), custom_call_target="tpu_custom_call" | custom-call | tf_op jit(solution)/shard_map/feed_back/pallas_call | solution.py:40
  301.1 14.9 %weight_gradient.5 = (bf16[384,1152]{1,0:T(8,128)(2,1)}, bf16[384,1152]{1,0:T(8,128)(2,1)}, bf16[384,1152]{1,0:T(8,128)(2,1)}, bf16[384,1152]{1,0:T(8,128)(2,1)}) custom-call(s32[8]{0:T(128)S(1)} %fusion.35.slot_ref, bf16[512,1536]{1,0:T(8,128)(2,1)S(1)} %multiply_convert_fusion.refs_0_, bf16[512,1536]{1,0:T(8,128)(2,1)S(1)} %copy-done.12, ...), custom_call_target="tpu_custom_call" | custom-call | tf_op jit(solution)/shard_map/weight_gradient/pallas_call | solution.py:40
  316.0 5.3 %collective-permute-done.30 = bf16[192,1152]{1,0:T(8,128)(2,1)S(1)} collective-permute-done((bf16[192,1152]{1,0:T(8,128)(2,1)}, bf16[192,1152]{1,0:T(8,128)(2,1)S(1)}, u32[]{:S(2)}, u32[]{:S(2)}) %collective-permute-start.30) | collective-permute-done | bytes 442400 | tf_op jit(solution)/shard_map/ppermute | solution.py:681
  325.3 13.0 %feed_back.3 = (bf16[512,1536]{1,0:T(8,128)(2,1)S(1)}, bf16[512,1536]{1,0:T(8,128)(2,1)S(1)}) custom-call(bf16[2048,1152]{1,0:T(8,128)(2,1)} %get-tuple-element.400.dgate_ref.refs_6_, bf16[2048,1152]{1,0:T(8,128)(2,1)} %get-tuple-element.401.dup_ref.refs_6_, bf16[1536,2304]{1,0:T(8,128)(2,1)} %all-gather.3.cloned.1.call-done.refs_2_.refs_4_.source), custom_call_target="tpu_custom_call" | custom-call | tf_op jit(solution)/shard_map/feed_back/pallas_call | solution.py:40
  338.3 7.1 %collective-permute-done.34 = bf16[192,1152]{1,0:T(8,128)(2,1)S(1)} collective-permute-done((bf16[192,1152]{1,0:T(8,128)(2,1)}, bf16[192,1152]{1,0:T(8,128)(2,1)S(1)}, u32[]{:S(2)}, u32[]{:S(2)}) %collective-permute-start.34) | collective-permute-done | bytes 442400 | tf_op jit(solution)/shard_map/ppermute | solution.py:681
  363.3 15.3 %collective-permute-done.39 = bf16[192,1152]{1,0:T(8,128)(2,1)S(1)} collective-permute-done((bf16[192,1152]{1,0:T(8,128)(2,1)}, bf16[192,1152]{1,0:T(8,128)(2,1)S(1)}, u32[]{:S(2)}, u32[]{:S(2)}) %collective-permute-start.39) | collective-permute-done | bytes 442400 | tf_op jit(solution)/shard_map/ppermute | solution.py:681
  388.2 11.0 %attention_backward.2 = (bf16[1024,384]{1,0:T(8,128)(2,1)S(1)}, f32[2048,128]{1,0:T(8,128)S(1)}, f32[2048,128]{1,0:T(8,128)S(1)}) custom-call(s32[1]{0:T(128)} %bitcast.1.chip_ref, bf16[1024,384]{1,0:T(8,128)(2,1)S(1)} %copy-done.42, bf16[1024,384]{1,0:T(8,128)(2,1)S(1)} %copy-done.43, bf16[1024,384]{1,0:T(8,128)(2,1)S(1)} %copy-done.46, ...), custom_call_target="tpu_custom_call" | custom-call | tf_op jit(solution)/shard_map/attention_backward/pallas_call | solution.py:40
  422.5 10.8 %attention_backward.3 = (bf16[1024,384]{1,0:T(8,128)(2,1)S(1)}, f32[2048,128]{1,0:T(8,128)S(1)}, f32[2048,128]{1,0:T(8,128)S(1)}) custom-call(s32[1]{0:T(128)} %bitcast.1.chip_ref, bf16[1024,512]{1,0:T(8,128)(2,1)S(1)} %copy-done.30, bf16[1024,384]{1,0:T(8,128)(2,1)S(1)} %maximum_select_fusion.2.g_ref, bf16[1024,384]{1,0:T(8,128)(2,1)S(1)} %copy-done.25, ...), custom_call_target="tpu_custom_call" | custom-call | tf_op jit(solution)/shard_map/attention_backward/pallas_call | solution.py:40
  433.3 6.9 %collective-permute-done.47 = bf16[192,1152]{1,0:T(8,128)(2,1)S(1)} collective-permute-done((bf16[192,1152]{1,0:T(8,128)(2,1)S(1)}, bf16[192,1152]{1,0:T(8,128)(2,1)S(1)}, u32[]{:S(2)}, u32[]{:S(2)}) %collective-permute-start.47) | collective-permute-done | bytes 442400 | tf_op jit(solution)/shard_map/ppermute | solution.py:681
  (460 shorter events, 245.6 us)
Async XLA Ops:
  7.2 151.6 %all-gather.3.cloned.1.call-start = ((), (), s32[]{:S(2)}) async-start(), calls=%async_computation | async-start | bytes 7962624 | tf_op jit(solution)/shard_map/all_gather | solution.py:746
  30.5 192.2 %all-gather.5.cloned.1.call-start = ((), (), s32[]{:S(2)}) async-start(), calls=%async_computation.1 | async-start | bytes 3981312 | tf_op jit(solution)/shard_map/all_gather | solution.py:789
  30.6 24.6 %collective-permute-start.5 = (bf16[768,512]{1,0:T(8,128)(2,1)S(1)}, bf16[768,512]{1,0:T(8,128)(2,1)S(1)}, u32[]{:S(2)}, u32[]{:S(2)}) collective-permute-start(bf16[768,512]{1,0:T(8,128)(2,1)S(1)} %pack_pieces.2.far), channel_id=1, source_target_pairs={{0,4},{4,0},{8,12},{12,8},{16,20},{20,16},{24,28},{28,24},{1,5},{5... | collective-permute-start | bytes 2359304 | tf_op jit(solution)/shard_map/ppermute | solution.py:686
  32.2 22.6 %collective-permute-start.4 = (bf16[768,384]{1,0:T(8,128)(2,1)S(1)}, bf16[768,384]{1,0:T(8,128)(2,1)S(1)}, u32[]{:S(2)}, u32[]{:S(2)}) collective-permute-start(bf16[768,384]{1,0:T(8,128)(2,1)S(1)} %slice.87), channel_id=1, source_target_pairs={{0,2},{1,3},{2,0},{3,1},{4,6},{5,7},{6,4},{7,5},{8,10},{9,11},{10,... | collective-permute-start | bytes 1769480 | tf_op jit(solution)/shard_map/ppermute | solution.py:690
  227.4 28.3 %collective-permute-start.22 = (bf16[512,1536]{1,0:T(8,128)(2,1)S(1)}, bf16[512,1536]{1,0:T(8,128)(2,1)S(1)}, u32[]{:S(2)}, u32[]{:S(2)}) collective-permute-start(bf16[512,1536]{1,0:T(8,128)(2,1)S(1)} %convolution_convert_fusion), channel_id=1, source_target_pairs={{0,1},{1,0},{2,3},{3,2},{4,5},{5,4},{6,7},{7,6},{8,9},{9,8},{10,11... | collective-permute-start | bytes 4718600 | tf_op jit(solution)/shard_map/ppermute | solution.py:690
  227.5 28.6 %collective-permute-start.23 = (bf16[384,1152]{1,0:T(8,128)(2,1)S(1)}, bf16[384,1152]{1,0:T(8,128)(2,1)S(1)}, u32[]{:S(2)}, u32[]{:S(2)}) collective-permute-start(bf16[384,1152]{1,0:T(8,128)(2,1)S(1)} %copy-done.106), channel_id=1, source_target_pairs={{0,4},{4,0},{8,12},{12,8},{16,20},{20,16},{24,28},{28,24},{1,5},{5... | collective-permute-start | bytes 2654216 | tf_op jit(solution)/shard_map/ppermute | solution.py:686
  256.1 37.2 %collective-permute-start.24 = (bf16[384,1152]{1,0:T(8,128)(2,1)S(1)}, bf16[384,1152]{1,0:T(8,128)(2,1)S(1)}, u32[]{:S(2)}, u32[]{:S(2)}) collective-permute-start(bf16[384,1152]{1,0:T(8,128)(2,1)S(1)} %copy-done.104), channel_id=1, source_target_pairs={{0,4},{4,0},{8,12},{12,8},{16,20},{20,16},{24,28},{28,24},{1,5},{5... | collective-permute-start | bytes 2654216 | tf_op jit(solution)/shard_map/ppermute | solution.py:686
  257.3 36.0 %collective-permute-start.25 = (bf16[256,1536]{1,0:T(8,128)(2,1)S(1)}, bf16[256,1536]{1,0:T(8,128)(2,1)S(1)}, u32[]{:S(2)}, u32[]{:S(2)}) collective-permute-start(bf16[256,1536]{1,0:T(8,128)(2,1)S(1)} %get-tuple-element.373), channel_id=1, source_target_pairs={{0,2},{1,3},{2,0},{3,1},{4,6},{5,7},{6,4},{7,5},{8,10},{9,11},{10,... | collective-permute-start | bytes 2359304 | tf_op jit(solution)/shard_map/ppermute | solution.py:690
  259.8 33.5 %collective-permute-start.26 = (bf16[192,1152]{1,0:T(8,128)(2,1)}, bf16[192,1152]{1,0:T(8,128)(2,1)S(1)}, u32[]{:S(2)}, u32[]{:S(2)}) collective-permute-start(bf16[192,1152]{1,0:T(8,128)(2,1)} %get-tuple-element.376), channel_id=1, source_target_pairs={{0,16},{4,20},{8,24},{12,28},{16,0},{20,4},{24,8},{28,12},{1,17},{... | collective-permute-start | bytes 1327112 | tf_op jit(solution)/shard_map/ppermute | solution.py:681
  294.4 26.9 %collective-permute-start.29 = (bf16[384,1152]{1,0:T(8,128)(2,1)S(1)}, bf16[384,1152]{1,0:T(8,128)(2,1)S(1)}, u32[]{:S(2)}, u32[]{:S(2)}) collective-permute-start(bf16[384,1152]{1,0:T(8,128)(2,1)S(1)} %copy-done.105), channel_id=1, source_target_pairs={{0,4},{4,0},{8,12},{12,8},{16,20},{20,16},{24,28},{28,24},{1,5},{5... | collective-permute-start | bytes 2654216 | tf_op jit(solution)/shard_map/ppermute | solution.py:686
  298.1 23.1 %collective-permute-start.28 = (bf16[256,1536]{1,0:T(8,128)(2,1)S(1)}, bf16[256,1536]{1,0:T(8,128)(2,1)S(1)}, u32[]{:S(2)}, u32[]{:S(2)}) collective-permute-start(bf16[256,1536]{1,0:T(8,128)(2,1)S(1)} %get-tuple-element.384), channel_id=1, source_target_pairs={{0,2},{1,3},{2,0},{3,1},{4,6},{5,7},{6,4},{7,5},{8,10},{9,11},{10,... | collective-permute-start | bytes 2359304 | tf_op jit(solution)/shard_map/ppermute | solution.py:690
  299.6 21.6 %collective-permute-start.30 = (bf16[192,1152]{1,0:T(8,128)(2,1)}, bf16[192,1152]{1,0:T(8,128)(2,1)S(1)}, u32[]{:S(2)}, u32[]{:S(2)}) collective-permute-start(bf16[192,1152]{1,0:T(8,128)(2,1)} %get-tuple-element.398), channel_id=1, source_target_pairs={{0,8},{4,12},{8,0},{12,4},{16,24},{20,28},{24,16},{28,20},{1,9},{5... | collective-permute-start | bytes 1327112 | tf_op jit(solution)/shard_map/ppermute | solution.py:681
  299.6 21.6 %collective-permute-start.31 = (bf16[192,1152]{1,0:T(8,128)(2,1)S(1)}, bf16[192,1152]{1,0:T(8,128)(2,1)S(1)}, u32[]{:S(2)}, u32[]{:S(2)}) collective-permute-start(bf16[192,1152]{1,0:T(8,128)(2,1)S(1)} %copy-done.109), channel_id=1, source_target_pairs={{0,24},{4,28},{8,16},{12,20},{16,8},{20,12},{24,0},{28,4},{1,25},{... | collective-permute-start | bytes 1327112 | tf_op jit(solution)/shard_map/ppermute | solution.py:681
  321.3 24.1 %collective-permute-start.32 = (bf16[384,1152]{1,0:T(8,128)(2,1)S(1)}, bf16[384,1152]{1,0:T(8,128)(2,1)S(1)}, u32[]{:S(2)}, u32[]{:S(2)}) collective-permute-start(bf16[384,1152]{1,0:T(8,128)(2,1)S(1)} %copy-done.103), channel_id=1, source_target_pairs={{0,4},{4,0},{8,12},{12,8},{16,20},{20,16},{24,28},{28,24},{1,5},{5... | collective-permute-start | bytes 2654216 | tf_op jit(solution)/shard_map/ppermute | solution.py:686
  322.0 23.4 %collective-permute-start.33 = (bf16[256,1536]{1,0:T(8,128)(2,1)S(1)}, bf16[256,1536]{1,0:T(8,128)(2,1)S(1)}, u32[]{:S(2)}, u32[]{:S(2)}) collective-permute-start(bf16[256,1536]{1,0:T(8,128)(2,1)S(1)} %get-tuple-element.407), channel_id=1, source_target_pairs={{0,2},{1,3},{2,0},{3,1},{4,6},{5,7},{6,4},{7,5},{8,10},{9,11},{10,... | collective-permute-start | bytes 2359304 | tf_op jit(solution)/shard_map/ppermute | solution.py:690
  354.3 24.3 %collective-permute-start.37 = (bf16[384,1152]{1,0:T(8,128)(2,1)S(1)}, bf16[384,1152]{1,0:T(8,128)(2,1)S(1)}, u32[]{:S(2)}, u32[]{:S(2)}) collective-permute-start(bf16[384,1152]{1,0:T(8,128)(2,1)S(1)} %copy-done.102), channel_id=1, source_target_pairs={{0,4},{4,0},{8,12},{12,8},{16,20},{20,16},{24,28},{28,24},{1,5},{5... | collective-permute-start | bytes 2654216 | tf_op jit(solution)/shard_map/ppermute | solution.py:686
  355.6 22.9 %collective-permute-start.38 = (bf16[256,1536]{1,0:T(8,128)(2,1)S(1)}, bf16[256,1536]{1,0:T(8,128)(2,1)S(1)}, u32[]{:S(2)}, u32[]{:S(2)}) collective-permute-start(bf16[256,1536]{1,0:T(8,128)(2,1)S(1)} %get-tuple-element.426), channel_id=1, source_target_pairs={{0,2},{1,3},{2,0},{3,1},{4,6},{5,7},{6,4},{7,5},{8,10},{9,11},{10,... | collective-permute-start | bytes 2359304 | tf_op jit(solution)/shard_map/ppermute | solution.py:690
  357.0 21.6 %collective-permute-start.39 = (bf16[192,1152]{1,0:T(8,128)(2,1)}, bf16[192,1152]{1,0:T(8,128)(2,1)S(1)}, u32[]{:S(2)}, u32[]{:S(2)}) collective-permute-start(bf16[192,1152]{1,0:T(8,128)(2,1)} %get-tuple-element.430), channel_id=1, source_target_pairs={{0,8},{4,12},{8,0},{12,4},{16,24},{20,28},{24,16},{28,20},{1,9},{5... | collective-permute-start | bytes 1327112 | tf_op jit(solution)/shard_map/ppermute | solution.py:681
  357.0 21.6 %collective-permute-start.40 = (bf16[192,1152]{1,0:T(8,128)(2,1)S(1)}, bf16[192,1152]{1,0:T(8,128)(2,1)S(1)}, u32[]{:S(2)}, u32[]{:S(2)}) collective-permute-start(bf16[192,1152]{1,0:T(8,128)(2,1)S(1)} %copy-done.107), channel_id=1, source_target_pairs={{0,24},{4,28},{8,16},{12,20},{16,8},{20,12},{24,0},{28,4},{1,25},{... | collective-permute-start | bytes 1327112 | tf_op jit(solution)/shard_map/ppermute | solution.py:681
  378.6 27.0 %collective-permute-start.41 = (bf16[1536,384]{1,0:T(8,128)(2,1)}, bf16[1536,384]{1,0:T(8,128)(2,1)}, u32[]{:S(2)}, u32[]{:S(2)}) collective-permute-start(bf16[1536,384]{1,0:T(8,128)(2,1)} %get-tuple-element.437), channel_id=1, source_target_pairs={{0,2},{1,3},{2,0},{3,1},{4,6},{5,7},{6,4},{7,5},{8,10},{9,11},{10,... | collective-permute-start | bytes 3538952 | tf_op jit(solution)/shard_map/ppermute | solution.py:690
  380.3 22.6 %collective-permute-start.42 = (bf16[384,1152]{1,0:T(8,128)(2,1)}, bf16[384,1152]{1,0:T(8,128)(2,1)}, u32[]{:S(2)}, u32[]{:S(2)}) collective-permute-start(bf16[384,1152]{1,0:T(8,128)(2,1)} %get-tuple-element.440), channel_id=1, source_target_pairs={{0,4},{4,0},{8,12},{12,8},{16,20},{20,16},{24,28},{28,24},{1,5},{5... | collective-permute-start | bytes 2654216 | tf_op jit(solution)/shard_map/ppermute | solution.py:686
  417.4 25.7 %collective-permute-start.44 = (bf16[1536,384]{1,0:T(8,128)(2,1)S(1)}, bf16[1536,384]{1,0:T(8,128)(2,1)S(1)}, u32[]{:S(2)}, u32[]{:S(2)}) collective-permute-start(bf16[1536,384]{1,0:T(8,128)(2,1)S(1)} %convolution_convert_fusion.4), channel_id=1, source_target_pairs={{0,2},{1,3},{2,0},{3,1},{4,6},{5,7},{6,4},{7,5},{8,10},{9,11},{10,... | collective-permute-start | bytes 3538952 | tf_op jit(solution)/shard_map/ppermute | solution.py:690
  419.1 21.1 %collective-permute-start.45 = (bf16[768,384]{1,0:T(8,128)(2,1)S(1)}, bf16[768,384]{1,0:T(8,128)(2,1)S(1)}, u32[]{:S(2)}, u32[]{:S(2)}) collective-permute-start(bf16[768,384]{1,0:T(8,128)(2,1)S(1)} %get-tuple-element.462), channel_id=1, source_target_pairs={{0,4},{4,0},{8,12},{12,8},{16,20},{20,16},{24,28},{28,24},{1,5},{5... | collective-permute-start | bytes 1769480 | tf_op jit(solution)/shard_map/ppermute | solution.py:686
  422.5 30.6 %collective-permute-start.51 = (bf16[512,1536]{1,0:T(8,128)(2,1)S(1)}, bf16[512,1536]{1,0:T(8,128)(2,1)S(1)}, u32[]{:S(2)}, u32[]{:S(2)}) collective-permute-start(bf16[512,1536]{1,0:T(8,128)(2,1)S(1)} %copy-done.101), channel_id=1, source_target_pairs={{0,1},{1,0},{2,3},{3,2},{4,5},{5,4},{6,7},{7,6},{8,9},{9,8},{10,11... | collective-permute-start | bytes 4718600 | tf_op jit(solution)/shard_map/ppermute | solution.py:690
  (157 other events, 1397.8 us)
Sparse Core Ops, SparseCore 0:
  30.6 123.7 all-gather.2
  156.6 66.0 all-gather.4

commit v5 on v4

--- a/solution.py
+++ b/solution.py
@@ -343,7 +343,7 @@
         compiler_params=pltpu.CompilerParams(vmem_limit_bytes=24 << 20),
         cost_estimate=SMALL,
         name="token_gradient",
-    )(own, came, tokens, through)
+    )(*in_memory(own, came, tokens, through))
 
 
 def query_back_kernel(core_ref, a_ref, b_ref, weight_a_ref, weight_b_ref, own_ref, other_ref):
@@ -370,6 +370,67 @@
         cost_estimate=SMALL,
         name="query_back",
     )(core, a, b, weight_a, weight_b)
+
+
+def in_memory(*operands):
+    return [pltpu.with_memory_space_constraint(x, pltpu.HBM) for x in operands]
+
+
+def finish_gradients_kernel(count, *refs):
+    gate, up = refs[:count], refs[count : 2 * count]
+    own_gate_ref, own_up_ref, gain_ref, gate_ref, up_ref, part_ref = refs[2 * count :]
+    gain = gain_ref[...]
+    part = 0.0
+    for pieces, own, out in ((gate, own_gate_ref, gate_ref), (up, own_up_ref, up_ref)):
+        total = pieces[0][...].astype(F32)
+        for piece in pieces[1:]:
+            total = total + piece[...].astype(F32)
+        out[...] = total * gain
+        part = part + jnp.sum(own[...].astype(F32) * total, axis=1, keepdims=True)
+    part_ref[...] = part
+
+
+def finish_gradients(gate, up, own_gate, own_up, gain):
+    operands = [*gate, *up, own_gate, own_up, gain]
+    whole = [pl.BlockSpec(x.shape, lambda i: (0, 0)) for x in operands]
+    return kernel_call(
+        functools.partial(finish_gradients_kernel, len(gate)),
+        grid=(1,),
+        in_specs=whole,
+        out_specs=[whole[0], whole[0], whole[-1]],
+        out_shape=(
+            OUT(own_gate.shape, F32),
+            OUT(own_gate.shape, F32),
+            jax.ShapeDtypeStruct(gain.shape, F32),
+        ),
+        compiler_params=pltpu.CompilerParams(vmem_limit_bytes=40 << 20),
+        cost_estimate=SMALL,
+        name="finish_gradients",
+    )(*in_memory(*operands[:-1]), gain)
+
+
+def finish_output_kernel(hidden_ref, own_ref, core_ref, *refs):
+    first = 0
+    for ref in refs[:-1]:
+        rows = slice(first, first + ref.shape[0])
+        total = hidden_ref[rows, :] + own_ref[rows, :].astype(F32) + core_ref[rows, :].astype(F32)
+        refs[-1][rows, :] = (total + ref[...].astype(F32)).astype(BF)
+        first += ref.shape[0]
+
+
+def finish_output(hidden, own, core, *came):
+    operands = (hidden, own, core, *came)
+    whole = [pl.BlockSpec(x.shape, lambda i: (0, 0)) for x in operands]
+    return kernel_call(
+        finish_output_kernel,
+        grid=(1,),
+        in_specs=whole,
+        out_specs=whole[0],
+        out_shape=OUT(hidden.shape, BF),
+        compiler_params=pltpu.CompilerParams(vmem_limit_bytes=40 << 20),
+        cost_estimate=SMALL,
+        name="finish_output",
+    )(*in_memory(*operands))
 
 
 def spans(parts, block):
@@ -606,7 +667,7 @@
     grad_ref[...] = dot(branch_ref[...], weight_ref[...]).astype(BF)
 
 
-def branch_gradients(branch, mixed, weight, *earlier):
+def branch_gradients(kind, branch, mixed, weight, *earlier):
     operands = (branch, mixed, weight, *earlier)
     whole = [pl.BlockSpec(x.shape, lambda i: (0, 0)) for x in operands]
     return kernel_call(
@@ -615,7 +676,7 @@
         in_specs=whole,
         out_specs=[whole[2], whole[1]],
         out_shape=(
-            jax.ShapeDtypeStruct(weight.shape, BF if earlier else F32),
+            jax.ShapeDtypeStruct(weight.shape, kind),
             jax.ShapeDtypeStruct(mixed.shape, BF),
         ),
         compiler_params=pltpu.CompilerParams(vmem_limit_bytes=32 << 20),
@@ -769,11 +830,12 @@
     before = lax.ppermute(half, "tp", [(0, 2), (1, 3)])
     far_out = pack([send_out] + far_out, heads)
     near_out = shards.near(far_out)
-    half, half_other, before, far_out, query_near = sync(
-        half, half_other, before, far_out, query_near
-    )
-
     query_near_b = tp_swap(query_near, 2)
+    half, half_other, before, far_out, near_out, query_near_b = sync(
+        half, half_other, before, far_out, near_out, query_near_b
+    )
+
+    out_far_b = tp_swap(far_out, 2)
     before_other = tp_swap(before, 1)
     own_pair = jnp.concatenate([before, half], 0)
     other_pair = jnp.concatenate([before_other, half_other], 0)
@@ -782,24 +844,18 @@
     keys_t = jnp.transpose(keys)
     values_t = jnp.transpose(values)
     mixed_a, lse_a = forward_attention(chip_table, query_half, keys, values_t)
-    mixed_a, query_near_b, far_out, near_out, send_down = sync(
-        mixed_a, query_near_b, far_out, near_out, send_down
-    )
+    mixed_a, out_far_b, send_down, keys_t = sync(mixed_a, out_far_b, send_down, keys_t)
 
     down_full = lax.all_gather(send_down, "shard", axis=0, tiled=True)
-    out_far_b = tp_swap(far_out, 2)
+    out_near_b = tp_swap(near_out, 2)
     in_query_b = unpack(places, query_far_b, query_near_b, half_count)
     query_b = (dot(unit, in_query_b) * (scale * LOG2E)).astype(BF)
     mixed_b, lse_b = forward_attention(chip_table, query_b, keys, values_t)
-    mixed_a, mixed_b, out_far_b, near_out = sync(mixed_a, mixed_b, out_far_b, near_out)
-
-    out_near_b = tp_swap(near_out, 2)
+    mixed_a, mixed_b, out_near_b = sync(mixed_a, mixed_b, out_near_b)
+
     out_full = unpack(places, far_out, near_out, half_count)
     branch_other = dot(rows_of(mixed_a, 1), out_full, NT)
     branch_own = dot(rows_of(mixed_a, 0), out_full, NT)
-    branch_other, branch_own, mixed_b, out_near_b = sync(
-        branch_other, branch_own, mixed_b, out_near_b
-    )
 
     out_full_b = unpack(places, out_far_b, out_near_b, half_count)
     branch_other = (branch_other + dot(rows_of(mixed_b, 1), out_full_b, NT)).astype(BF)
@@ -843,12 +899,13 @@
     others = [k for k in range(1, half_count) if k != part]
     came_down.append(shards.near(sent))
     down_came = [tp_swap(down_far[0], 2)]
+    down_core = tp_swap(down_parts[1], 1)
     sums_down = list(fold(kept_down[0], came_down[0], part))
     far_sums = [shards.far(sums_down[0], part)]
     kept_gate, sent_gate = weight_gradient(shards.slots, norms, dgate)
     back_x, back_diagonal = feed_back(2 * rows, 2 * rows, dgate, dup, gate_up_full)
-    dgate, dup, back_x, back_diagonal, came_down[1], *pieces = sync(
-        dgate, dup, back_x, back_diagonal, came_down[1],
+    dgate, dup, back_x, back_diagonal, down_core, came_down[1], *pieces = sync(
+        dgate, dup, back_x, back_diagonal, down_core, came_down[1],
         *sent_gate, *down_came, *far_sums, *sums_down, *norms
     )
     sent_gate, down_came, far_sums, sums_down, norms = (
@@ -903,12 +960,19 @@
     )
     branch_own = grad_hidden.astype(BF)
     branch_other = tp_swap(branch_own, 1)
-    g_own, grad_own = branch_gradients(branch_own, rows_of(mixed_b, 0), out_full_b)
+    g_own, grad_own = branch_gradients(F32, branch_own, rows_of(mixed_b, 0), out_full_b)
     branch_other = after(branch_other, g_own, grad_own)
-    g_out_b, grad_other = branch_gradients(branch_other, rows_of(mixed_b, 1), out_full_b, g_own)
+    g_out_b, grad_other = branch_gradients(
+        BF, branch_other, rows_of(mixed_b, 1), out_full_b, g_own
+    )
     grad_mixed_b = in_order(grad_own, grad_other)
-    grad_mixed_b, g_out_b, branch_own, branch_other, sent, *pieces = sync(
-        grad_mixed_b, g_out_b, branch_own, branch_other, sent_up[1], *came_up, *down_came, *far_sums
+    g_own, grad_own = branch_gradients(
+        F32, branch_own, rows_of(mixed_a, 0), after(out_full, grad_other)
+    )
+    g_out, grad_other = branch_gradients(F32, branch_other, rows_of(mixed_a, 1), out_full, g_own)
+    grad_mixed_a = in_order(grad_own, grad_other)
+    grad_mixed_b, grad_mixed_a, g_out_b, g_out, sent, *pieces = sync(
+        grad_mixed_b, grad_mixed_a, g_out_b, g_out, sent_up[1], *came_up, *down_came, *far_sums
     )
     came_up, down_came, far_sums_gate = pieces[:1], pieces[1:3], pieces[3:]
 
@@ -919,21 +983,14 @@
     dq_b, dk_b, dv_b = backward_attention(
         chip_table, query_b, grad_mixed_b, mixed_b, lse_b, keys, keys_t, values
     )
-    dq_b, dk_b, dv_b, g_out_came, branch_own, branch_other, came_up[1], *pieces = sync(
-        dq_b, dk_b, dv_b, g_out_came, branch_own, branch_other, came_up[1], *far_sums, *sums_up
+    dq_b, dk_b, dv_b, g_out_came, came_up[1], *pieces = sync(
+        dq_b, dk_b, dv_b, g_out_came, came_up[1], *far_sums, *sums_up
     )
     far_sums, sums_up = pieces[:1], list(fold(kept_up[1], came_up[1], part)) + pieces[1:]
 
     g_query_b = dot(unit, dq_b, TN).astype(BF)
-    g_out = (
-        dot(branch_own, rows_of(mixed_a, 0), TN)
-        + dot(branch_other, rows_of(mixed_a, 1), TN)
-        + g_out_came.astype(F32)
-    )
-    (kept_out,), (sent_out,) = split(places, g_out.astype(BF), half_count)
-    grad_mixed_a = in_order(
-        dot(branch_own, out_full).astype(BF), dot(branch_other, out_full).astype(BF)
-    )
+    g_out = (g_out + g_out_came.astype(F32)).astype(BF)
+    (kept_out,), (sent_out,) = split(places, g_out, half_count)
     g_query_b, sent_out, grad_mixed_a, kept_out, *sums_up = sync(
         g_query_b, sent_out, grad_mixed_a, kept_out, *sums_up
     )
@@ -944,8 +1001,9 @@
     dq_a, dk_a, dv_a = backward_attention(
         chip_table, query_half, grad_mixed_a, mixed_a, lse_a, keys, keys_t, values
     )
-    dq_a, dk_a, dv_a, g_query_came, came_out, *far_sums_up = sync(
-        dq_a, dk_a, dv_a, g_query_came, came_out, *far_sums
+    output = finish_output(hidden, down_parts[0], down_core, *down_came)
+    dq_a, dk_a, dv_a, g_query_came, came_out, output, *far_sums_up = sync(
+        dq_a, dk_a, dv_a, g_query_came, came_out, output, *far_sums
     )
 
     grad_keys = (dk_a + dk_b) * LN2
@@ -974,53 +1032,64 @@
     came_query = shards.near(sent_query)
     far_out_sums = [shards.far(sums_out[k], k) for k in range(1, half_count)]
     back_own, back_other = query_back(jnp.reshape(core, (1,)), dq_a, dq_b, in_query, in_query_b)
-    down_core = tp_swap(down_parts[1], 1)
-    sum_gate = total(sums_gate[0], far_sums_gate)
-    sum_up = total(sums_up[0], far_sums_up)
-    grad_w_gate = sum_gate * gain_two
-    grad_w_up = sum_up * gain_two
-    gain_two_part = jnp.sum(own_gate * sum_gate + own_up * sum_up, axis=1)
-    back_own, back_other, earlier, came_query, down_core, grad_w_gate, grad_w_up, gain_two_part, *far_out_sums = sync(
-        back_own, back_other, earlier, came_query, down_core, grad_w_gate, grad_w_up, gain_two_part, *far_out_sums
+    grad_w_gate, grad_w_up, gain_two_part = finish_gradients(
+        [sums_gate[0], *far_sums_gate],
+        [sums_up[0], *far_sums_up],
+        w_gate.astype(BF),
+        w_up.astype(BF),
+        gain_two,
+    )
+    back_own, back_other, earlier, came_query, grad_w_gate, grad_w_up, gain_two_part, *far_out_sums = sync(
+        back_own,
+        back_other,
+        earlier,
+        came_query,
+        grad_w_gate,
+        grad_w_up,
+        gain_two_part,
+        *far_out_sums,
     )
 
     grad_half = (mine + earlier.astype(F32)).astype(BF)
     g_half = dot(unit, grad_half, TN).astype(BF)
     (kept_half,), (sent_half,) = split(places, g_half, half_count)
     sums_query = fold(kept_query, came_query, half_count)
+    back_other, back_own, grad_half, sent_half, *sums_query = sync(
+        back_other, back_own, grad_half, sent_half, *sums_query
+    )
+
+    came_half = shards.near(sent_half)
+    far_query = [shards.far(sums_query[k], k) for k in range(1, half_count)]
     in_half = in_full[:, heads:]
     back_other = (back_other + dot(rows_of(grad_half, 1), in_half, NT)).astype(BF)
+    back_came = tp_swap(back_other, 1)
     back_own = back_own + dot(rows_of(grad_half, 0), in_half, NT)
-    back_other, back_own, kept_half, sent_half, *sums_query = sync(
-        back_other, back_own, kept_half, sent_half, *sums_query
-    )
-
-    came_half = shards.near(sent_half)
-    back_came = tp_swap(back_other, 1)
-    far_query = [shards.far(sums_query[k], k) for k in range(1, half_count)]
+    came_half, back_own, back_came, sums_down[0], sums_out[0], *far_query = sync(
+        came_half, back_own, back_came, sums_down[0], sums_out[0], *far_query
+    )
+
+    sums_half = fold(kept_half, came_half, half_count)
+    far_half = [shards.far(sums_half[k], k) for k in range(1, half_count)]
+    sums_half = list(sums_half)
+    sums_half[0], back_own, sums_down[0], sums_out[0], *far_half = sync(
+        sums_half[0], back_own, sums_down[0], sums_out[0], *far_half
+    )
+    sum_query = total(sums_query[0], far_query)
+    sum_half = total(sums_half[0], far_half)
+
+    gain_one_part = jnp.sum(own_query * sum_query, axis=1) + jnp.sum(keyval_half * sum_half, axis=1)
+    small = jnp.concatenate(
+        [jnp.transpose(sum_half), gain_one_part[None], jnp.transpose(gain_two_part), jnp.zeros((6, sum_half.shape[0]), F32)], 0
+    )
+    small_came = tp_swap(small, 2)
     grad_tokens = token_gradient(back_own, back_came, tokens.reshape(rows, width), grad_hidden)
+    small, small_came, grad_tokens, sums_down[0], sums_out[0] = sync(
+        small, small_came, grad_tokens, sums_down[0], sums_out[0]
+    )
+    small = small + small_came
+    other = tp_swap(small, 1)
     grad_w_down = jnp.transpose(total(sums_down[0], far_sums_down))
     grad_w_out = jnp.transpose(total(sums_out[0], far_out_sums))
-    output = (
-        hidden
-        + down_parts[0].astype(F32)
-        + down_core.astype(F32)
-        + jnp.concatenate(down_came, 0).astype(F32)
-    ).astype(BF)
-    came_half, grad_tokens, output, *far_query = sync(came_half, grad_tokens, output, *far_query)
-
-    sums_half = fold(kept_half, came_half, half_count)
-    far_half = [shards.far(sums_half[k], k) for k in range(1, half_count)]
-
-    sum_query = total(sums_query[0], far_query)
-    sum_half = total(sums_half[0], far_half)
-
-    gain_one_part = jnp.sum(own_query * sum_query, axis=1) + jnp.sum(keyval_half * sum_half, axis=1)
-    small = jnp.concatenate(
-        [jnp.transpose(sum_half), gain_one_part[None], gain_two_part[None], jnp.zeros((6, sum_half.shape[0]), F32)], 0
-    )
-    small = small + tp_swap(small, 2)
-    other = tp_swap(small, 1)
     gains = small[HD : HD + 2] + other[HD : HD + 2]
     sum_half = jnp.transpose(small[:HD])
     half_swapped = jnp.transpose(other[:HD])

time: 526 us -> 510 us (0.970)
  Pallas kernels: 180 us -> 196 us
  local copies, waits for them, and re-layouts: 36.3 us -> 24.4 us
  waiting for transfers between devices: 137 us -> 127 us
  other arithmetic: 36.7 us -> 29.8 us
    pallas_call x36 -> x40, Pallas kernels: 180 us -> 196 us  [run(): call(*(pltpu.with_memory_space_constraint(x, pltpu.HBM) if x.size > LARGE...]
    unnamed x228 -> x202, local copies, waits for them, and re-layouts: 23.4 us -> 10.3 us
    all_gather x1, waiting for transfers between devices: 13.9 us -> 1.77 us  [local(): down_full = lax.all_gather(send_down, 'shard', axis=0, tiled=True)]
    ppermute x1, waiting for transfers between devices: 5.12 us -> 14 us  [local(): before = lax.ppermute(half, 'tp', [(0, 2), (1, 3)])]
    reduce_sum x3 -> x0, other arithmetic: 6.11 us -> none  [the longest x1 3.03 us: local(): gain_two_part = jnp.sum(own_gate * sum_gate + own_up * sum_up, axis=1)]
    dot_general x19 -> x15, matrix products: 36.1 us -> 36.8 us  [dot(): return lax.dot_general(a, b, dims, preferred_element_type=F32)]
  transfers between devices with their start and end apart: 67 -> 67, of which waited for: 27 -> 25; matrix products, arithmetic and copies ran while one was open for 11% -> 12% of each run, Pallas kernels for 33% -> 38%
where the time goes in v5:
time: 510 us; the launch traced here: 504 us
  Pallas kernels  196 us (38%)
  waiting for transfers between devices  127 us (25%)
  starting transfers between devices  74.2 us (15%)
  matrix products  36.8 us (7%)
  other arithmetic  29.8 us (6%)
  local copies, waits for them, and re-layouts  24.4 us (5%)
  between operations  16.1 us (3%)
    pallas_call x40, Pallas kernels, run(): call(*(pltpu.with_memory_space_constraint(x, pltpu.HBM) if x.size > LARGE...  196 us
    ppermute x24, waiting for transfers between devices, far(): lax.ppermute(value, 'shard', [(i, (i // 2 ^ k) * 2 + i % 2) for i in rang...  58.6 us
    ppermute x28, waiting for transfers between devices, tp_swap(): return lax.ppermute(value, 'tp', [(i, i ^ mask) for i in range(4)])  48.7 us
    dot_general x15, matrix products, dot(): return lax.dot_general(a, b, dims, preferred_element_type=F32)  36.8 us
    ppermute x24, starting transfers between devices, far(): lax.ppermute(value, 'shard', [(i, (i // 2 ^ k) * 2 + i % 2) for i in rang...  36.3 us
    ppermute x28, starting transfers between devices, tp_swap(): return lax.ppermute(value, 'tp', [(i, i ^ mask) for i in range(4)])  20.1 us
    ppermute x1, waiting for transfers between devices, local(): before = lax.ppermute(half, 'tp', [(0, 2), (1, 3)])  14 us
    ppermute x11, starting transfers between devices, near(): return lax.ppermute(value, 'shard', [(i, i ^ 1) for i in range(self.count)])  12.8 us
  transfers between devices with their start and end apart: 67, of which 25 were waited for; matrix products, arithmetic and copies ran while one was open for 12% of the time, Pallas kernels for 38%

profile of v5, /device:TPU:0, one launch (start us, length us, event | category | flops | bytes accessed | tf_op | source)
XLA Modules:
  0.0 503.7 jit_solution(10132057488127662340)
XLA Ops:
  20.3 5.7 %dynamic-slice_bitcast_fusion = (bf16[512,1536]{1,0:T(8,128)(2,1)}, bf16[512,1536]{1,0:T(8,128)(2,1)}, bf16[512,1536]{1,0:T(8,128)(2,1)}, bf16[512,1536]{1,0:T(8,128)(2,1)}) fusion(bf16[4,512,1536]{2,1,0:T(8,128)(2,1)} %bitcast.69, s32[]{:T(128)S(6)} %select_n.132, s32[]{:T(128)S(6)} %select_n.131, s32[]{:T(128)S(6)} %select_n.130, s32[]{:T(128)S(6)} %select_n.129), kind=kLoop, calls=%fused_computation.31 | loop fusion | bytes 12582928 | tf_op jit(solution)/shard_map/jit(dynamic_index_in_dim)/squeeze | solution.py:802
  42.1 12.7 %collective-permute-done.7.refs_2_ = bf16[192,384]{1,0:T(8,128)(2,1)S(1)} collective-permute-done((bf16[192,384]{1,0:T(8,128)(2,1)S(1)}, bf16[192,384]{1,0:T(8,128)(2,1)S(1)}, u32[]{:S(2)}, u32[]{:S(2)}) %collective-permute-start.7) | collective-permute-done | bytes 147488 | tf_op jit(solution)/shard_map/ppermute | solution.py:742
  71.1 14.0 %collective-permute-done.10 = bf16[1024,128]{1,0:T(8,128)(2,1)} collective-permute-done((bf16[1024,128]{1,0:T(8,128)(2,1)S(1)}, bf16[1024,128]{1,0:T(8,128)(2,1)}, u32[]{:S(2)}, u32[]{:S(2)}) %collective-permute-start.10) | collective-permute-done | bytes 262176 | tf_op jit(solution)/shard_map/ppermute | solution.py:830
  85.7 5.0 multiply_convert_fusion.3.q_ref
  98.5 6.0 %attention_forward.2 = (bf16[1024,384]{1,0:T(8,128)(2,1)S(1)}, f32[8,1024]{1,0:T(8,128)S(1)}) custom-call(s32[1]{0:T(128)} %bitcast.chip_ref, bf16[1024,512]{1,0:T(8,128)(2,1)S(1)} %multiply_convert_fusion.1.q_ref, bf16[2048,128]{1,0:T(8,128)(2,1)S(1)} %get-tuple-element.595.k_ref, bf16[128,2048]{1,0:T(8,128)(2,1)S(1)} %copy-done.23), custom_call_target="tpu_custom_call" | custom-call | tf_op jit(solution)/shard_map/attention_forward/pallas_call | solution.py:40
  104.5 5.9 %attention_forward.3 = (bf16[1024,384]{1,0:T(8,128)(2,1)S(1)}, f32[8,1024]{1,0:T(8,128)S(1)}) custom-call(s32[1]{0:T(128)} %bitcast.chip_ref, bf16[1024,384]{1,0:T(8,128)(2,1)S(1)} %copy-done.35, bf16[2048,128]{1,0:T(8,128)(2,1)S(1)} %get-tuple-element.595.k_ref, bf16[128,2048]{1,0:T(8,128)(2,1)S(1)} %copy-done.24), custom_call_target="tpu_custom_call" | custom-call | tf_op jit(solution)/shard_map/attention_forward/pallas_call | solution.py:40
  110.5 9.8 %collective-permute-done.15.near = bf16[768,384]{1,0:T(8,128)(2,1)} collective-permute-done((bf16[768,384]{1,0:T(8,128)(2,1)}, bf16[768,384]{1,0:T(8,128)(2,1)}, u32[]{:S(2)}, u32[]{:S(2)}) %collective-permute-start.15) | collective-permute-done | bytes 589856 | tf_op jit(solution)/shard_map/ppermute | solution.py:751
  138.5 18.2 %collective-permute-done.18.refs_0_.refs_2_ = bf16[256,1536]{1,0:T(8,128)(2,1)} collective-permute-done((bf16[256,1536]{1,0:T(8,128)(2,1)S(1)}, bf16[256,1536]{1,0:T(8,128)(2,1)}, u32[]{:S(2)}, u32[]{:S(2)}) %collective-permute-start.18) | collective-permute-done | bytes 786464 | tf_op jit(solution)/shard_map/ppermute | solution.py:751
  161.9 13.2 %gate_up_first.1 = (bf16[2048,1152]{1,0:T(8,128)(2,1)}, bf16[2048,1152]{1,0:T(8,128)(2,1)}, bf16[2048,1152]{1,0:T(8,128)(2,1)}) custom-call(bf16[512,1536]{1,0:T(8,128)(2,1)S(1)} %multiply_convert_fusion.refs_0_, bf16[512,1536]{1,0:T(8,128)(2,1)S(1)} %copy-done.11, bf16[1536,2304]{1,0:T(8,128)(2,1)} %all-gather.3.cloned.1.call-done.refs_2_.refs_4_.source), custom_call_target="tpu_custom_call" | custom-call | tf_op jit(solution)/shard_map/gate_up_first/pallas_call | solution.py:40
  180.6 15.0 %gate_up_rest.1 = (bf16[2048,1152]{1,0:T(8,128)(2,1)}, bf16[2048,1152]{1,0:T(8,128)(2,1)}, bf16[2048,1152]{1,0:T(8,128)(2,1)}) custom-call(bf16[256,1536]{1,0:T(8,128)(2,1)} %collective-permute-done.18.refs_0_.refs_2_, bf16[256,1536]{1,0:T(8,128)(2,1)} %collective-permute-done.19.refs_1_.refs_3_, ...), custom_call_target="tpu_custom_call", output_to_operand_aliasing={{0}: (5, {}), {1}: (6, {}), {2}: (7, {})} | custom-call | tf_op jit(solution)/shard_map/gate_up_rest/pallas_call | solution.py:40
  195.7 14.9 %weight_gradient.3 = (bf16[384,1152]{1,0:T(8,128)(2,1)}, bf16[384,1152]{1,0:T(8,128)(2,1)}, bf16[384,1152]{1,0:T(8,128)(2,1)}, bf16[384,1152]{1,0:T(8,128)(2,1)}) custom-call(s32[8]{0:T(128)S(1)} %fusion.22.slot_ref, bf16[512,1536]{1,0:T(8,128)(2,1)S(1)} %copy-done.2, bf16[512,1536]{1,0:T(8,128)(2,1)S(1)} %copy-done.8, bf16[512,1536]{1,0:T(8,128)(2,1)S(1)} %copy-done.6, ...), custom_call_target="tpu_custom_call" | custom-call | tf_op jit(solution)/shard_map/weight_gradient/pallas_call | solution.py:40
  227.8 16.2 %product_gradient.1 = (bf16[2048,1152]{1,0:T(8,128)(2,1)}, bf16[2048,1152]{1,0:T(8,128)(2,1)}) custom-call(bf16[512,1536]{1,0:T(8,128)(2,1)S(1)} %copy-done.3, bf16[512,1536]{1,0:T(8,128)(2,1)S(1)} %copy-done.9, bf16[512,1536]{1,0:T(8,128)(2,1)S(1)} %copy-done.7, bf16[512,1536]{1,0:T(8,128)(2,1)S(1)} %copy-done.5, ...), custom_call_target="tpu_custom_call" | custom-call | tf_op jit(solution)/shard_map/product_gradient/pallas_call | solution.py:40
  250.1 14.9 %weight_gradient.4 = (bf16[384,1152]{1,0:T(8,128)(2,1)}, bf16[384,1152]{1,0:T(8,128)(2,1)}, bf16[384,1152]{1,0:T(8,128)(2,1)}, bf16[384,1152]{1,0:T(8,128)(2,1)}) custom-call(s32[8]{0:T(128)S(1)} %fusion.22.slot_ref, bf16[512,1536]{1,0:T(8,128)(2,1)S(1)} %multiply_convert_fusion.refs_0_, bf16[512,1536]{1,0:T(8,128)(2,1)S(1)} %copy-done.12, ...), custom_call_target="tpu_custom_call" | custom-call | tf_op jit(solution)/shard_map/weight_gradient/pallas_call | solution.py:40
  264.9 13.2 %feed_back.2 = (bf16[512,1536]{1,0:T(8,128)(2,1)S(1)}, bf16[512,1536]{1,0:T(8,128)(2,1)S(1)}) custom-call(bf16[2048,1152]{1,0:T(8,128)(2,1)} %get-tuple-element.413.dgate_ref.refs_6_, bf16[2048,1152]{1,0:T(8,128)(2,1)} %get-tuple-element.414.dup_ref.refs_6_, bf16[1536,2304]{1,0:T(8,128)(2,1)} %all-gather.3.cloned.1.call-done.refs_2_.refs_4_.source), custom_call_target="tpu_custom_call" | custom-call | tf_op jit(solution)/shard_map/feed_back/pallas_call | solution.py:40
  287.4 14.9 %weight_gradient.5 = (bf16[384,1152]{1,0:T(8,128)(2,1)}, bf16[384,1152]{1,0:T(8,128)(2,1)}, bf16[384,1152]{1,0:T(8,128)(2,1)}, bf16[384,1152]{1,0:T(8,128)(2,1)}) custom-call(s32[8]{0:T(128)S(1)} %fusion.22.slot_ref, bf16[512,1536]{1,0:T(8,128)(2,1)S(1)} %multiply_convert_fusion.refs_0_, bf16[512,1536]{1,0:T(8,128)(2,1)S(1)} %copy-done.12, ...), custom_call_target="tpu_custom_call" | custom-call | tf_op jit(solution)/shard_map/weight_gradient/pallas_call | solution.py:40
  310.5 13.0 %feed_back.3 = (bf16[512,1536]{1,0:T(8,128)(2,1)S(1)}, bf16[512,1536]{1,0:T(8,128)(2,1)S(1)}) custom-call(bf16[2048,1152]{1,0:T(8,128)(2,1)} %get-tuple-element.413.dgate_ref.refs_6_, bf16[2048,1152]{1,0:T(8,128)(2,1)} %get-tuple-element.414.dup_ref.refs_6_, bf16[1536,2304]{1,0:T(8,128)(2,1)} %all-gather.3.cloned.1.call-done.refs_2_.refs_4_.source), custom_call_target="tpu_custom_call" | custom-call | tf_op jit(solution)/shard_map/feed_back/pallas_call | solution.py:40
  323.5 7.5 %collective-permute-done.35.refs_1_ = bf16[192,1152]{1,0:T(8,128)(2,1)S(1)} collective-permute-done((bf16[192,1152]{1,0:T(8,128)(2,1)}, bf16[192,1152]{1,0:T(8,128)(2,1)S(1)}, u32[]{:S(2)}, u32[]{:S(2)}) %collective-permute-start.35) | collective-permute-done | bytes 442400 | tf_op jit(solution)/shard_map/ppermute | solution.py:742
  355.7 8.6 %collective-permute-done.41.refs_3_ = bf16[192,1152]{1,0:T(8,128)(2,1)S(1)} collective-permute-done((bf16[192,1152]{1,0:T(8,128)(2,1)S(1)}, bf16[192,1152]{1,0:T(8,128)(2,1)S(1)}, u32[]{:S(2)}, u32[]{:S(2)}) %collective-permute-start.41) | collective-permute-done | bytes 442400 | tf_op jit(solution)/shard_map/ppermute | solution.py:742
  371.0 10.8 %attention_backward.2 = (bf16[1024,384]{1,0:T(8,128)(2,1)S(1)}, f32[2048,128]{1,0:T(8,128)S(1)}, f32[2048,128]{1,0:T(8,128)S(1)}) custom-call(s32[1]{0:T(128)} %bitcast.chip_ref, bf16[1024,384]{1,0:T(8,128)(2,1)S(1)} %copy-done.36, bf16[1024,384]{1,0:T(8,128)(2,1)S(1)} %copy-done.40, bf16[1024,384]{1,0:T(8,128)(2,1)S(1)} %copy-done.38, ...), custom_call_target="tpu_custom_call" | custom-call | tf_op jit(solution)/shard_map/attention_backward/pallas_call | solution.py:40
  381.8 6.9 %collective-permute-done.44.refs_5_ = bf16[192,1152]{1,0:T(8,128)(2,1)} collective-permute-done((bf16[192,1152]{1,0:T(8,128)(2,1)}, bf16[192,1152]{1,0:T(8,128)(2,1)}, u32[]{:S(2)}, u32[]{:S(2)}) %collective-permute-start.44) | collective-permute-done | bytes 442400 | tf_op jit(solution)/shard_map/ppermute | solution.py:742
  402.7 5.0 finish_output.1
  407.7 10.7 %attention_backward.3 = (bf16[1024,384]{1,0:T(8,128)(2,1)S(1)}, f32[2048,128]{1,0:T(8,128)S(1)}, f32[2048,128]{1,0:T(8,128)S(1)}) custom-call(s32[1]{0:T(128)} %bitcast.chip_ref, bf16[1024,512]{1,0:T(8,128)(2,1)S(1)} %copy-done.20, bf16[1024,384]{1,0:T(8,128)(2,1)S(1)} %copy-done.39, bf16[1024,384]{1,0:T(8,128)(2,1)S(1)} %copy-done.34, ...), custom_call_target="tpu_custom_call" | custom-call | tf_op jit(solution)/shard_map/attention_backward/pallas_call | solution.py:40
  462.9 7.4 %collective-permute-done.58 = bf16[192,384]{1,0:T(8,128)(2,1)S(1)} collective-permute-done((bf16[192,384]{1,0:T(8,128)(2,1)S(1)}, bf16[192,384]{1,0:T(8,128)(2,1)S(1)}, u32[]{:S(2)}, u32[]{:S(2)}) %collective-permute-start.58) | collective-permute-done | bytes 147488 | tf_op jit(solution)/shard_map/ppermute | solution.py:742
  485.1 6.6 %token_gradient.1 = f32[512,1,1536]{2,1,0:T(1,128)} custom-call(f32[512,1536]{1,0:T(8,128)} %convolution_add_fusion.1.own_ref, bf16[512,1536]{1,0:T(8,128)(2,1)} %copy-done.68, bf16[512,1536]{1,0:T(8,128)(2,1)} %bitcast.68, f32[512,1536]{1,0:T(8,128)} %get-tuple-element.589.through_ref), custom_call_target="tpu_custom_call" | custom-call | tf_op jit(solution)/shard_map/token_gradient/pallas_call | solution.py:40
  (430 shorter events, 231.6 us)
Async XLA Ops:
  7.2 153.3 %all-gather.3.cloned.1.call-start = ((), (), s32[]{:S(2)}) async-start(), calls=%async_computation | async-start | bytes 7962624 | tf_op jit(solution)/shard_map/all_gather | solution.py:807
  30.4 181.9 %all-gather.5.cloned.1.call-start = ((), (), s32[]{:S(2)}) async-start(), calls=%async_computation.1 | async-start | bytes 3981312 | tf_op jit(solution)/shard_map/all_gather | solution.py:849
  30.5 27.8 %collective-permute-start.5 = (bf16[768,512]{1,0:T(8,128)(2,1)S(1)}, bf16[768,512]{1,0:T(8,128)(2,1)S(1)}, u32[]{:S(2)}, u32[]{:S(2)}) collective-permute-start(bf16[768,512]{1,0:T(8,128)(2,1)S(1)} %pack_pieces.2.far), channel_id=1, source_target_pairs={{0,4},{4,0},{8,12},{12,8},{16,20},{20,16},{24,28},{28,24},{1,5},{5... | collective-permute-start | bytes 2359304 | tf_op jit(solution)/shard_map/ppermute | solution.py:747
  32.3 22.6 %collective-permute-start.4 = (bf16[768,384]{1,0:T(8,128)(2,1)S(1)}, bf16[768,384]{1,0:T(8,128)(2,1)S(1)}, u32[]{:S(2)}, u32[]{:S(2)}) collective-permute-start(bf16[768,384]{1,0:T(8,128)(2,1)S(1)} %slice.87), channel_id=1, source_target_pairs={{0,2},{1,3},{2,0},{3,1},{4,6},{5,7},{6,4},{7,5},{8,10},{9,11},{10,... | collective-permute-start | bytes 1769480 | tf_op jit(solution)/shard_map/ppermute | solution.py:751
  63.9 21.1 %collective-permute-start.11 = (bf16[768,384]{1,0:T(8,128)(2,1)}, bf16[768,384]{1,0:T(8,128)(2,1)}, u32[]{:S(2)}, u32[]{:S(2)}) collective-permute-start(bf16[768,384]{1,0:T(8,128)(2,1)} %pack_pieces.3.far), channel_id=1, source_target_pairs={{0,4},{4,0},{8,12},{12,8},{16,20},{20,16},{24,28},{28,24},{1,5},{5... | collective-permute-start | bytes 1769480 | tf_op jit(solution)/shard_map/ppermute | solution.py:747
  93.3 26.9 %collective-permute-start.15 = (bf16[768,384]{1,0:T(8,128)(2,1)}, bf16[768,384]{1,0:T(8,128)(2,1)}, u32[]{:S(2)}, u32[]{:S(2)}) collective-permute-start(bf16[768,384]{1,0:T(8,128)(2,1)} %collective-permute-done.11.near), channel_id=1, source_target_pairs={{0,2},{1,3},{2,0},{3,1},{4,6},{5,7},{6,4},{7,5},{8,10},{9,11},{10,... | collective-permute-start | bytes 1769480 | tf_op jit(solution)/shard_map/ppermute | solution.py:751
  217.0 27.0 %collective-permute-start.22 = (bf16[512,1536]{1,0:T(8,128)(2,1)S(1)}, bf16[512,1536]{1,0:T(8,128)(2,1)S(1)}, u32[]{:S(2)}, u32[]{:S(2)}) collective-permute-start(bf16[512,1536]{1,0:T(8,128)(2,1)S(1)} %convolution_convert_fusion), channel_id=1, source_target_pairs={{0,1},{1,0},{2,3},{3,2},{4,5},{5,4},{6,7},{7,6},{8,9},{9,8},{10,11... | collective-permute-start | bytes 4718600 | tf_op jit(solution)/shard_map/ppermute | solution.py:751
  217.1 27.3 %collective-permute-start.23 = (bf16[384,1152]{1,0:T(8,128)(2,1)S(1)}, bf16[384,1152]{1,0:T(8,128)(2,1)S(1)}, u32[]{:S(2)}, u32[]{:S(2)}) collective-permute-start(bf16[384,1152]{1,0:T(8,128)(2,1)S(1)} %copy-done.93), channel_id=1, source_target_pairs={{0,4},{4,0},{8,12},{12,8},{16,20},{20,16},{24,28},{28,24},{1,5},{5... | collective-permute-start | bytes 2654216 | tf_op jit(solution)/shard_map/ppermute | solution.py:747
  244.4 33.8 %collective-permute-start.24 = (bf16[512,1536]{1,0:T(8,128)(2,1)S(1)}, bf16[512,1536]{1,0:T(8,128)(2,1)S(1)}, u32[]{:S(2)}, u32[]{:S(2)}) collective-permute-start(bf16[512,1536]{1,0:T(8,128)(2,1)S(1)} %convolution_convert_fusion.2), channel_id=1, source_target_pairs={{0,1},{1,0},{2,3},{3,2},{4,5},{5,4},{6,7},{7,6},{8,9},{9,8},{10,11... | collective-permute-start | bytes 4718600 | tf_op jit(solution)/shard_map/ppermute | solution.py:751
  244.5 33.7 %collective-permute-start.25 = (bf16[384,1152]{1,0:T(8,128)(2,1)S(1)}, bf16[384,1152]{1,0:T(8,128)(2,1)S(1)}, u32[]{:S(2)}, u32[]{:S(2)}) collective-permute-start(bf16[384,1152]{1,0:T(8,128)(2,1)S(1)} %copy-done.91), channel_id=1, source_target_pairs={{0,4},{4,0},{8,12},{12,8},{16,20},{20,16},{24,28},{28,24},{1,5},{5... | collective-permute-start | bytes 2654216 | tf_op jit(solution)/shard_map/ppermute | solution.py:747
  245.8 32.4 %collective-permute-start.26 = (bf16[256,1536]{1,0:T(8,128)(2,1)S(1)}, bf16[256,1536]{1,0:T(8,128)(2,1)S(1)}, u32[]{:S(2)}, u32[]{:S(2)}) collective-permute-start(bf16[256,1536]{1,0:T(8,128)(2,1)S(1)} %get-tuple-element.386), channel_id=1, source_target_pairs={{0,2},{1,3},{2,0},{3,1},{4,6},{5,7},{6,4},{7,5},{8,10},{9,11},{10,... | collective-permute-start | bytes 2359304 | tf_op jit(solution)/shard_map/ppermute | solution.py:751
  248.2 29.9 %collective-permute-start.27 = (bf16[192,1152]{1,0:T(8,128)(2,1)}, bf16[192,1152]{1,0:T(8,128)(2,1)S(1)}, u32[]{:S(2)}, u32[]{:S(2)}) collective-permute-start(bf16[192,1152]{1,0:T(8,128)(2,1)} %get-tuple-element.389), channel_id=1, source_target_pairs={{0,16},{4,20},{8,24},{12,28},{16,0},{20,4},{24,8},{28,12},{1,17},{... | collective-permute-start | bytes 1327112 | tf_op jit(solution)/shard_map/ppermute | solution.py:742
  279.4 27.7 %collective-permute-start.30 = (bf16[384,1152]{1,0:T(8,128)(2,1)S(1)}, bf16[384,1152]{1,0:T(8,128)(2,1)S(1)}, u32[]{:S(2)}, u32[]{:S(2)}) collective-permute-start(bf16[384,1152]{1,0:T(8,128)(2,1)S(1)} %copy-done.92), channel_id=1, source_target_pairs={{0,4},{4,0},{8,12},{12,8},{16,20},{20,16},{24,28},{28,24},{1,5},{5... | collective-permute-start | bytes 2654216 | tf_op jit(solution)/shard_map/ppermute | solution.py:747
  283.2 23.9 %collective-permute-start.29 = (bf16[256,1536]{1,0:T(8,128)(2,1)S(1)}, bf16[256,1536]{1,0:T(8,128)(2,1)S(1)}, u32[]{:S(2)}, u32[]{:S(2)}) collective-permute-start(bf16[256,1536]{1,0:T(8,128)(2,1)S(1)} %get-tuple-element.397), channel_id=1, source_target_pairs={{0,2},{1,3},{2,0},{3,1},{4,6},{5,7},{6,4},{7,5},{8,10},{9,11},{10,... | collective-permute-start | bytes 2359304 | tf_op jit(solution)/shard_map/ppermute | solution.py:751
  285.6 21.4 %collective-permute-start.32 = (bf16[192,1152]{1,0:T(8,128)(2,1)S(1)}, bf16[192,1152]{1,0:T(8,128)(2,1)S(1)}, u32[]{:S(2)}, u32[]{:S(2)}) collective-permute-start(bf16[192,1152]{1,0:T(8,128)(2,1)S(1)} %copy-done.96), channel_id=1, source_target_pairs={{0,24},{4,28},{8,16},{12,20},{16,8},{20,12},{24,0},{28,4},{1,25},{... | collective-permute-start | bytes 1327112 | tf_op jit(solution)/shard_map/ppermute | solution.py:742
  307.1 24.0 %collective-permute-start.33 = (bf16[384,1152]{1,0:T(8,128)(2,1)S(1)}, bf16[384,1152]{1,0:T(8,128)(2,1)S(1)}, u32[]{:S(2)}, u32[]{:S(2)}) collective-permute-start(bf16[384,1152]{1,0:T(8,128)(2,1)S(1)} %copy-done.90), channel_id=1, source_target_pairs={{0,4},{4,0},{8,12},{12,8},{16,20},{20,16},{24,28},{28,24},{1,5},{5... | collective-permute-start | bytes 2654216 | tf_op jit(solution)/shard_map/ppermute | solution.py:747
  308.0 23.1 %collective-permute-start.34 = (bf16[256,1536]{1,0:T(8,128)(2,1)S(1)}, bf16[256,1536]{1,0:T(8,128)(2,1)S(1)}, u32[]{:S(2)}, u32[]{:S(2)}) collective-permute-start(bf16[256,1536]{1,0:T(8,128)(2,1)S(1)} %get-tuple-element.420), channel_id=1, source_target_pairs={{0,2},{1,3},{2,0},{3,1},{4,6},{5,7},{6,4},{7,5},{8,10},{9,11},{10,... | collective-permute-start | bytes 2359304 | tf_op jit(solution)/shard_map/ppermute | solution.py:751
  339.9 24.4 %collective-permute-start.38 = (bf16[384,1152]{1,0:T(8,128)(2,1)S(1)}, bf16[384,1152]{1,0:T(8,128)(2,1)S(1)}, u32[]{:S(2)}, u32[]{:S(2)}) collective-permute-start(bf16[384,1152]{1,0:T(8,128)(2,1)S(1)} %copy-done.89), channel_id=1, source_target_pairs={{0,4},{4,0},{8,12},{12,8},{16,20},{20,16},{24,28},{28,24},{1,5},{5... | collective-permute-start | bytes 2654216 | tf_op jit(solution)/shard_map/ppermute | solution.py:747
  341.3 23.0 %collective-permute-start.39 = (bf16[256,1536]{1,0:T(8,128)(2,1)S(1)}, bf16[256,1536]{1,0:T(8,128)(2,1)S(1)}, u32[]{:S(2)}, u32[]{:S(2)}) collective-permute-start(bf16[256,1536]{1,0:T(8,128)(2,1)S(1)} %get-tuple-element.444), channel_id=1, source_target_pairs={{0,2},{1,3},{2,0},{3,1},{4,6},{5,7},{6,4},{7,5},{8,10},{9,11},{10,... | collective-permute-start | bytes 2359304 | tf_op jit(solution)/shard_map/ppermute | solution.py:751
  342.7 21.6 %collective-permute-start.41 = (bf16[192,1152]{1,0:T(8,128)(2,1)S(1)}, bf16[192,1152]{1,0:T(8,128)(2,1)S(1)}, u32[]{:S(2)}, u32[]{:S(2)}) collective-permute-start(bf16[192,1152]{1,0:T(8,128)(2,1)S(1)} %copy-done.94), channel_id=1, source_target_pairs={{0,24},{4,28},{8,16},{12,20},{16,8},{20,12},{24,0},{28,4},{1,25},{... | collective-permute-start | bytes 1327112 | tf_op jit(solution)/shard_map/ppermute | solution.py:742
  364.3 27.4 %collective-permute-start.42 = (bf16[1536,384]{1,0:T(8,128)(2,1)}, bf16[1536,384]{1,0:T(8,128)(2,1)}, u32[]{:S(2)}, u32[]{:S(2)}) collective-permute-start(bf16[1536,384]{1,0:T(8,128)(2,1)} %get-tuple-element.456), channel_id=1, source_target_pairs={{0,2},{1,3},{2,0},{3,1},{4,6},{5,7},{6,4},{7,5},{8,10},{9,11},{10,... | collective-permute-start | bytes 3538952 | tf_op jit(solution)/shard_map/ppermute | solution.py:751
  366.1 22.7 %collective-permute-start.43 = (bf16[384,1152]{1,0:T(8,128)(2,1)}, bf16[384,1152]{1,0:T(8,128)(2,1)}, u32[]{:S(2)}, u32[]{:S(2)}) collective-permute-start(bf16[384,1152]{1,0:T(8,128)(2,1)} %get-tuple-element.457), channel_id=1, source_target_pairs={{0,4},{4,0},{8,12},{12,8},{16,20},{20,16},{24,28},{28,24},{1,5},{5... | collective-permute-start | bytes 2654216 | tf_op jit(solution)/shard_map/ppermute | solution.py:747
  367.8 20.9 %collective-permute-start.44 = (bf16[192,1152]{1,0:T(8,128)(2,1)}, bf16[192,1152]{1,0:T(8,128)(2,1)}, u32[]{:S(2)}, u32[]{:S(2)}) collective-permute-start(bf16[192,1152]{1,0:T(8,128)(2,1)} %get-tuple-element.460), channel_id=1, source_target_pairs={{0,16},{4,20},{8,24},{12,28},{16,0},{20,4},{24,8},{28,12},{1,17},{... | collective-permute-start | bytes 1327112 | tf_op jit(solution)/shard_map/ppermute | solution.py:742
  398.2 26.2 %collective-permute-start.45 = (bf16[1536,384]{1,0:T(8,128)(2,1)S(1)}, bf16[1536,384]{1,0:T(8,128)(2,1)S(1)}, u32[]{:S(2)}, u32[]{:S(2)}) collective-permute-start(bf16[1536,384]{1,0:T(8,128)(2,1)S(1)} %convolution_convert_fusion.4), channel_id=1, source_target_pairs={{0,2},{1,3},{2,0},{3,1},{4,6},{5,7},{6,4},{7,5},{8,10},{9,11},{10,... | collective-permute-start | bytes 3538952 | tf_op jit(solution)/shard_map/ppermute | solution.py:751
  (144 other events, 1454.0 us)
Sparse Core Ops, SparseCore 0:
  30.5 116.1 all-gather.2
  148.9 63.3 all-gather.4

commit v6 on v5

--- a/solution.py
+++ b/solution.py
@@ -800,8 +800,8 @@
     unit_other = tp_swap(unit_own, 1)
     cot = cotangent.reshape(4, rows, width)
     cots = [lax.dynamic_index_in_dim(cot, tp ^ k, 0, keepdims=False) for k in range(4)]
-    send_in, send_out, send_down, send_gate_up, unit_other, *pieces = sync(
-        send_in, send_out, send_down, send_gate_up, unit_other, *cots, *far_in
+    send_in, send_out, send_gate_up, unit_other, *pieces = sync(
+        send_in, send_out, send_gate_up, unit_other, *cots, *far_in
     )
     cots, far_in = pieces[:4], pieces[4:]
     gate_up_full = lax.all_gather(send_gate_up, "shard", axis=0, tiled=True)
@@ -888,24 +888,23 @@
 
     came_down = [shards.near(sent_down[0])]
     down_parts = [
-        dot(product[at * rows : (at + 1) * rows], down_full, NT).astype(BF) for at in (3, 2, 1, 0)
-    ][::-1]
-    down_diagonal = tp_swap(down_parts[3], 1)
+        dot(product[at * rows : (at + 1) * rows], down_full, NT).astype(BF) for at in (3, 2)
+    ]
+    down_diagonal = tp_swap(down_parts[0], 1)
     dgate, dup = product_gradient(cots, after(to_gate, *down_parts), to_up, down_full)
-    down_far = combine(down_parts[2], down_diagonal)
-    dgate, dup, *pieces = sync(dgate, dup, sent_down[1], *down_parts, *down_far, *came_down)
-    sent, down_parts, down_far, came_down = pieces[0], pieces[1:5], pieces[5:7], pieces[7:]
+    down_far = combine(down_parts[1], down_diagonal)
+    dgate, dup, *pieces = sync(dgate, dup, sent_down[1], *down_far, *came_down)
+    sent, down_far, came_down = pieces[0], pieces[1:3], pieces[3:]
 
     others = [k for k in range(1, half_count) if k != part]
     came_down.append(shards.near(sent))
     down_came = [tp_swap(down_far[0], 2)]
-    down_core = tp_swap(down_parts[1], 1)
     sums_down = list(fold(kept_down[0], came_down[0], part))
     far_sums = [shards.far(sums_down[0], part)]
     kept_gate, sent_gate = weight_gradient(shards.slots, norms, dgate)
     back_x, back_diagonal = feed_back(2 * rows, 2 * rows, dgate, dup, gate_up_full)
-    dgate, dup, back_x, back_diagonal, down_core, came_down[1], *pieces = sync(
-        dgate, dup, back_x, back_diagonal, down_core, came_down[1],
+    dgate, dup, back_x, back_diagonal, came_down[1], *pieces = sync(
+        dgate, dup, back_x, back_diagonal, came_down[1],
         *sent_gate, *down_came, *far_sums, *sums_down, *norms
     )
     sent_gate, down_came, far_sums, sums_down, norms = (
@@ -939,8 +938,8 @@
     far_sums = [shards.far(sums_gate[0], part)]
     back_came.append(tp_swap(back_far, 2))
     back_own, back_core = feed_back(0, 2 * rows, dgate, dup, gate_up_full)
-    back_own, back_core, came_gate[1], down_far[1], *pieces = sync(
-        back_own, back_core, came_gate[1], down_far[1], *back_came, *sent_up, *far_sums, *sums_gate
+    back_own, back_core, product, came_gate[1], down_far[1], *pieces = sync(
+        back_own, back_core, product, came_gate[1], down_far[1], *back_came, *sent_up, *far_sums, *sums_gate
     )
     back_came, sent_up, far_sums, sums_gate = pieces[:2], pieces[2:4], pieces[4:5], pieces[5:]
 
@@ -960,7 +959,11 @@
     )
     branch_own = grad_hidden.astype(BF)
     branch_other = tp_swap(branch_own, 1)
-    g_own, grad_own = branch_gradients(F32, branch_own, rows_of(mixed_b, 0), out_full_b)
+    down_own = dot(product[:rows], down_full, NT).astype(BF)
+    down_core = dot(product[rows : 2 * rows], down_full, NT).astype(BF)
+    g_own, grad_own = branch_gradients(
+        F32, branch_own, rows_of(mixed_b, 0), after(out_full_b, down_own, down_core)
+    )
     branch_other = after(branch_other, g_own, grad_own)
     g_out_b, grad_other = branch_gradients(
         BF, branch_other, rows_of(mixed_b, 1), out_full_b, g_own
@@ -971,8 +974,8 @@
     )
     g_out, grad_other = branch_gradients(F32, branch_other, rows_of(mixed_a, 1), out_full, g_own)
     grad_mixed_a = in_order(grad_own, grad_other)
-    grad_mixed_b, grad_mixed_a, g_out_b, g_out, sent, *pieces = sync(
-        grad_mixed_b, grad_mixed_a, g_out_b, g_out, sent_up[1], *came_up, *down_came, *far_sums
+    grad_mixed_b, grad_mixed_a, g_out_b, g_out, down_own, down_core, sent, *pieces = sync(
+        grad_mixed_b, grad_mixed_a, g_out_b, g_out, down_own, down_core, sent_up[1], *came_up, *down_came, *far_sums
     )
     came_up, down_came, far_sums_gate = pieces[:1], pieces[1:3], pieces[3:]
 
@@ -980,11 +983,12 @@
     sums_up = list(fold(kept_up[0], came_up[0], part))
     far_sums = [shards.far(sums_up[0], part)]
     g_out_came = tp_swap(g_out_b, 2)
+    down_core = tp_swap(down_core, 1)
     dq_b, dk_b, dv_b = backward_attention(
         chip_table, query_b, grad_mixed_b, mixed_b, lse_b, keys, keys_t, values
     )
-    dq_b, dk_b, dv_b, g_out_came, came_up[1], *pieces = sync(
-        dq_b, dk_b, dv_b, g_out_came, came_up[1], *far_sums, *sums_up
+    dq_b, dk_b, dv_b, g_out_came, down_core, came_up[1], *pieces = sync(
+        dq_b, dk_b, dv_b, g_out_came, down_core, came_up[1], *far_sums, *sums_up
     )
     far_sums, sums_up = pieces[:1], list(fold(kept_up[1], came_up[1], part)) + pieces[1:]
 
@@ -1001,7 +1005,7 @@
     dq_a, dk_a, dv_a = backward_attention(
         chip_table, query_half, grad_mixed_a, mixed_a, lse_a, keys, keys_t, values
     )
-    output = finish_output(hidden, down_parts[0], down_core, *down_came)
+    output = finish_output(hidden, down_own, down_core, *down_came)
     dq_a, dk_a, dv_a, g_query_came, came_out, output, *far_sums_up = sync(
         dq_a, dk_a, dv_a, g_query_came, came_out, output, *far_sums
     )

time: 510 us -> 508 us (level)
  waiting for transfers between devices: 127 us -> 117 us
    ppermute x24, starting transfers between devices: 36.3 us -> 44.9 us  [far(): lax.ppermute(value, 'shard', [(i, (i // 2 ^ k) * 2 + i % 2) for i in rang...]
    all_gather x1, waiting for transfers between devices: 1.77 us -> 10.2 us  [local(): down_full = lax.all_gather(send_down, 'shard', axis=0, tiled=True)]
    ppermute x1, waiting for transfers between devices: 14 us -> 5.61 us  [local(): before = lax.ppermute(half, 'tp', [(0, 2), (1, 3)])]
    ppermute x28, waiting for transfers between devices: 48.7 us -> 43.5 us  [tp_swap(): return lax.ppermute(value, 'tp', [(i, i ^ mask) for i in range(4)])]
    unnamed x202 -> x200, local copies, waits for them, and re-layouts: 10.3 us -> 10.8 us
where the time goes in v6:
time: 508 us; the launch traced here: 501 us
  Pallas kernels  196 us (39%)
  waiting for transfers between devices  117 us (23%)
  starting transfers between devices  79 us (16%)
  matrix products  38 us (7%)
  other arithmetic  30.2 us (6%)
  local copies, waits for them, and re-layouts  24.6 us (5%)
  between operations  16 us (3%)
    pallas_call x40, Pallas kernels, run(): call(*(pltpu.with_memory_space_constraint(x, pltpu.HBM) if x.size > LARGE...  196 us
    ppermute x24, waiting for transfers between devices, far(): lax.ppermute(value, 'shard', [(i, (i // 2 ^ k) * 2 + i % 2) for i in rang...  55 us
    ppermute x24, starting transfers between devices, far(): lax.ppermute(value, 'shard', [(i, (i // 2 ^ k) * 2 + i % 2) for i in rang...  44.9 us
    ppermute x28, waiting for transfers between devices, tp_swap(): return lax.ppermute(value, 'tp', [(i, i ^ mask) for i in range(4)])  43.5 us
    dot_general x15, matrix products, dot(): return lax.dot_general(a, b, dims, preferred_element_type=F32)  38 us
    ppermute x28, starting transfers between devices, tp_swap(): return lax.ppermute(value, 'tp', [(i, i ^ mask) for i in range(4)])  18.3 us
    ppermute x11, starting transfers between devices, near(): return lax.ppermute(value, 'shard', [(i, i ^ 1) for i in range(self.count)])  11.2 us
    unnamed x200, local copies, waits for them, and re-layouts  10.8 us
  transfers between devices with their start and end apart: 67, of which 25 were waited for; matrix products, arithmetic and copies ran while one was open for 12% of the time, Pallas kernels for 38%

profile of v6, /device:TPU:0, one launch (start us, length us, event | category | flops | bytes accessed | tf_op | source)
XLA Modules:
  0.0 501.4 jit_solution(10556022237742673143)
XLA Ops:
  20.4 5.6 %dynamic-slice_bitcast_fusion = (bf16[512,1536]{1,0:T(8,128)(2,1)}, bf16[512,1536]{1,0:T(8,128)(2,1)}, bf16[512,1536]{1,0:T(8,128)(2,1)}, bf16[512,1536]{1,0:T(8,128)(2,1)}) fusion(bf16[4,512,1536]{2,1,0:T(8,128)(2,1)} %bitcast.71, s32[]{:T(128)S(6)} %select_n.132, s32[]{:T(128)S(6)} %select_n.131, s32[]{:T(128)S(6)} %select_n.130, s32[]{:T(128)S(6)} %select_n.129), kind=kLoop, calls=%fused_computation.31 | loop fusion | bytes 12582928 | tf_op jit(solution)/shard_map/jit(dynamic_index_in_dim)/squeeze | solution.py:802
  42.1 12.6 %collective-permute-done.7.refs_2_ = bf16[192,384]{1,0:T(8,128)(2,1)S(1)} collective-permute-done((bf16[192,384]{1,0:T(8,128)(2,1)S(1)}, bf16[192,384]{1,0:T(8,128)(2,1)S(1)}, u32[]{:S(2)}, u32[]{:S(2)}) %collective-permute-start.7) | collective-permute-done | bytes 147488 | tf_op jit(solution)/shard_map/ppermute | solution.py:742
  70.9 5.6 %collective-permute-done.10 = bf16[1024,128]{1,0:T(8,128)(2,1)} collective-permute-done((bf16[1024,128]{1,0:T(8,128)(2,1)S(1)}, bf16[1024,128]{1,0:T(8,128)(2,1)}, u32[]{:S(2)}, u32[]{:S(2)}) %collective-permute-start.10) | collective-permute-done | bytes 262176 | tf_op jit(solution)/shard_map/ppermute | solution.py:830
  77.3 5.0 %multiply_convert_fusion.3.q_ref = bf16[1024,384]{1,0:T(8,128)(2,1)} fusion(bf16[1024,1536]{1,0:T(8,128)(2,1)} %copy-done.58, bf16[1536,384]{1,0:T(8,128)(2,1)S(1)} %unpack_pieces.5.weight_b_ref), kind=kOutput, calls=%fused_computation.30 | convolution fusion | flops 1208745984 | bytes 5111808 | tf_op jit(solution)/shard_map/dot_general | solution.py:29
  91.2 5.9 %attention_forward.3 = (bf16[1024,384]{1,0:T(8,128)(2,1)S(1)}, f32[8,1024]{1,0:T(8,128)S(1)}) custom-call(s32[1]{0:T(128)} %bitcast.chip_ref, bf16[1024,384]{1,0:T(8,128)(2,1)S(1)} %copy-done.34, bf16[2048,128]{1,0:T(8,128)(2,1)S(1)} %get-tuple-element.597.k_ref, bf16[128,2048]{1,0:T(8,128)(2,1)S(1)} %copy-done.23), custom_call_target="tpu_custom_call" | custom-call | tf_op jit(solution)/shard_map/attention_forward/pallas_call | solution.py:40
  97.1 6.2 %attention_forward.2 = (bf16[1024,384]{1,0:T(8,128)(2,1)S(1)}, f32[8,1024]{1,0:T(8,128)S(1)}) custom-call(s32[1]{0:T(128)} %bitcast.chip_ref, bf16[1024,512]{1,0:T(8,128)(2,1)S(1)} %multiply_convert_fusion.1.q_ref, bf16[2048,128]{1,0:T(8,128)(2,1)S(1)} %get-tuple-element.597.k_ref, bf16[128,2048]{1,0:T(8,128)(2,1)S(1)} %copy-done.23), custom_call_target="tpu_custom_call" | custom-call | tf_op jit(solution)/shard_map/attention_forward/pallas_call | solution.py:40
  103.4 8.4 %collective-permute-done.15.near = bf16[768,384]{1,0:T(8,128)(2,1)} collective-permute-done((bf16[768,384]{1,0:T(8,128)(2,1)}, bf16[768,384]{1,0:T(8,128)(2,1)}, u32[]{:S(2)}, u32[]{:S(2)}) %collective-permute-start.15) | collective-permute-done | bytes 589856 | tf_op jit(solution)/shard_map/ppermute | solution.py:751
  130.0 18.2 %collective-permute-done.18.refs_0_.refs_2_ = bf16[256,1536]{1,0:T(8,128)(2,1)} collective-permute-done((bf16[256,1536]{1,0:T(8,128)(2,1)S(1)}, bf16[256,1536]{1,0:T(8,128)(2,1)}, u32[]{:S(2)}, u32[]{:S(2)}) %collective-permute-start.18) | collective-permute-done | bytes 786464 | tf_op jit(solution)/shard_map/ppermute | solution.py:751
  153.5 13.3 %gate_up_first.1 = (bf16[2048,1152]{1,0:T(8,128)(2,1)}, bf16[2048,1152]{1,0:T(8,128)(2,1)}, bf16[2048,1152]{1,0:T(8,128)(2,1)}) custom-call(bf16[512,1536]{1,0:T(8,128)(2,1)S(1)} %multiply_convert_fusion.refs_0_, bf16[512,1536]{1,0:T(8,128)(2,1)S(1)} %copy-done.11, bf16[1536,2304]{1,0:T(8,128)(2,1)} %all-gather.3.cloned.1.call-done.refs_2_.refs_4_.source), custom_call_target="tpu_custom_call" | custom-call | tf_op jit(solution)/shard_map/gate_up_first/pallas_call | solution.py:40
  172.1 14.9 %gate_up_rest.1 = (bf16[2048,1152]{1,0:T(8,128)(2,1)}, bf16[2048,1152]{1,0:T(8,128)(2,1)}, bf16[2048,1152]{1,0:T(8,128)(2,1)}) custom-call(bf16[256,1536]{1,0:T(8,128)(2,1)} %collective-permute-done.18.refs_0_.refs_2_, bf16[256,1536]{1,0:T(8,128)(2,1)} %collective-permute-done.19.refs_1_.refs_3_, ...), custom_call_target="tpu_custom_call", output_to_operand_aliasing={{0}: (5, {}), {1}: (6, {}), {2}: (7, {})} | custom-call | tf_op jit(solution)/shard_map/gate_up_rest/pallas_call | solution.py:40
  187.1 14.9 %weight_gradient.3 = (bf16[384,1152]{1,0:T(8,128)(2,1)}, bf16[384,1152]{1,0:T(8,128)(2,1)}, bf16[384,1152]{1,0:T(8,128)(2,1)}, bf16[384,1152]{1,0:T(8,128)(2,1)}) custom-call(s32[8]{0:T(128)S(1)} %fusion.22.slot_ref, bf16[512,1536]{1,0:T(8,128)(2,1)S(1)} %copy-done.2, bf16[512,1536]{1,0:T(8,128)(2,1)S(1)} %copy-done.8, bf16[512,1536]{1,0:T(8,128)(2,1)S(1)} %copy-done.6, ...), custom_call_target="tpu_custom_call" | custom-call | tf_op jit(solution)/shard_map/weight_gradient/pallas_call | solution.py:40
  202.0 10.2 %all-gather.5.cloned.1.call-done.refs_6_ = bf16[1536,1152]{1,0:T(8,128)(2,1)} async-done(((bf16[192,1152]{1,0:T(8,128)(2,1)}), bf16[1536,1152]{1,0:T(8,128)(2,1)}) %all-gather.5.cloned.1.call-update) | async-done | bytes 3538960 | tf_op jit(solution)/shard_map/all_gather | solution.py:849
  221.7 16.0 %product_gradient.1 = (bf16[2048,1152]{1,0:T(8,128)(2,1)}, bf16[2048,1152]{1,0:T(8,128)(2,1)}) custom-call(bf16[512,1536]{1,0:T(8,128)(2,1)S(1)} %copy-done.3, bf16[512,1536]{1,0:T(8,128)(2,1)S(1)} %copy-done.9, bf16[512,1536]{1,0:T(8,128)(2,1)S(1)} %copy-done.7, bf16[512,1536]{1,0:T(8,128)(2,1)S(1)} %copy-done.5, ...), custom_call_target="tpu_custom_call" | custom-call | tf_op jit(solution)/shard_map/product_gradient/pallas_call | solution.py:40
  244.0 15.3 %weight_gradient.4 = (bf16[384,1152]{1,0:T(8,128)(2,1)}, bf16[384,1152]{1,0:T(8,128)(2,1)}, bf16[384,1152]{1,0:T(8,128)(2,1)}, bf16[384,1152]{1,0:T(8,128)(2,1)}) custom-call(s32[8]{0:T(128)S(1)} %fusion.22.slot_ref, bf16[512,1536]{1,0:T(8,128)(2,1)S(1)} %multiply_convert_fusion.refs_0_, bf16[512,1536]{1,0:T(8,128)(2,1)S(1)} %copy-done.12, ...), custom_call_target="tpu_custom_call" | custom-call | tf_op jit(solution)/shard_map/weight_gradient/pallas_call | solution.py:40
  259.3 12.8 %feed_back.2 = (bf16[512,1536]{1,0:T(8,128)(2,1)S(1)}, bf16[512,1536]{1,0:T(8,128)(2,1)S(1)}) custom-call(bf16[2048,1152]{1,0:T(8,128)(2,1)} %get-tuple-element.412.dgate_ref.refs_6_, bf16[2048,1152]{1,0:T(8,128)(2,1)} %get-tuple-element.413.dup_ref.refs_6_, bf16[1536,2304]{1,0:T(8,128)(2,1)} %all-gather.3.cloned.1.call-done.refs_2_.refs_4_.source), custom_call_target="tpu_custom_call" | custom-call | tf_op jit(solution)/shard_map/feed_back/pallas_call | solution.py:40
  281.2 14.9 %weight_gradient.5 = (bf16[384,1152]{1,0:T(8,128)(2,1)}, bf16[384,1152]{1,0:T(8,128)(2,1)}, bf16[384,1152]{1,0:T(8,128)(2,1)}, bf16[384,1152]{1,0:T(8,128)(2,1)}) custom-call(s32[8]{0:T(128)S(1)} %fusion.22.slot_ref, bf16[512,1536]{1,0:T(8,128)(2,1)S(1)} %multiply_convert_fusion.refs_0_, bf16[512,1536]{1,0:T(8,128)(2,1)S(1)} %copy-done.12, ...), custom_call_target="tpu_custom_call" | custom-call | tf_op jit(solution)/shard_map/weight_gradient/pallas_call | solution.py:40
  306.2 12.9 %feed_back.3 = (bf16[512,1536]{1,0:T(8,128)(2,1)S(1)}, bf16[512,1536]{1,0:T(8,128)(2,1)S(1)}) custom-call(bf16[2048,1152]{1,0:T(8,128)(2,1)} %get-tuple-element.412.dgate_ref.refs_6_, bf16[2048,1152]{1,0:T(8,128)(2,1)} %get-tuple-element.413.dup_ref.refs_6_, bf16[1536,2304]{1,0:T(8,128)(2,1)} %all-gather.3.cloned.1.call-done.refs_2_.refs_4_.source), custom_call_target="tpu_custom_call" | custom-call | tf_op jit(solution)/shard_map/feed_back/pallas_call | solution.py:40
  319.0 6.1 %collective-permute-done.34.refs_1_ = bf16[192,1152]{1,0:T(8,128)(2,1)S(1)} collective-permute-done((bf16[192,1152]{1,0:T(8,128)(2,1)}, bf16[192,1152]{1,0:T(8,128)(2,1)S(1)}, u32[]{:S(2)}, u32[]{:S(2)}) %collective-permute-start.34) | collective-permute-done | bytes 442400 | tf_op jit(solution)/shard_map/ppermute | solution.py:742
  365.9 10.8 %attention_backward.2 = (bf16[1024,384]{1,0:T(8,128)(2,1)S(1)}, f32[2048,128]{1,0:T(8,128)S(1)}, f32[2048,128]{1,0:T(8,128)S(1)}) custom-call(s32[1]{0:T(128)} %bitcast.chip_ref, bf16[1024,384]{1,0:T(8,128)(2,1)S(1)} %copy-done.35, bf16[1024,384]{1,0:T(8,128)(2,1)S(1)} %copy-done.39, bf16[1024,384]{1,0:T(8,128)(2,1)S(1)} %copy-done.37, ...), custom_call_target="tpu_custom_call" | custom-call | tf_op jit(solution)/shard_map/attention_backward/pallas_call | solution.py:40
  376.7 7.8 %collective-permute-done.44.refs_5_ = bf16[192,1152]{1,0:T(8,128)(2,1)} collective-permute-done((bf16[192,1152]{1,0:T(8,128)(2,1)}, bf16[192,1152]{1,0:T(8,128)(2,1)}, u32[]{:S(2)}, u32[]{:S(2)}) %collective-permute-start.44) | collective-permute-done | bytes 442400 | tf_op jit(solution)/shard_map/ppermute | solution.py:742
  400.2 10.9 %attention_backward.3 = (bf16[1024,384]{1,0:T(8,128)(2,1)S(1)}, f32[2048,128]{1,0:T(8,128)S(1)}, f32[2048,128]{1,0:T(8,128)S(1)}) custom-call(s32[1]{0:T(128)} %bitcast.chip_ref, bf16[1024,512]{1,0:T(8,128)(2,1)S(1)} %copy-done.20, bf16[1024,384]{1,0:T(8,128)(2,1)S(1)} %copy-done.38, bf16[1024,384]{1,0:T(8,128)(2,1)S(1)} %copy-done.33, ...), custom_call_target="tpu_custom_call" | custom-call | tf_op jit(solution)/shard_map/attention_backward/pallas_call | solution.py:40
  411.1 5.3 %finish_output.1 = bf16[512,1536]{1,0:T(8,128)(2,1)} custom-call(f32[512,1536]{1,0:T(8,128)} %copy-done.54, bf16[512,1536]{1,0:T(8,128)(2,1)} %convolution_convert_fusion.1.own_ref, bf16[512,1536]{1,0:T(8,128)(2,1)} %collective-permute-done.42.core_ref, bf16[256,1536]{1,0:T(8,128)(2,1)} %copy-done.69, bf16[256,1536]{1,0:T(8,128)(2,1)} %copy-done.70), custom_call_target="tpu_custom_call" | custom-call | tf_op jit(solution)/shard_map/finish_output/pallas_call | solution.py:40
  460.8 7.5 %collective-permute-done.58 = bf16[192,384]{1,0:T(8,128)(2,1)S(1)} collective-permute-done((bf16[192,384]{1,0:T(8,128)(2,1)S(1)}, bf16[192,384]{1,0:T(8,128)(2,1)S(1)}, u32[]{:S(2)}, u32[]{:S(2)}) %collective-permute-start.58) | collective-permute-done | bytes 147488 | tf_op jit(solution)/shard_map/ppermute | solution.py:742
  482.7 6.6 %token_gradient.1 = f32[512,1,1536]{2,1,0:T(1,128)} custom-call(f32[512,1536]{1,0:T(8,128)} %convolution_add_fusion.1.own_ref, bf16[512,1536]{1,0:T(8,128)(2,1)} %copy-done.67, bf16[512,1536]{1,0:T(8,128)(2,1)} %bitcast.68, f32[512,1536]{1,0:T(8,128)} %get-tuple-element.591.through_ref), custom_call_target="tpu_custom_call" | custom-call | tf_op jit(solution)/shard_map/token_gradient/pallas_call | solution.py:40
  (429 shorter events, 237.7 us)
Async XLA Ops:
  7.2 144.9 %all-gather.3.cloned.1.call-start = ((), (), s32[]{:S(2)}) async-start(), calls=%async_computation | async-start | bytes 7962624 | tf_op jit(solution)/shard_map/all_gather | solution.py:807
  30.4 181.9 %all-gather.5.cloned.1.call-start = ((), (), s32[]{:S(2)}) async-start(), calls=%async_computation.1 | async-start | bytes 3981312 | tf_op jit(solution)/shard_map/all_gather | solution.py:849
  30.5 25.7 %collective-permute-start.5 = (bf16[768,512]{1,0:T(8,128)(2,1)S(1)}, bf16[768,512]{1,0:T(8,128)(2,1)S(1)}, u32[]{:S(2)}, u32[]{:S(2)}) collective-permute-start(bf16[768,512]{1,0:T(8,128)(2,1)S(1)} %pack_pieces.2.far), channel_id=1, source_target_pairs={{0,4},{4,0},{8,12},{12,8},{16,20},{20,16},{24,28},{28,24},{1,5},{5... | collective-permute-start | bytes 2359304 | tf_op jit(solution)/shard_map/ppermute | solution.py:747
  32.1 22.6 %collective-permute-start.4 = (bf16[768,384]{1,0:T(8,128)(2,1)S(1)}, bf16[768,384]{1,0:T(8,128)(2,1)S(1)}, u32[]{:S(2)}, u32[]{:S(2)}) collective-permute-start(bf16[768,384]{1,0:T(8,128)(2,1)S(1)} %slice.87), channel_id=1, source_target_pairs={{0,2},{1,3},{2,0},{3,1},{4,6},{5,7},{6,4},{7,5},{8,10},{9,11},{10,... | collective-permute-start | bytes 1769480 | tf_op jit(solution)/shard_map/ppermute | solution.py:751
  84.9 26.9 %collective-permute-start.15 = (bf16[768,384]{1,0:T(8,128)(2,1)}, bf16[768,384]{1,0:T(8,128)(2,1)}, u32[]{:S(2)}, u32[]{:S(2)}) collective-permute-start(bf16[768,384]{1,0:T(8,128)(2,1)} %collective-permute-done.11.near), channel_id=1, source_target_pairs={{0,2},{1,3},{2,0},{3,1},{4,6},{5,7},{6,4},{7,5},{8,10},{9,11},{10,... | collective-permute-start | bytes 1769480 | tf_op jit(solution)/shard_map/ppermute | solution.py:751
  217.1 22.1 %collective-permute-start.23 = (bf16[384,1152]{1,0:T(8,128)(2,1)S(1)}, bf16[384,1152]{1,0:T(8,128)(2,1)S(1)}, u32[]{:S(2)}, u32[]{:S(2)}) collective-permute-start(bf16[384,1152]{1,0:T(8,128)(2,1)S(1)} %copy-done.91), channel_id=1, source_target_pairs={{0,4},{4,0},{8,12},{12,8},{16,20},{20,16},{24,28},{28,24},{1,5},{5... | collective-permute-start | bytes 2654216 | tf_op jit(solution)/shard_map/ppermute | solution.py:747
  239.2 33.0 %collective-permute-start.24 = (bf16[384,1152]{1,0:T(8,128)(2,1)S(1)}, bf16[384,1152]{1,0:T(8,128)(2,1)S(1)}, u32[]{:S(2)}, u32[]{:S(2)}) collective-permute-start(bf16[384,1152]{1,0:T(8,128)(2,1)S(1)} %copy-done.90), channel_id=1, source_target_pairs={{0,4},{4,0},{8,12},{12,8},{16,20},{20,16},{24,28},{28,24},{1,5},{5... | collective-permute-start | bytes 2654216 | tf_op jit(solution)/shard_map/ppermute | solution.py:747
  239.7 32.4 %collective-permute-start.25 = (bf16[256,1536]{1,0:T(8,128)(2,1)S(1)}, bf16[256,1536]{1,0:T(8,128)(2,1)S(1)}, u32[]{:S(2)}, u32[]{:S(2)}) collective-permute-start(bf16[256,1536]{1,0:T(8,128)(2,1)S(1)} %get-tuple-element.385), channel_id=1, source_target_pairs={{0,2},{1,3},{2,0},{3,1},{4,6},{5,7},{6,4},{7,5},{8,10},{9,11},{10,... | collective-permute-start | bytes 2359304 | tf_op jit(solution)/shard_map/ppermute | solution.py:751
  242.2 29.9 %collective-permute-start.26 = (bf16[192,1152]{1,0:T(8,128)(2,1)}, bf16[192,1152]{1,0:T(8,128)(2,1)S(1)}, u32[]{:S(2)}, u32[]{:S(2)}) collective-permute-start(bf16[192,1152]{1,0:T(8,128)(2,1)} %get-tuple-element.388), channel_id=1, source_target_pairs={{0,16},{4,20},{8,24},{12,28},{16,0},{20,4},{24,8},{28,12},{1,17},{... | collective-permute-start | bytes 1327112 | tf_op jit(solution)/shard_map/ppermute | solution.py:742
  273.2 27.7 %collective-permute-start.29 = (bf16[384,1152]{1,0:T(8,128)(2,1)S(1)}, bf16[384,1152]{1,0:T(8,128)(2,1)S(1)}, u32[]{:S(2)}, u32[]{:S(2)}) collective-permute-start(bf16[384,1152]{1,0:T(8,128)(2,1)S(1)} %copy-done.89), channel_id=1, source_target_pairs={{0,4},{4,0},{8,12},{12,8},{16,20},{20,16},{24,28},{28,24},{1,5},{5... | collective-permute-start | bytes 2654216 | tf_op jit(solution)/shard_map/ppermute | solution.py:747
  276.9 24.0 %collective-permute-start.28 = (bf16[256,1536]{1,0:T(8,128)(2,1)S(1)}, bf16[256,1536]{1,0:T(8,128)(2,1)S(1)}, u32[]{:S(2)}, u32[]{:S(2)}) collective-permute-start(bf16[256,1536]{1,0:T(8,128)(2,1)S(1)} %get-tuple-element.396), channel_id=1, source_target_pairs={{0,2},{1,3},{2,0},{3,1},{4,6},{5,7},{6,4},{7,5},{8,10},{9,11},{10,... | collective-permute-start | bytes 2359304 | tf_op jit(solution)/shard_map/ppermute | solution.py:751
  279.2 21.7 %collective-permute-start.31 = (bf16[192,1152]{1,0:T(8,128)(2,1)S(1)}, bf16[192,1152]{1,0:T(8,128)(2,1)S(1)}, u32[]{:S(2)}, u32[]{:S(2)}) collective-permute-start(bf16[192,1152]{1,0:T(8,128)(2,1)S(1)} %copy-done.93), channel_id=1, source_target_pairs={{0,24},{4,28},{8,16},{12,20},{16,8},{20,12},{24,0},{28,4},{1,25},{... | collective-permute-start | bytes 1327112 | tf_op jit(solution)/shard_map/ppermute | solution.py:742
  300.9 24.2 %collective-permute-start.32 = (bf16[384,1152]{1,0:T(8,128)(2,1)S(1)}, bf16[384,1152]{1,0:T(8,128)(2,1)S(1)}, u32[]{:S(2)}, u32[]{:S(2)}) collective-permute-start(bf16[384,1152]{1,0:T(8,128)(2,1)S(1)} %copy-done.88), channel_id=1, source_target_pairs={{0,4},{4,0},{8,12},{12,8},{16,20},{20,16},{24,28},{28,24},{1,5},{5... | collective-permute-start | bytes 2654216 | tf_op jit(solution)/shard_map/ppermute | solution.py:747
  302.5 22.7 %collective-permute-start.33 = (bf16[256,1536]{1,0:T(8,128)(2,1)S(1)}, bf16[256,1536]{1,0:T(8,128)(2,1)S(1)}, u32[]{:S(2)}, u32[]{:S(2)}) collective-permute-start(bf16[256,1536]{1,0:T(8,128)(2,1)S(1)} %get-tuple-element.419), channel_id=1, source_target_pairs={{0,2},{1,3},{2,0},{3,1},{4,6},{5,7},{6,4},{7,5},{8,10},{9,11},{10,... | collective-permute-start | bytes 2359304 | tf_op jit(solution)/shard_map/ppermute | solution.py:751
  335.3 22.5 %collective-permute-start.37 = (bf16[384,1152]{1,0:T(8,128)(2,1)}, bf16[384,1152]{1,0:T(8,128)(2,1)S(1)}, u32[]{:S(2)}, u32[]{:S(2)}) collective-permute-start(bf16[384,1152]{1,0:T(8,128)(2,1)} %get-tuple-element.443), channel_id=1, source_target_pairs={{0,4},{4,0},{8,12},{12,8},{16,20},{20,16},{24,28},{28,24},{1,5},{5... | collective-permute-start | bytes 2654216 | tf_op jit(solution)/shard_map/ppermute | solution.py:747
  335.9 21.9 %collective-permute-start.38 = (bf16[256,1536]{1,0:T(8,128)(2,1)S(1)}, bf16[256,1536]{1,0:T(8,128)(2,1)S(1)}, u32[]{:S(2)}, u32[]{:S(2)}) collective-permute-start(bf16[256,1536]{1,0:T(8,128)(2,1)S(1)} %get-tuple-element.445), channel_id=1, source_target_pairs={{0,2},{1,3},{2,0},{3,1},{4,6},{5,7},{6,4},{7,5},{8,10},{9,11},{10,... | collective-permute-start | bytes 2359304 | tf_op jit(solution)/shard_map/ppermute | solution.py:751
  336.5 21.4 %collective-permute-start.40 = (bf16[192,1152]{1,0:T(8,128)(2,1)}, bf16[192,1152]{1,0:T(8,128)(2,1)S(1)}, u32[]{:S(2)}, u32[]{:S(2)}) collective-permute-start(bf16[192,1152]{1,0:T(8,128)(2,1)} %get-tuple-element.450), channel_id=1, source_target_pairs={{0,24},{4,28},{8,16},{12,20},{16,8},{20,12},{24,0},{28,4},{1,25},{... | collective-permute-start | bytes 1327112 | tf_op jit(solution)/shard_map/ppermute | solution.py:742
  357.9 28.8 %collective-permute-start.42 = (bf16[512,1536]{1,0:T(8,128)(2,1)}, bf16[512,1536]{1,0:T(8,128)(2,1)}, u32[]{:S(2)}, u32[]{:S(2)}) collective-permute-start(bf16[512,1536]{1,0:T(8,128)(2,1)} %convolution_convert_fusion), channel_id=1, source_target_pairs={{0,1},{1,0},{2,3},{3,2},{4,5},{5,4},{6,7},{7,6},{8,9},{9,8},{10,11... | collective-permute-start | bytes 4718600 | tf_op jit(solution)/shard_map/ppermute | solution.py:751
  357.9 28.7 %collective-permute-start.41 = (bf16[1536,384]{1,0:T(8,128)(2,1)}, bf16[1536,384]{1,0:T(8,128)(2,1)}, u32[]{:S(2)}, u32[]{:S(2)}) collective-permute-start(bf16[1536,384]{1,0:T(8,128)(2,1)} %get-tuple-element.457), channel_id=1, source_target_pairs={{0,2},{1,3},{2,0},{3,1},{4,6},{5,7},{6,4},{7,5},{8,10},{9,11},{10,... | collective-permute-start | bytes 3538952 | tf_op jit(solution)/shard_map/ppermute | solution.py:751
  358.6 26.0 %collective-permute-start.43 = (bf16[384,1152]{1,0:T(8,128)(2,1)}, bf16[384,1152]{1,0:T(8,128)(2,1)}, u32[]{:S(2)}, u32[]{:S(2)}) collective-permute-start(bf16[384,1152]{1,0:T(8,128)(2,1)} %get-tuple-element.459), channel_id=1, source_target_pairs={{0,4},{4,0},{8,12},{12,8},{16,20},{20,16},{24,28},{28,24},{1,5},{5... | collective-permute-start | bytes 2654216 | tf_op jit(solution)/shard_map/ppermute | solution.py:747
  360.2 24.4 %collective-permute-start.44 = (bf16[192,1152]{1,0:T(8,128)(2,1)}, bf16[192,1152]{1,0:T(8,128)(2,1)}, u32[]{:S(2)}, u32[]{:S(2)}) collective-permute-start(bf16[192,1152]{1,0:T(8,128)(2,1)} %get-tuple-element.462), channel_id=1, source_target_pairs={{0,16},{4,20},{8,24},{12,28},{16,0},{20,4},{24,8},{28,12},{1,17},{... | collective-permute-start | bytes 1327112 | tf_op jit(solution)/shard_map/ppermute | solution.py:742
  393.3 27.5 %collective-permute-start.45 = (bf16[1536,384]{1,0:T(8,128)(2,1)S(1)}, bf16[1536,384]{1,0:T(8,128)(2,1)S(1)}, u32[]{:S(2)}, u32[]{:S(2)}) collective-permute-start(bf16[1536,384]{1,0:T(8,128)(2,1)S(1)} %convolution_convert_fusion.4), channel_id=1, source_target_pairs={{0,2},{1,3},{2,0},{3,1},{4,6},{5,7},{6,4},{7,5},{8,10},{9,11},{10,... | collective-permute-start | bytes 3538952 | tf_op jit(solution)/shard_map/ppermute | solution.py:751
  393.8 25.2 %collective-permute-start.46 = (bf16[768,384]{1,0:T(8,128)(2,1)S(1)}, bf16[768,384]{1,0:T(8,128)(2,1)S(1)}, u32[]{:S(2)}, u32[]{:S(2)}) collective-permute-start(bf16[768,384]{1,0:T(8,128)(2,1)S(1)} %get-tuple-element.481), channel_id=1, source_target_pairs={{0,4},{4,0},{8,12},{12,8},{16,20},{20,16},{24,28},{28,24},{1,5},{5... | collective-permute-start | bytes 1769480 | tf_op jit(solution)/shard_map/ppermute | solution.py:747
  394.4 22.0 %collective-permute-start.47 = (bf16[192,1152]{1,0:T(8,128)(2,1)}, bf16[192,1152]{1,0:T(8,128)(2,1)S(1)}, u32[]{:S(2)}, u32[]{:S(2)}) collective-permute-start(bf16[192,1152]{1,0:T(8,128)(2,1)} %get-tuple-element.487), channel_id=1, source_target_pairs={{0,8},{4,12},{8,0},{12,4},{16,24},{20,28},{24,16},{28,20},{1,9},{5... | collective-permute-start | bytes 1327112 | tf_op jit(solution)/shard_map/ppermute | solution.py:742
  (143 other events, 1433.0 us)
Sparse Core Ops, SparseCore 0:
  30.5 116.1 all-gather.2
  148.8 63.3 all-gather.4
